TPU v7x, 256 devices: a whole 4x4x8 slice. The times are simulated.
256 devices in a mesh: ctx: 32 (over z, x), head: 4 (over y_hi, core), side: 2 (over y_lo).
Axes of the slice: x: 4, y: 4 (y_hi: 2, y_lo: 2; y = y_hi * 2 + y_lo), z: 8, core: 2. Of those that a mesh axis runs over, the one named last changes fastest.
Arguments:
- prefill_query: bfloat16 [8192, 64, 128], P('ctx', ('head', 'side')), may hold values from -6 to 6
- prefill_keys: bfloat16 [8192, 8, 128], P('ctx', ('head', 'side')), may hold values from -6 to 6
- prefill_values: bfloat16 [8192, 8, 128], P('ctx', ('head', 'side')), may hold values from -6 to 6
- token_pos: int32 [8192], P('ctx'), may hold values from 0 to 8191, as said below
- scale_exp: int32 [1024, 8, 2], P('ctx', ('head', 'side')), may hold values from -7 to -5
- page_owner: int32 [1024], P('ctx'), may hold values from 0 to 31, as said below
- draft_query: bfloat16 [256, 64, 128], P(None, ('head', 'side')), may hold values from -6 to 6
- draft_keys: bfloat16 [256, 8, 128], P('side', 'head'), may hold values from -6 to 6
- draft_values: bfloat16 [256, 8, 128], P('side', 'head'), may hold values from -6 to 6
- parents: int32 [256], replicated, may hold values from 0 to 254, as said below
Outputs:
- prefill_out: bfloat16 [8192, 64, 128], P('ctx', ('head', 'side'))
- cache_keys: bfloat16 [8192, 8, 128], P('ctx', ('head', 'side'))
- cache_values: bfloat16 [8192, 8, 128], P('ctx', ('head', 'side'))
- verify_out: bfloat16 [256, 64, 128], P('ctx', ('head', 'side'))
Inputs may be any that keep to these rules, and one draw needn't show every extreme that they name: `token_pos`: a permutation of 0 to 8191; the rows of shard c of ctx hold the runs a and 2 * 32 - 1 - a of 128 consecutive positions, in order, with a different a for each shard. `page_owner`: the 1024 // 32 entries of one ctx shard are a permutation of 0 to 32 - 1. parents[0] = 0, and parents[r] < r for r >= 1.
All inputs are finite; a program needn't handle non-finite values.
Results may differ from a plain program's by a relative error of at most 0.0049.
Values may be sent and summed in bfloat16 or wider, within the bound.
No kernel may reach another device: no remote copies, remote signals or barrier semaphores. Data moves between devices by JAX's collectives and lax.ppermute only.
A program may use at most 64 MiB of HBM per device.

v0:
```python
import functools

import jax
import jax.numpy as jnp
from jax import lax
from jax.experimental import pallas as pl
from jax.experimental.pallas import tpu as pltpu
from jax.sharding import Mesh
from jax.sharding import PartitionSpec as P


CTX = ("z", "x")
NEG = -1.0e30
LOG_TWO_E = 1.4426950408889634
TOK = 256
HALF = 128
GROUPS = 8
WIDTH = 128
PAGES = 32
META = 32
PAY = 2 * TOK + META
QH = HALF * GROUPS
SLOTS = 4
COEF = WIDTH**-0.5 * LOG_TWO_E
BF = jnp.bfloat16
F32 = jnp.float32


def iota(shape, dim):
    return lax.broadcasted_iota(jnp.int32, shape, dim)


def dot_t(a, b):
    return lax.dot_general(a, b, (((1,), (1,)), ((), ())), preferred_element_type=F32)


def dot(a, b):
    return jnp.dot(a, b, preferred_element_type=F32)


def held(x):
    return pltpu.with_memory_space_constraint(x, pltpu.VMEM)


def vmem(n):
    return [pl.BlockSpec(memory_space=pltpu.VMEM)] * n


def pack_kernel(pos_ref, scale_ref, owner_ref, k_ref, v_ref, out_ref):
    out_ref[0:TOK, :] = k_ref[...]
    out_ref[TOK : 2 * TOK, :] = v_ref[...]
    first = (pos_ref[0] // HALF).astype(F32)
    diag = iota((PAGES, PAGES), 0) == iota((PAGES, PAGES), 1)

    def column(row):
        return jnp.sum(jnp.where(diag, row, 0.0), axis=1, keepdims=True)

    scale = scale_ref[...]
    bound = jnp.where(scale == -7, 3.5, jnp.where(scale == -6, 7.0, 14.0)).astype(F32)
    lane = iota((META, WIDTH), 1)
    meta = jnp.where(
        lane < 32,
        column(bound[0:1, :]),
        jnp.where(
            lane < 64,
            column(bound[1:2, :]),
            jnp.where(lane < 96, column(owner_ref[...].astype(F32)), first),
        ),
    )
    out_ref[2 * TOK :, :] = meta.astype(BF)


def me_index():
    return lax.axis_index("z") * 4 + lax.axis_index("x")


def softmax_update(s, v, m_ref, acc_ref, rows):
    keys = s.shape[1]
    top = jnp.broadcast_to(jnp.max(s, axis=1, keepdims=True), (s.shape[0], WIDTH))
    old = m_ref[rows, :]
    new = jnp.maximum(old, jnp.ceil(top))
    factor = jnp.exp2(old - new)
    p = jnp.exp2(s - jnp.tile(new, (1, keys // WIDTH))).astype(BF)
    acc_ref[rows, :] = acc_ref[rows, :] * jnp.tile(factor, (1, 2)) + dot(p, v)
    m_ref[rows, :] = new


def softmax_start(s, v, m_ref, acc_ref, rows):
    keys = s.shape[1]
    top = jnp.broadcast_to(jnp.max(s, axis=1, keepdims=True), (s.shape[0], WIDTH))
    new = jnp.ceil(top)
    p = jnp.exp2(s - jnp.tile(new, (1, keys // WIDTH))).astype(BF)
    acc_ref[rows, :] = dot(p, v)
    m_ref[rows, :] = new


def with_ones(v):
    return jnp.concatenate([v, jnp.ones(v.shape, BF)], axis=1)


def clipped_source(src_ref, base, col, mine, kc_ref, vc_ref, slot, ck_ref, cv_ref):
    meta = src_ref[base + 2 * TOK : base + PAY, :]
    pick = iota((WIDTH, 3 * WIDTH), 0) == (iota((WIDTH, 3 * WIDTH), 1) // WIDTH) * 32
    spread = dot(meta, pick.astype(BF)).astype(BF)
    grow = (iota((TOK, META), 0) // 8 == iota((TOK, META), 1)).astype(BF)
    rows = dot(grow, spread)
    k = src_ref[base : base + TOK, :].astype(F32)
    v = src_ref[base + TOK : base + 2 * TOK, :].astype(F32)
    kb, vb, own = rows[:, :WIDTH], rows[:, WIDTH : 2 * WIDTH], rows[:, 2 * WIDTH :]
    k = jnp.maximum(jnp.minimum(k, kb), -kb)
    v = jnp.maximum(jnp.minimum(v, vb), -vb)
    kc_ref[slot * TOK : (slot + 1) * TOK, :] = k.astype(BF)
    vc_ref[slot * TOK : (slot + 1) * TOK, :] = with_ones(v.astype(BF))
    hit = own == mine.astype(F32)
    at = pl.ds(pl.multiple_of(col * 8, 8), 8)
    ck_ref[at, :] = jnp.sum(jnp.where(hit, k, 0.0).reshape(PAGES, 8, WIDTH), axis=0)
    cv_ref[at, :] = jnp.sum(jnp.where(hit, v, 0.0).reshape(PAGES, 8, WIDTH), axis=0)


def first_of(src_ref, base):
    meta = src_ref[base + 2 * TOK : base + PAY, :].astype(F32)
    return jnp.max(meta[:, 96:]).astype(jnp.int32)


def own_kernel(
    q_ref, own_ref, dq_ref, tree_ref, far_ref, par_ref,
    mh_ref, ah_ref, ml_ref, al_ref, mv_ref, av_ref, ck_ref, cv_ref,
    kc_ref, vc_ref,
):
    me = me_index()
    side = lax.axis_index("side")
    first = first_of(own_ref, 0)
    swap = (first >= PAGES).astype(jnp.int32)
    lo = pl.multiple_of(swap * HALF, HALF)
    hi = pl.multiple_of(HALF - swap * HALF, HALF)
    k_lo, k_hi = own_ref[pl.ds(lo, HALF), :], own_ref[pl.ds(hi, HALF), :]
    v_lo = with_ones(own_ref[pl.ds(pl.multiple_of(TOK + lo, HALF), HALF), :])
    v_hi = with_ones(own_ref[pl.ds(pl.multiple_of(TOK + hi, HALF), HALF), :])
    k_both = jnp.concatenate([k_lo, k_hi], axis=0)
    v_both = jnp.concatenate([v_lo, v_hi], axis=0)
    part = 256
    for t in range(QH // part):
        rows = pl.ds(t * part, part)
        token = iota((part, HALF), 0) // GROUPS + t * part // GROUPS
        open_ = iota((part, HALF), 1) <= token
        q = q_ref[pl.ds(pl.multiple_of(hi * GROUPS + t * part, part), part), :]
        s = dot_t(q, k_both) * COEF
        s = jnp.concatenate([s[:, :HALF], jnp.where(open_, s[:, HALF:], NEG)], axis=1)
        softmax_start(s, v_both, mh_ref, ah_ref, rows)
        q = q_ref[pl.ds(pl.multiple_of(lo * GROUPS + t * part, part), part), :]
        s = jnp.where(open_, dot_t(q, k_lo) * COEF, NEG)
        softmax_start(s, v_lo, ml_ref, al_ref, rows)

    link = (par_ref[...] == iota((TOK, TOK), 0)) | (iota((TOK, TOK), 0) == iota((TOK, TOK), 1))
    link = link.astype(F32).astype(BF)
    for _ in range(8):
        link = jnp.minimum(dot(link, link), 1.0).astype(BF)
    rows64 = GROUPS * 8
    take = (iota((rows64, TOK), 1) == me * 8 + iota((rows64, TOK), 0) // GROUPS).astype(F32).astype(BF)
    allowed = dot_t(take, link) > 0.5

    def head(ref, at):
        zero, one = ref[:, at : at + WIDTH], ref[:, at + WIDTH : at + 2 * WIDTH]
        return jnp.where(side == 0, zero, one)

    def rows_of(at):
        near, far = head(tree_ref, at), head(far_ref, at)
        return jnp.concatenate(
            [jnp.where(side == 0, near, far), jnp.where(side == 0, far, near)], axis=0
        )

    dq = dq_ref[pl.ds(pl.multiple_of(me * rows64, rows64), rows64), :]
    s = jnp.where(allowed, dot_t(dq, rows_of(0)) * COEF, NEG)
    softmax_start(s, with_ones(rows_of(2 * WIDTH)), mv_ref, av_ref, pl.ds(0, rows64))
    clipped_source(own_ref, 0, me, me, kc_ref, vc_ref, 0, ck_ref, cv_ref)
    s = dot_t(dq, kc_ref[...]) * COEF
    softmax_update(s, vc_ref[...], mv_ref, av_ref, pl.ds(0, rows64))


def flash_chunks(q_ref, q_at, k_ref, v_ref, base, chunks, m_ref, acc_ref):
    part = 256
    span = SLOTS * HALF

    def chunk(i, _):
        at = pl.multiple_of(base * HALF + i * span, HALF)
        k = k_ref[pl.ds(at, span), :]
        v = v_ref[pl.ds(at, span), :]
        for t in range(QH // part):
            q = q_ref[pl.ds(pl.multiple_of(q_at + t * part, part), part), :]
            softmax_update(dot_t(q, k) * COEF, v, m_ref, acc_ref, pl.ds(t * part, part))
        return 0

    lax.fori_loop(0, chunks, chunk, 0)


def step_kernel(layout, last, *refs):
    n_in = len(layout)
    q_ref, own_ref, dq_ref = refs[:3]
    srcs = refs[3 : 3 + n_in]
    state = refs[11 + n_in : 19 + n_in]
    if last:
        out_ref, ver_ref, ok_ref, ov_ref = refs[19 + n_in : 23 + n_in]
    kk_ref, vv_ref, kc_ref, vc_ref = refs[-4:]
    mh_ref, ah_ref, ml_ref, al_ref, mv_ref, av_ref, ck_ref, cv_ref = state
    me, z, x = me_index(), lax.axis_index("z"), lax.axis_index("x")
    first = first_of(own_ref, 0)
    swap = (first >= PAGES).astype(jnp.int32)
    mine = jnp.minimum(first, 2 * PAGES - 1 - first)
    blocks = [(r, i * PAY, d) for r, ds in zip(srcs, layout) for i, d in enumerate(ds)]
    n = len(blocks)
    lo_base = 2 * n + SLOTS
    n_hi, n_lo = jnp.int32(0), jnp.int32(0)
    for i, (ref, base, _) in enumerate(blocks):
        f = first_of(ref, base)
        other = (f >= PAGES).astype(jnp.int32)
        later = (jnp.minimum(f, 2 * PAGES - 1 - f) > mine).astype(jnp.int32)
        lo = base + other * HALF
        hi = base + HALF - other * HALF
        sel = jnp.where(later == 1, hi, lo)
        to = jnp.where(later == 1, n + n_hi, lo_base + n_lo)
        kk_ref[i * HALF : (i + 1) * HALF, :] = ref[pl.ds(pl.multiple_of(lo, 32), HALF), :]
        vv_ref[i * HALF : (i + 1) * HALF, :] = with_ones(
            ref[pl.ds(pl.multiple_of(lo + TOK, 32), HALF), :]
        )
        at = pl.ds(pl.multiple_of(to * HALF, HALF), HALF)
        kk_ref[at, :] = ref[pl.ds(pl.multiple_of(sel, 32), HALF), :]
        vv_ref[at, :] = with_ones(ref[pl.ds(pl.multiple_of(sel + TOK, 32), HALF), :])
        n_hi, n_lo = n_hi + later, n_lo + 1 - later
    for start, count in ((0, n + n_hi), (lo_base, n_lo)):
        for j in range(SLOTS - 1):
            at = pl.ds(pl.multiple_of((start + count + j) * HALF, HALF), HALF)
            kk_ref[at, :] = kk_ref[start * HALF : (start + 1) * HALF, :]
            vv_ref[at, :] = jnp.zeros((HALF, 2 * WIDTH), BF)
    q_lo = swap * QH
    q_hi = QH - swap * QH
    flash_chunks(q_ref, q_hi, kk_ref, vv_ref, 0, (n + n_hi + SLOTS - 1) // SLOTS, mh_ref, ah_ref)
    flash_chunks(q_ref, q_lo, kk_ref, vv_ref, lo_base, (n_lo + SLOTS - 1) // SLOTS, ml_ref, al_ref)

    for i, (ref, base, (dz, dx)) in enumerate(blocks):
        col = ((z + dz + 8) % 8) * 4 + (x + dx + 4) % 4
        clipped_source(ref, base, col, me, kc_ref, vc_ref, i, ck_ref, cv_ref)
    rows64 = GROUPS * 8
    dq = dq_ref[pl.ds(pl.multiple_of(me * rows64, rows64), rows64), :]
    softmax_update(dot_t(dq, kc_ref[...]) * COEF, vc_ref[...], mv_ref, av_ref, pl.ds(0, rows64))
    if last:
        part = 256
        for t in range(QH // part):
            rows = pl.ds(t * part, part)
            for at, acc in ((q_hi, ah_ref), (q_lo, al_ref)):
                a = acc[rows, :]
                out_ref[pl.ds(pl.multiple_of(at + t * part, part), part), :] = (
                    a[:, :WIDTH] / a[:, WIDTH:]
                ).astype(BF)
        a = av_ref[...]
        ver_ref[...] = (a[:, :WIDTH] / a[:, WIDTH:]).astype(BF)
        ok_ref[...] = ck_ref[...].astype(BF)
        ov_ref[...] = cv_ref[...].astype(BF)


STATE = [
    pltpu.VMEM((QH, WIDTH), F32),
    pltpu.VMEM((QH, 2 * WIDTH), F32),
    pltpu.VMEM((QH, WIDTH), F32),
    pltpu.VMEM((QH, 2 * WIDTH), F32),
    pltpu.VMEM((64, WIDTH), F32),
    pltpu.VMEM((64, 2 * WIDTH), F32),
    pltpu.VMEM((TOK, WIDTH), F32),
    pltpu.VMEM((TOK, WIDTH), F32),
]
GRANT = pltpu.CompilerParams(vmem_limit_bytes=40 * 1024 * 1024)


def cost(n):
    return pl.CostEstimate(
        flops=n * 4 * TOK * QH * WIDTH, bytes_accessed=n * PAY * WIDTH * 2, transcendentals=0
    )


def step(q, own, dq, sources, layout, state, last=False):
    n = sum(len(d) for d in layout)
    outs = STATE
    alias = {3 + len(layout) + i: i for i in range(8)}
    if last:
        outs = STATE + [
            jax.ShapeDtypeStruct((2 * QH, WIDTH), BF),
            jax.ShapeDtypeStruct((64, WIDTH), BF),
            jax.ShapeDtypeStruct((TOK, WIDTH), BF),
            jax.ShapeDtypeStruct((TOK, WIDTH), BF),
        ]
    slots = 3 * n + 2 * SLOTS
    return pl.pallas_call(
        functools.partial(step_kernel, layout, last),
        out_shape=outs,
        in_specs=vmem(11 + len(layout)),
        out_specs=vmem(len(outs)),
        scratch_shapes=[
            pltpu.VMEM((slots * HALF, WIDTH), BF),
            pltpu.VMEM((slots * HALF, 2 * WIDTH), BF),
            pltpu.VMEM((n * TOK, WIDTH), BF),
            pltpu.VMEM((n * TOK, 2 * WIDTH), BF),
        ],
        input_output_aliases=alias,
        cost_estimate=cost(n),
        compiler_params=GRANT,
    )(*(held(a) for a in (q, own, dq, *sources, *state)))


def shift(b, axis, d):
    n = lax.axis_size(axis)
    return lax.ppermute(b, axis, [(i, (i + d) % n) for i in range(n)])


def work(
    prefill_query, prefill_keys, prefill_values, token_pos, scale_exp, page_owner,
    draft_query, draft_keys, draft_values, parents,
):
    q = prefill_query.reshape(2 * QH, WIDTH)
    dq = draft_query.reshape(2 * QH, WIDTH)
    own = pl.pallas_call(
        pack_kernel,
        out_shape=pltpu.VMEM((PAY, WIDTH), BF),
        compiler_params=pltpu.CompilerParams(vmem_limit_bytes=4 * 1024 * 1024),
        in_specs=[pl.BlockSpec(memory_space=pltpu.SMEM)] + vmem(4),
        out_specs=vmem(1)[0],
        name="pack",
    )(
        token_pos,
        jnp.transpose(scale_exp, (1, 2, 0)).reshape(2, PAGES),
        page_owner.reshape(1, PAGES),
        prefill_keys.reshape(TOK, WIDTH),
        prefill_values.reshape(TOK, WIDTH),
    )
    tree = jnp.concatenate(
        [draft_keys.reshape(HALF, 2 * WIDTH), draft_values.reshape(HALF, 2 * WIDTH)], axis=1
    )
    xs = [shift(own, "x", 1), shift(own, "x", -1), shift(own, "x", 2)]
    far = shift(tree, "side", 1)
    near_x = jnp.concatenate(xs, axis=0)
    own_call = pl.pallas_call(
        own_kernel,
        out_shape=STATE,
        in_specs=vmem(6),
        out_specs=vmem(8),
        scratch_shapes=[pltpu.VMEM((TOK, WIDTH), BF), pltpu.VMEM((TOK, 2 * WIDTH), BF)],
        cost_estimate=cost(2),
        compiler_params=GRANT,
        name="own",
    )
    state = own_call(*(held(a) for a in (q, own, dq, tree, far)), parents.reshape(1, TOK))
    dxs = (-1, 1, 2)
    state = step(q, own, dq, [near_x], [[(0, d) for d in dxs]], state)
    ra = la = own
    rb = lb = near_x
    for s in range(1, 4):
        ra, la = shift(ra, "z", 1), shift(la, "z", -1)
        rb, lb = shift(rb, "z", 1), shift(lb, "z", -1)
        state = step(
            q, own, dq, [ra, la, rb, lb],
            [[(-s, 0)], [(s, 0)], [(-s, d) for d in dxs], [(s, d) for d in dxs]],
            state,
        )
    oa = shift(la, "z", -1)
    ob = shift(rb[: 2 * PAY], "z", 1)
    oc = shift(lb[2 * PAY :], "z", -1)
    out, ver, ck, cv = step(
        q, own, dq, [oa, ob, oc],
        [[(4, 0)], [(4, d) for d in dxs[:2]], [(4, dxs[2])]],
        state, last=True,
    )[8:]
    return (
        out.reshape(TOK, GROUPS, WIDTH),
        ck.reshape(TOK, 1, WIDTH),
        cv.reshape(TOK, 1, WIDTH),
        ver.reshape(8, GROUPS, WIDTH),
    )


def solution(mesh):
    finer = Mesh(
        mesh.devices.reshape(8, 4, mesh.shape["head"], mesh.shape["side"]),
        ("z", "x", "head", "side"),
    )
    full = P(CTX, ("head", "side"), None)
    in_specs = (
        full, full, full, P(CTX), full, P(CTX),
        P(None, ("head", "side"), None),
        P("side", "head", None), P("side", "head", None), P(),
    )
    return jax.shard_map(
        work, mesh=finer, in_specs=in_specs, out_specs=(full, full, full, full), check_vma=False
    )
```

profile of v0, /device:TPU:8, one launch (start us, length us, event | category | flops | bytes accessed | tf_op | source)
XLA Modules:
  0.0 99.5 jit_solution(16227957508651445110)
XLA Ops:
  0.7 0.7 copy-done.5
  1.3 0.8 copy-done.2
  2.2 0.8 copy-done.3
  3.0 0.6 pack.1.own_ref.refs_1_
  3.7 1.6 %collective-permute-start.4 = (bf16[544,128]{1,0:T(8,128)(2,1)S(1)}, bf16[544,128]{1,0:T(8,128)(2,1)S(1)}, u32[]{:S(2)}, u32[]{:S(2)}) collective-permute-start(bf16[544,128]{1,0:T(8,128)(2,1)S(1)} %pack.1.own_ref.refs_1_), channel_id=1, source_target_pairs={{0,8},{8,16},{16,24},{24,0},{1,9},{9,17},{17,25},{25,1},{2,10},{10... | collective-permute-start | bytes 417800 | tf_op jit(solution)/shard_map/ppermute | solution.py:310
  5.3 1.7 %collective-permute-start.5 = (bf16[544,128]{1,0:T(8,128)(2,1)S(1)}, bf16[544,128]{1,0:T(8,128)(2,1)S(1)}, u32[]{:S(2)}, u32[]{:S(2)}) collective-permute-start(bf16[544,128]{1,0:T(8,128)(2,1)S(1)} %pack.1.own_ref.refs_1_), channel_id=1, source_target_pairs={{0,24},{8,0},{16,8},{24,16},{1,25},{9,1},{17,9},{25,17},{2,26},{10... | collective-permute-start | bytes 417800 | tf_op jit(solution)/shard_map/ppermute | solution.py:310
  7.0 1.8 %collective-permute-start.6 = (bf16[544,128]{1,0:T(8,128)(2,1)S(1)}, bf16[544,128]{1,0:T(8,128)(2,1)S(1)}, u32[]{:S(2)}, u32[]{:S(2)}) collective-permute-start(bf16[544,128]{1,0:T(8,128)(2,1)S(1)} %pack.1.own_ref.refs_1_), channel_id=1, source_target_pairs={{0,16},{8,24},{16,0},{24,8},{1,17},{9,25},{17,1},{25,9},{2,18},{10... | collective-permute-start | bytes 417800 | tf_op jit(solution)/shard_map/ppermute | solution.py:310
  8.8 1.6 %collective-permute-done.4 = bf16[544,128]{1,0:T(8,128)(2,1)S(1)} collective-permute-done((bf16[544,128]{1,0:T(8,128)(2,1)S(1)}, bf16[544,128]{1,0:T(8,128)(2,1)S(1)}, u32[]{:S(2)}, u32[]{:S(2)}) %collective-permute-start.4) | collective-permute-done | bytes 139296 | tf_op jit(solution)/shard_map/ppermute | solution.py:310
  10.4 2.3 %collective-permute-done.5 = bf16[544,128]{1,0:T(8,128)(2,1)S(1)} collective-permute-done((bf16[544,128]{1,0:T(8,128)(2,1)S(1)}, bf16[544,128]{1,0:T(8,128)(2,1)S(1)}, u32[]{:S(2)}, u32[]{:S(2)}) %collective-permute-start.5) | collective-permute-done | bytes 139296 | tf_op jit(solution)/shard_map/ppermute | solution.py:310
  12.7 1.7 %collective-permute-done.6 = bf16[544,128]{1,0:T(8,128)(2,1)S(1)} collective-permute-done((bf16[544,128]{1,0:T(8,128)(2,1)S(1)}, bf16[544,128]{1,0:T(8,128)(2,1)S(1)}, u32[]{:S(2)}, u32[]{:S(2)}) %collective-permute-start.6) | collective-permute-done | bytes 139296 | tf_op jit(solution)/shard_map/ppermute | solution.py:310
  14.4 5.9 %collective-permute-start.11 = (bf16[1632,128]{1,0:T(8,128)(2,1)S(1)}, bf16[1632,128]{1,0:T(8,128)(2,1)S(1)}, u32[]{:S(2)}, u32[]{:S(2)}) collective-permute-start(bf16[1632,128]{1,0:T(8,128)(2,1)S(1)} %constant_dynamic-update-slice_fusion.refs_3_), channel_id=1, source_target_pairs={{0,224},{32,0},{64,32},{96,64},{128,96},{160,128},{192,160},{224,1... | collective-permute-start | bytes 1253384 | tf_op jit(solution)/shard_map/ppermute | solution.py:310
  20.3 8.2 %collective-permute-done.11.refs_6_ = bf16[1632,128]{1,0:T(8,128)(2,1)S(1)} collective-permute-done((bf16[1632,128]{1,0:T(8,128)(2,1)S(1)}, bf16[1632,128]{1,0:T(8,128)(2,1)S(1)}, u32[]{:S(2)}, u32[]{:S(2)}) %collective-permute-start.11) | collective-permute-done | bytes 417824 | tf_op jit(solution)/shard_map/ppermute | solution.py:310
  28.5 3.7 %collective-permute-start.12 = (bf16[1632,128]{1,0:T(8,128)(2,1)S(1)}, bf16[1632,128]{1,0:T(8,128)(2,1)S(1)}, u32[]{:S(2)}, u32[]{:S(2)}) collective-permute-start(bf16[1632,128]{1,0:T(8,128)(2,1)S(1)} %collective-permute-done.11.refs_6_), channel_id=1, source_target_pairs={{0,224},{32,0},{64,32},{96,64},{128,96},{160,128},{192,160},{224,1... | collective-permute-start | bytes 1253384 | tf_op jit(solution)/shard_map/ppermute | solution.py:310
  32.2 3.2 %collective-permute-start = (bf16[544,128]{1,0:T(8,128)(2,1)S(1)}, bf16[544,128]{1,0:T(8,128)(2,1)S(1)}, u32[]{:S(2)}, u32[]{:S(2)}) collective-permute-start(bf16[544,128]{1,0:T(8,128)(2,1)S(1)} %pack.1.own_ref.refs_1_), channel_id=1, source_target_pairs={{0,224},{32,0},{64,32},{96,64},{128,96},{160,128},{192,160},{224,1... | collective-permute-start | bytes 417800 | tf_op jit(solution)/shard_map/ppermute | solution.py:310
  35.4 7.0 %collective-permute-done.refs_4_ = bf16[544,128]{1,0:T(8,128)(2,1)S(1)} collective-permute-done((bf16[544,128]{1,0:T(8,128)(2,1)S(1)}, bf16[544,128]{1,0:T(8,128)(2,1)S(1)}, u32[]{:S(2)}, u32[]{:S(2)}) %collective-permute-start) | collective-permute-done | bytes 139296 | tf_op jit(solution)/shard_map/ppermute | solution.py:310
  42.5 3.7 %collective-permute-start.1 = (bf16[544,128]{1,0:T(8,128)(2,1)S(1)}, bf16[544,128]{1,0:T(8,128)(2,1)S(1)}, u32[]{:S(2)}, u32[]{:S(2)}) collective-permute-start(bf16[544,128]{1,0:T(8,128)(2,1)S(1)} %collective-permute-done.refs_4_), channel_id=1, source_target_pairs={{0,224},{32,0},{64,32},{96,64},{128,96},{160,128},{192,160},{224,1... | collective-permute-start | bytes 417800 | tf_op jit(solution)/shard_map/ppermute | solution.py:310
  46.2 0.0 collective-permute-start.13
  46.2 2.0 %collective-permute-start.9 = (bf16[1632,128]{1,0:T(8,128)(2,1)S(1)}, bf16[1632,128]{1,0:T(8,128)(2,1)S(1)}, u32[]{:S(2)}, u32[]{:S(2)}) collective-permute-start(bf16[1632,128]{1,0:T(8,128)(2,1)S(1)} %collective-permute-done.8.refs_5_), channel_id=1, source_target_pairs={{0,32},{32,64},{64,96},{96,128},{128,160},{160,192},{192,224},{224... | collective-permute-start | bytes 1253384 | tf_op jit(solution)/shard_map/ppermute | solution.py:310
  48.2 0.5 collective-permute-start.18
  48.8 1.5 %collective-permute-done.1.refs_4_ = bf16[544,128]{1,0:T(8,128)(2,1)S(1)} collective-permute-done((bf16[544,128]{1,0:T(8,128)(2,1)S(1)}, bf16[544,128]{1,0:T(8,128)(2,1)S(1)}, u32[]{:S(2)}, u32[]{:S(2)}) %collective-permute-start.1) | collective-permute-done | bytes 139296 | tf_op jit(solution)/shard_map/ppermute | solution.py:310
  50.2 3.7 %collective-permute-start.2 = (bf16[544,128]{1,0:T(8,128)(2,1)S(1)}, bf16[544,128]{1,0:T(8,128)(2,1)S(1)}, u32[]{:S(2)}, u32[]{:S(2)}) collective-permute-start(bf16[544,128]{1,0:T(8,128)(2,1)S(1)} %collective-permute-done.1.refs_4_), channel_id=1, source_target_pairs={{0,224},{32,0},{64,32},{96,64},{128,96},{160,128},{192,160},{224,1... | collective-permute-start | bytes 417800 | tf_op jit(solution)/shard_map/ppermute | solution.py:310
  54.0 0.7 copy-done.6
  54.6 3.5 %own.1 = (f32[1024,128]{1,0:T(8,128)S(1)}, f32[1024,256]{1,0:T(8,128)S(1)}, f32[1024,128]{1,0:T(8,128)S(1)}, f32[1024,256]{1,0:T(8,128)S(1)}, f32[64,128]{1,0:T(...) custom-call(bf16[2048,128]{1,0:T(8,128)(2,1)S(1)} %bitcast.19, ...), custom_call_target="tpu_custom_call" | custom-call | flops 268435456 | bytes 278528 | tf_op jit(solution)/shard_map/own/pallas_call | solution.py:349
  58.2 3.7 %shard_map.129 = (f32[1024,128]{1,0:T(8,128)S(1)}, f32[1024,256]{1,0:T(8,128)S(1)}, f32[1024,128]{1,0:T(8,128)S(1)}, f32[1024,256]{1,0:T(8,128)S(1)}, f32[64,128...) custom-call(bf16[2048,128]{1,0:T(8,128)(2,1)S(1)} %bitcast.20, ...), custom_call_target="tpu_custom_call", output_to_operand_aliasing={{0}: (4, {}), {1}: (5, {}), {2}: (6, {}), {3}: (7, {}), {4}... | custom-call | flops 402653184 | bytes 417792 | tf_op jit(solution)/shard_map/pallas_call | solution.py:291
  61.8 0.1 collective-permute-start.17
  62.0 3.2 %collective-permute-start.3 = (bf16[544,128]{1,0:T(8,128)(2,1)S(1)}, bf16[544,128]{1,0:T(8,128)(2,1)S(1)}, u32[]{:S(2)}, u32[]{:S(2)}) collective-permute-start(bf16[544,128]{1,0:T(8,128)(2,1)S(1)} %collective-permute-done.2.refs_4_), channel_id=1, source_target_pairs={{0,224},{32,0},{64,32},{96,64},{128,96},{160,128},{192,160},{224,1... | collective-permute-start | bytes 417800 | tf_op jit(solution)/shard_map/ppermute | solution.py:310
  65.2 0.1 collective-permute-start.10
  65.3 8.2 %shard_map.130 = (f32[1024,128]{1,0:T(8,128)S(1)}, f32[1024,256]{1,0:T(8,128)S(1)}, f32[1024,128]{1,0:T(8,128)S(1)}, f32[1024,256]{1,0:T(8,128)S(1)}, f32[64,128...) custom-call(bf16[2048,128]{1,0:T(8,128)(2,1)S(1)} %bitcast.21, ...), custom_call_target="tpu_custom_call", output_to_operand_aliasing={{0}: (7, {}), {1}: (8, {}), {2}: (9, {}), {3}: (10, {}), {4... | custom-call | flops 1073741824 | bytes 1114112 | tf_op jit(solution)/shard_map/pallas_call | solution.py:291
  73.5 3.3 %collective-permute-start.14 = (bf16[544,128]{1,0:T(8,128)(2,1)S(1)}, bf16[544,128]{1,0:T(8,128)(2,1)S(1)}, u32[]{:S(2)}, u32[]{:S(2)}) collective-permute-start(bf16[544,128]{1,0:T(8,128)(2,1)S(1)} %slice.9), channel_id=1, source_target_pairs={{0,224},{32,0},{64,32},{96,64},{128,96},{160,128},{192,160},{224,1... | collective-permute-start | bytes 417800 | tf_op jit(solution)/shard_map/ppermute | solution.py:310
  76.8 8.4 %shard_map.131 = (f32[1024,128]{1,0:T(8,128)S(1)}, f32[1024,256]{1,0:T(8,128)S(1)}, f32[1024,128]{1,0:T(8,128)S(1)}, f32[1024,256]{1,0:T(8,128)S(1)}, f32[64,128...) custom-call(bf16[2048,128]{1,0:T(8,128)(2,1)S(1)} %bitcast.22, ...), custom_call_target="tpu_custom_call", output_to_operand_aliasing={{0}: (7, {}), {1}: (8, {}), {2}: (9, {}), {3}: (10, {}), {4... | custom-call | flops 1073741824 | bytes 1114112 | tf_op jit(solution)/shard_map/pallas_call | solution.py:291
  85.3 8.2 %shard_map.132 = (f32[1024,128]{1,0:T(8,128)S(1)}, f32[1024,256]{1,0:T(8,128)S(1)}, f32[1024,128]{1,0:T(8,128)S(1)}, f32[1024,256]{1,0:T(8,128)S(1)}, f32[64,128...) custom-call(bf16[2048,128]{1,0:T(8,128)(2,1)S(1)} %bitcast.23, ...), custom_call_target="tpu_custom_call", output_to_operand_aliasing={{0}: (7, {}), {1}: (8, {}), {2}: (9, {}), {3}: (10, {}), {4... | custom-call | flops 1073741824 | bytes 1114112 | tf_op jit(solution)/shard_map/pallas_call | solution.py:291
  93.5 5.9 %shard_map.133 = (f32[1024,128]{1,0:T(8,128)S(1)}, f32[1024,256]{1,0:T(8,128)S(1)}, f32[1024,128]{1,0:T(8,128)S(1)}, f32[1024,256]{1,0:T(8,128)S(1)}, f32[64,128...) custom-call(bf16[2048,128]{1,0:T(8,128)(2,1)S(1)} %bitcast.24, ...), custom_call_target="tpu_custom_call", output_to_operand_aliasing={{0}: (6, {}), {1}: (7, {}), {2}: (8, {}), {3}: (9, {}), {4}... | custom-call | flops 536870912 | bytes 557056 | tf_op jit(solution)/shard_map/pallas_call | solution.py:291
  (40 shorter events, 0.2 us)
Async XLA Ops:
  0.6 0.7 copy-start.5
  0.6 0.7 copy-start.4
  0.7 0.7 copy-start.7
  1.3 0.8 copy-start.2
  2.2 0.8 copy-start.3
  3.0 32.4 %copy-start.8 = (bf16[128,2,128]{2,1,0:T(2,128)(2,1)S(1)}, bf16[128,2,128]{2,1,0:T(2,128)(2,1)}, u32[]{:S(2)}) copy-start(bf16[128,2,128]{2,1,0:T(2,128)(2,1)} %param.17) | copy-start | bytes 196612
  3.0 45.2 %copy-start.9 = (bf16[128,2,128]{2,1,0:T(2,128)(2,1)S(1)}, bf16[128,2,128]{2,1,0:T(2,128)(2,1)}, u32[]{:S(2)}) copy-start(bf16[128,2,128]{2,1,0:T(2,128)(2,1)} %param.18) | copy-start | bytes 196612
  3.7 50.3 %copy-start = (bf16[256,8,128]{2,1,0:T(8,128)(2,1)S(1)}, bf16[256,8,128]{2,1,0:T(8,128)(2,1)}, u32[]{:S(2)}) copy-start(bf16[256,8,128]{2,1,0:T(8,128)(2,1)} %param.10) | copy-start | bytes 1572868
  3.7 50.3 %copy-start.1 = (bf16[256,8,128]{2,1,0:T(8,128)(2,1)S(1)}, bf16[256,8,128]{2,1,0:T(8,128)(2,1)}, u32[]{:S(2)}) copy-start(bf16[256,8,128]{2,1,0:T(8,128)(2,1)} %param.16) | copy-start | bytes 1572868
  3.7 6.7 %collective-permute-start.4 = (bf16[544,128]{1,0:T(8,128)(2,1)S(1)}, bf16[544,128]{1,0:T(8,128)(2,1)S(1)}, u32[]{:S(2)}, u32[]{:S(2)}) collective-permute-start(bf16[544,128]{1,0:T(8,128)(2,1)S(1)} %pack.1.own_ref.refs_1_), channel_id=1, source_target_pairs={{0,8},{8,16},{16,24},{24,0},{1,9},{9,17},{17,25},{25,1},{2,10},{10... | collective-permute-start | bytes 417800 | tf_op jit(solution)/shard_map/ppermute | solution.py:310
  5.3 7.4 %collective-permute-start.5 = (bf16[544,128]{1,0:T(8,128)(2,1)S(1)}, bf16[544,128]{1,0:T(8,128)(2,1)S(1)}, u32[]{:S(2)}, u32[]{:S(2)}) collective-permute-start(bf16[544,128]{1,0:T(8,128)(2,1)S(1)} %pack.1.own_ref.refs_1_), channel_id=1, source_target_pairs={{0,24},{8,0},{16,8},{24,16},{1,25},{9,1},{17,9},{25,17},{2,26},{10... | collective-permute-start | bytes 417800 | tf_op jit(solution)/shard_map/ppermute | solution.py:310
  7.0 7.4 %collective-permute-start.6 = (bf16[544,128]{1,0:T(8,128)(2,1)S(1)}, bf16[544,128]{1,0:T(8,128)(2,1)S(1)}, u32[]{:S(2)}, u32[]{:S(2)}) collective-permute-start(bf16[544,128]{1,0:T(8,128)(2,1)S(1)} %pack.1.own_ref.refs_1_), channel_id=1, source_target_pairs={{0,16},{8,24},{16,0},{24,8},{1,17},{9,25},{17,1},{25,9},{2,18},{10... | collective-permute-start | bytes 417800 | tf_op jit(solution)/shard_map/ppermute | solution.py:310
  14.4 14.1 %collective-permute-start.11 = (bf16[1632,128]{1,0:T(8,128)(2,1)S(1)}, bf16[1632,128]{1,0:T(8,128)(2,1)S(1)}, u32[]{:S(2)}, u32[]{:S(2)}) collective-permute-start(bf16[1632,128]{1,0:T(8,128)(2,1)S(1)} %constant_dynamic-update-slice_fusion.refs_3_), channel_id=1, source_target_pairs={{0,224},{32,0},{64,32},{96,64},{128,96},{160,128},{192,160},{224,1... | collective-permute-start | bytes 1253384 | tf_op jit(solution)/shard_map/ppermute | solution.py:310
  20.3 11.9 %collective-permute-start.7 = (bf16[1632,128]{1,0:T(8,128)(2,1)S(1)}, bf16[1632,128]{1,0:T(8,128)(2,1)S(1)}, u32[]{:S(2)}, u32[]{:S(2)}) collective-permute-start(bf16[1632,128]{1,0:T(8,128)(2,1)S(1)} %constant_dynamic-update-slice_fusion.refs_3_), channel_id=1, source_target_pairs={{0,32},{32,64},{64,96},{96,128},{128,160},{160,192},{192,224},{224... | collective-permute-start | bytes 1253384 | tf_op jit(solution)/shard_map/ppermute | solution.py:310
  28.5 17.7 %collective-permute-start.12 = (bf16[1632,128]{1,0:T(8,128)(2,1)S(1)}, bf16[1632,128]{1,0:T(8,128)(2,1)S(1)}, u32[]{:S(2)}, u32[]{:S(2)}) collective-permute-start(bf16[1632,128]{1,0:T(8,128)(2,1)S(1)} %collective-permute-done.11.refs_6_), channel_id=1, source_target_pairs={{0,224},{32,0},{64,32},{96,64},{128,96},{160,128},{192,160},{224,1... | collective-permute-start | bytes 1253384 | tf_op jit(solution)/shard_map/ppermute | solution.py:310
  32.2 14.0 %collective-permute-start.8 = (bf16[1632,128]{1,0:T(8,128)(2,1)S(1)}, bf16[1632,128]{1,0:T(8,128)(2,1)S(1)}, u32[]{:S(2)}, u32[]{:S(2)}) collective-permute-start(bf16[1632,128]{1,0:T(8,128)(2,1)S(1)} %collective-permute-done.7.refs_5_), channel_id=1, source_target_pairs={{0,32},{32,64},{64,96},{96,128},{128,160},{160,192},{192,224},{224... | collective-permute-start | bytes 1253384 | tf_op jit(solution)/shard_map/ppermute | solution.py:310
  32.2 10.3 %collective-permute-start = (bf16[544,128]{1,0:T(8,128)(2,1)S(1)}, bf16[544,128]{1,0:T(8,128)(2,1)S(1)}, u32[]{:S(2)}, u32[]{:S(2)}) collective-permute-start(bf16[544,128]{1,0:T(8,128)(2,1)S(1)} %pack.1.own_ref.refs_1_), channel_id=1, source_target_pairs={{0,224},{32,0},{64,32},{96,64},{128,96},{160,128},{192,160},{224,1... | collective-permute-start | bytes 417800 | tf_op jit(solution)/shard_map/ppermute | solution.py:310
  35.4 13.4 %collective-permute-start.15 = (bf16[544,128]{1,0:T(8,128)(2,1)S(1)}, bf16[544,128]{1,0:T(8,128)(2,1)S(1)}, u32[]{:S(2)}, u32[]{:S(2)}) collective-permute-start(bf16[544,128]{1,0:T(8,128)(2,1)S(1)} %pack.1.own_ref.refs_1_), channel_id=1, source_target_pairs={{0,32},{32,64},{64,96},{96,128},{128,160},{160,192},{192,224},{224... | collective-permute-start | bytes 417800 | tf_op jit(solution)/shard_map/ppermute | solution.py:310
  42.5 7.8 %collective-permute-start.1 = (bf16[544,128]{1,0:T(8,128)(2,1)S(1)}, bf16[544,128]{1,0:T(8,128)(2,1)S(1)}, u32[]{:S(2)}, u32[]{:S(2)}) collective-permute-start(bf16[544,128]{1,0:T(8,128)(2,1)S(1)} %collective-permute-done.refs_4_), channel_id=1, source_target_pairs={{0,224},{32,0},{64,32},{96,64},{128,96},{160,128},{192,160},{224,1... | collective-permute-start | bytes 417800 | tf_op jit(solution)/shard_map/ppermute | solution.py:310
  46.2 27.3 %collective-permute-start.13 = (bf16[1632,128]{1,0:T(8,128)(2,1)S(1)}, bf16[1632,128]{1,0:T(8,128)(2,1)S(1)}, u32[]{:S(2)}, u32[]{:S(2)}) collective-permute-start(bf16[1632,128]{1,0:T(8,128)(2,1)S(1)} %collective-permute-done.12.refs_6_), channel_id=1, source_target_pairs={{0,224},{32,0},{64,32},{96,64},{128,96},{160,128},{192,160},{224,1... | collective-permute-start | bytes 1253384 | tf_op jit(solution)/shard_map/ppermute | solution.py:310
  46.2 19.0 %collective-permute-start.9 = (bf16[1632,128]{1,0:T(8,128)(2,1)S(1)}, bf16[1632,128]{1,0:T(8,128)(2,1)S(1)}, u32[]{:S(2)}, u32[]{:S(2)}) collective-permute-start(bf16[1632,128]{1,0:T(8,128)(2,1)S(1)} %collective-permute-done.8.refs_5_), channel_id=1, source_target_pairs={{0,32},{32,64},{64,96},{96,128},{128,160},{160,192},{192,224},{224... | collective-permute-start | bytes 1253384 | tf_op jit(solution)/shard_map/ppermute | solution.py:310
  48.2 5.7 %collective-permute-start.18 = (bf16[128,512]{1,0:T(8,128)(2,1)S(1)}, bf16[128,512]{1,0:T(8,128)(2,1)S(1)}, u32[]{:S(2)}, u32[]{:S(2)}) collective-permute-start(bf16[128,512]{1,0:T(8,128)(2,1)S(1)} %bitcast_dynamic-update-slice_fusion.tree_ref), channel_id=1, source_target_pairs={{0,1},{1,0},{2,3},{3,2},{4,5},{5,4},{6,7},{7,6},{8,9},{9,8},{10,11... | collective-permute-start | bytes 393224 | tf_op jit(solution)/shard_map/ppermute | solution.py:310
  48.8 13.1 %collective-permute-start.16 = (bf16[544,128]{1,0:T(8,128)(2,1)S(1)}, bf16[544,128]{1,0:T(8,128)(2,1)S(1)}, u32[]{:S(2)}, u32[]{:S(2)}) collective-permute-start(bf16[544,128]{1,0:T(8,128)(2,1)S(1)} %collective-permute-done.15.refs_3_), channel_id=1, source_target_pairs={{0,32},{32,64},{64,96},{96,128},{128,160},{160,192},{192,224},{224... | collective-permute-start | bytes 417800 | tf_op jit(solution)/shard_map/ppermute | solution.py:310
  50.2 11.7 %collective-permute-start.2 = (bf16[544,128]{1,0:T(8,128)(2,1)S(1)}, bf16[544,128]{1,0:T(8,128)(2,1)S(1)}, u32[]{:S(2)}, u32[]{:S(2)}) collective-permute-start(bf16[544,128]{1,0:T(8,128)(2,1)S(1)} %collective-permute-done.1.refs_4_), channel_id=1, source_target_pairs={{0,224},{32,0},{64,32},{96,64},{128,96},{160,128},{192,160},{224,1... | collective-permute-start | bytes 417800 | tf_op jit(solution)/shard_map/ppermute | solution.py:310
  53.9 0.7 copy-start.6
  61.8 23.4 %collective-permute-start.17 = (bf16[544,128]{1,0:T(8,128)(2,1)S(1)}, bf16[544,128]{1,0:T(8,128)(2,1)S(1)}, u32[]{:S(2)}, u32[]{:S(2)}) collective-permute-start(bf16[544,128]{1,0:T(8,128)(2,1)S(1)} %collective-permute-done.16.refs_3_), channel_id=1, source_target_pairs={{0,32},{32,64},{64,96},{96,128},{128,160},{160,192},{192,224},{224... | collective-permute-start | bytes 417800 | tf_op jit(solution)/shard_map/ppermute | solution.py:310
  62.0 31.6 %collective-permute-start.3 = (bf16[544,128]{1,0:T(8,128)(2,1)S(1)}, bf16[544,128]{1,0:T(8,128)(2,1)S(1)}, u32[]{:S(2)}, u32[]{:S(2)}) collective-permute-start(bf16[544,128]{1,0:T(8,128)(2,1)S(1)} %collective-permute-done.2.refs_4_), channel_id=1, source_target_pairs={{0,224},{32,0},{64,32},{96,64},{128,96},{160,128},{192,160},{224,1... | collective-permute-start | bytes 417800 | tf_op jit(solution)/shard_map/ppermute | solution.py:310
  65.2 28.3 %collective-permute-start.10 = (bf16[1088,128]{1,0:T(8,128)(2,1)S(1)}, bf16[1088,128]{1,0:T(8,128)(2,1)S(1)}, u32[]{:S(2)}, u32[]{:S(2)}) collective-permute-start(bf16[1088,128]{1,0:T(8,128)(2,1)S(1)} %slice.8), channel_id=1, source_target_pairs={{0,32},{32,64},{64,96},{96,128},{128,160},{160,192},{192,224},{224... | collective-permute-start | bytes 835592 | tf_op jit(solution)/shard_map/ppermute | solution.py:310
  73.5 20.0 %collective-permute-start.14 = (bf16[544,128]{1,0:T(8,128)(2,1)S(1)}, bf16[544,128]{1,0:T(8,128)(2,1)S(1)}, u32[]{:S(2)}, u32[]{:S(2)}) collective-permute-start(bf16[544,128]{1,0:T(8,128)(2,1)S(1)} %slice.9), channel_id=1, source_target_pairs={{0,224},{32,0},{64,32},{96,64},{128,96},{160,128},{192,160},{224,1... | collective-permute-start | bytes 417800 | tf_op jit(solution)/shard_map/ppermute | solution.py:310
where the time goes:
time: 99.7 us; the launch traced here: 99.5 us
  Pallas kernels  38.6 us (39%)
  starting transfers between devices  34.6 us (35%)
  waiting for transfers between devices  22.2 us (22%)
  local copies, waits for them, and re-layouts  3.14 us (3%)
    ppermute x19, starting transfers between devices, shift(): return lax.ppermute(b, axis, [(i, (i + d) % n) for i in range(n)])  34.6 us
    pallas_call x5, Pallas kernels, step(): pl.pallas_call(functools.partial(step_kernel, layout, last), out_shape=ou...  34.5 us
    ppermute x19, waiting for transfers between devices, shift(): return lax.ppermute(b, axis, [(i, (i + d) % n) for i in range(n)])  22.2 us
    pallas_call x1, Pallas kernels, work(): own_call(*(held(a) for a in (q, own, dq, tree, far)), parents.reshape(1,...  3.54 us
    unnamed x23, local copies, waits for them, and re-layouts  3.08 us
  transfers between devices with their start and end apart: 19, of which 6 were waited for; matrix products, arithmetic and copies ran while one was open for 0% of the time, Pallas kernels for 32%

commit v1 on v0

v1 whole, which is shorter than its diff:
```python
import functools

import jax
import jax.numpy as jnp
from jax import lax
from jax.experimental import pallas as pl
from jax.experimental.pallas import tpu as pltpu
from jax.sharding import Mesh
from jax.sharding import PartitionSpec as P


CTX = ("z", "x")
NEG = -1.0e30
LOG_TWO_E = 1.4426950408889634
TOK = 256
HALF = 128
GROUPS = 8
WIDTH = 128
PAGES = 32
EXTRA = 16
PAY = 2 * TOK + EXTRA
DEEP = WIDTH + EXTRA
QH = HALF * GROUPS
SLOTS = 4
PART = 256
COEF = WIDTH**-0.5 * LOG_TWO_E
BF = jnp.bfloat16
F32 = jnp.float32


def iota(shape, dim):
    return lax.broadcasted_iota(jnp.int32, shape, dim)


def dot_t(a, b):
    return lax.dot_general(a, b, (((1,), (1,)), ((), ())), preferred_element_type=F32)


def dot(a, b):
    return jnp.dot(a, b, preferred_element_type=F32)


def outside(x):
    return pltpu.with_memory_space_constraint(x, pltpu.HBM)


def held(x):
    return pltpu.with_memory_space_constraint(x, pltpu.VMEM)


def vmem(n):
    return [pl.BlockSpec(memory_space=pltpu.VMEM)] * n


def pack_kernel(
    pos_hbm, scale_hbm, owner_hbm, k_hbm, v_hbm, out_ref, pos_ref, scale_ref, owner_ref, v_ref, sems
):
    copies = [
        pltpu.make_async_copy(a, b, sems.at[i])
        for i, (a, b) in enumerate(
            (
                (v_hbm, v_ref),
                (k_hbm, out_ref.at[0:TOK, :]),
                (pos_hbm, pos_ref),
                (scale_hbm, scale_ref),
                (owner_hbm, owner_ref),
            )
        )
    ]
    for c in copies:
        c.start()
    for c in copies:
        c.wait()
    v = jnp.transpose(v_ref[...].astype(F32)).astype(BF)
    out_ref[TOK : TOK + HALF, :] = v[:, :HALF]
    out_ref[TOK + HALF : 2 * TOK, :] = v[:, HALF:]
    first = (pos_ref[0] // HALF).astype(F32)
    scale = scale_ref[...]
    bound = jnp.where(scale == -7, 3.5, jnp.where(scale == -6, 7.0, 14.0)).astype(F32)
    own = owner_ref[...].astype(F32)
    grow = (iota((PAGES, TOK), 0) == iota((PAGES, TOK), 1) // 8).astype(F32).astype(BF)
    row = iota((EXTRA, PAGES), 0)
    few = jnp.where(row < 2, bound[0:1, :], jnp.where(row < 4, bound[1:2, :], own))
    wide = dot(few.astype(BF), grow)
    row = iota((EXTRA, HALF), 0)
    left = (row == 0) | (row == 2) | (row == 4)
    meta = jnp.where(row < 6, jnp.where(left, wide[:, :HALF], wide[:, HALF:]), first)
    out_ref[2 * TOK :, :] = meta.astype(BF)


def me_index():
    return lax.axis_index("z") * 4 + lax.axis_index("x")


def weights_of(s, old):
    top = jnp.ceil(jnp.max(s, axis=0, keepdims=True))
    new = top if old is None else jnp.maximum(old, top)
    return new, jnp.exp2(s - new).astype(BF)


def verify_update(s, v_t, m_ref, l_ref, acc_ref, start=False):
    rows, keys = s.shape
    new = jnp.broadcast_to(jnp.ceil(jnp.max(s, axis=1, keepdims=True)), (rows, WIDTH))
    if not start:
        old = m_ref[...]
        new = jnp.maximum(old, new)
    p = jnp.exp2(s - jnp.tile(new, (1, keys // WIDTH)))
    mass = jnp.broadcast_to(jnp.sum(p, axis=1, keepdims=True), (rows, WIDTH))
    numer = dot_t(p.astype(BF), v_t)
    if not start:
        factor = jnp.exp2(old - new)
        mass = mass + l_ref[...] * factor
        numer = numer + acc_ref[...] * factor
    m_ref[...] = new
    l_ref[...] = mass
    acc_ref[...] = numer


def clipped_source(src_ref, base, col, mine, kc_ref, vc_ref, slot, ck_ref, cv_ref, b_ref):
    wide = src_ref[base + 2 * TOK : base + PAY, :].astype(F32)
    limit = slot * PAGES
    near = iota((PAGES // 2, HALF), 1) == 8 * iota((PAGES // 2, HALF), 0)
    picks = [jnp.where(near, wide[h : h + 1, :], 0.0) for h in range(2)]
    b_ref[limit : limit + PAGES, :] = dot(
        jnp.concatenate(picks, axis=0).astype(BF), jnp.ones((HALF, WIDTH), BF)
    )
    place = iota((2, HALF), 1) // 8 + 16 * iota((2, HALF), 0)
    hit = wide[4:6, :] == mine.astype(F32)
    page = jnp.max(jnp.where(hit, place, 0).astype(F32)).astype(jnp.int32)
    at = pl.ds(pl.multiple_of(col * 8, 8), 8)
    x = src_ref[base : base + TOK, :].astype(F32)
    pieces = []
    for p in range(PAGES):
        row = b_ref[pl.ds(limit + p, 8, stride=0), :]
        pieces.append(jnp.maximum(jnp.minimum(x[p * 8 : p * 8 + 8, :], row), -row))
    kc_ref[slot * TOK : (slot + 1) * TOK, :] = jnp.concatenate(pieces, axis=0).astype(BF)
    top = b_ref[pl.ds(limit + page, 8, stride=0), :]
    got = src_ref[pl.ds(pl.multiple_of(base + page * 8, 8), 8), :].astype(F32)
    ck_ref[at, :] = jnp.maximum(jnp.minimum(got, top), -top)
    total = None
    for h in range(2):
        raw = base + TOK + h * HALF
        row = wide[2 + h : 3 + h, :]
        x = src_ref[raw : raw + HALF, :].astype(F32)
        x = jnp.maximum(jnp.minimum(x, row), -row).astype(BF)
        vc_ref[2 * slot + h] = x
        one = iota((8, HALF), 1) + h * HALF == page * 8 + iota((8, HALF), 0)
        part = dot_t(one.astype(F32).astype(BF), x)
        total = part if total is None else total + part
    cv_ref[at, :] = total


def first_of(src_ref, base):
    meta = src_ref[base + 2 * TOK : base + PAY, :].astype(F32)
    return jnp.max(meta[8:, :]).astype(jnp.int32)


def joined(ref, first, count):
    return jnp.concatenate([ref[first + i] for i in range(count)], axis=1)


def own_kernel(
    q_ref, own_ref, dq_ref, tree_ref, far_ref, par_ref,
    m_ref, acc_ref, mv_ref, lv_ref, av_ref, ck_ref, cv_ref,
    kc_ref, vc_ref, b_ref,
):
    me = me_index()
    side = lax.axis_index("side")
    first = first_of(own_ref, 0)
    swap = (first >= PAGES).astype(jnp.int32)
    lo = pl.multiple_of(swap * HALF, HALF)
    hi = pl.multiple_of(HALF - swap * HALF, HALF)
    ones = jnp.ones((EXTRA, HALF), BF)
    k_lo, k_hi = own_ref[pl.ds(lo, HALF), :], own_ref[pl.ds(hi, HALF), :]
    v_lo = own_ref[pl.ds(pl.multiple_of(TOK + lo, HALF), HALF), :]
    v_hi = own_ref[pl.ds(pl.multiple_of(TOK + hi, HALF), HALF), :]
    v_lo = jnp.concatenate([v_lo, ones], axis=0)
    v_hi = jnp.concatenate([v_hi, ones], axis=0)
    k_both = jnp.concatenate([k_lo, k_hi], axis=0)
    v_both = jnp.concatenate([v_lo, v_hi], axis=1)
    for t in range(QH // PART):
        cols = slice(t * PART, (t + 1) * PART)
        token = iota((HALF, PART), 1) // GROUPS + t * PART // GROUPS
        open_ = iota((HALF, PART), 0) <= token
        q = q_ref[pl.ds(pl.multiple_of(hi * GROUPS + t * PART, PART), PART), :]
        s = dot_t(k_both, q) * COEF
        s = jnp.concatenate([s[:HALF], jnp.where(open_, s[HALF:], NEG)], axis=0)
        new, p = weights_of(s, None)
        acc_ref[1, :, cols] = dot(v_both, p)
        m_ref[1, :, cols] = jnp.broadcast_to(new, (8, PART))
        q = q_ref[pl.ds(pl.multiple_of(lo * GROUPS + t * PART, PART), PART), :]
        new, p = weights_of(jnp.where(open_, dot_t(k_lo, q) * COEF, NEG), None)
        acc_ref[0, :, cols] = dot(v_lo, p)
        m_ref[0, :, cols] = jnp.broadcast_to(new, (8, PART))

    link = (par_ref[...] == iota((TOK, TOK), 0)) | (iota((TOK, TOK), 0) == iota((TOK, TOK), 1))
    link = link.astype(F32).astype(BF)
    for _ in range(8):
        link = jnp.minimum(dot(link, link), 1.0).astype(BF)
    rows64 = GROUPS * 8
    take = iota((rows64, TOK), 1) == me * 8 + iota((rows64, TOK), 0) // GROUPS
    allowed = dot_t(take.astype(F32).astype(BF), link) > 0.5

    def head(ref, at):
        zero, one = ref[:, at : at + WIDTH], ref[:, at + WIDTH : at + 2 * WIDTH]
        return jnp.where(side == 0, zero, one)

    def rows_of(at):
        near, far = head(tree_ref, at), head(far_ref, at)
        return jnp.concatenate(
            [jnp.where(side == 0, near, far), jnp.where(side == 0, far, near)], axis=0
        )

    dq = dq_ref[pl.ds(pl.multiple_of(me * rows64, rows64), rows64), :]
    s = jnp.where(allowed, dot_t(dq, rows_of(0)) * COEF, NEG)
    v_t = jnp.transpose(rows_of(2 * WIDTH).astype(F32)).astype(BF)
    verify_update(s, v_t, mv_ref, lv_ref, av_ref, start=True)
    clipped_source(own_ref, 0, me, me, kc_ref, vc_ref, 0, ck_ref, cv_ref, b_ref)
    verify_update(dot_t(dq, kc_ref[...]) * COEF, joined(vc_ref, 0, 2), mv_ref, lv_ref, av_ref)


def flash_chunks(q_ref, q_at, half, k_ref, v_ref, base, chunks, m_ref, acc_ref):
    span = SLOTS * HALF

    def chunk(i, _):
        slot = base + i * SLOTS
        k = k_ref[pl.ds(pl.multiple_of(slot * HALF, HALF), span), :]
        v = joined(v_ref, slot, SLOTS)

        def scores(t):
            q = q_ref[pl.ds(pl.multiple_of(q_at + t * PART, PART), PART), :]
            return dot_t(k, q) * COEF

        s = scores(0)
        for t in range(QH // PART):
            ahead = scores(t + 1) if t + 1 < QH // PART else None
            cols = slice(t * PART, (t + 1) * PART)
            old = m_ref[half, 0:1, cols]
            new, p = weights_of(s, old)
            acc_ref[half, :, cols] = acc_ref[half, :, cols] * jnp.exp2(old - new) + dot(v, p)
            m_ref[half, :, cols] = jnp.broadcast_to(new, (8, PART))
            s = ahead
        return 0

    lax.fori_loop(0, chunks, chunk, 0)


def step_kernel(layout, last, *refs):
    n_in = len(layout)
    q_ref, own_ref, dq_ref = refs[:3]
    srcs = refs[3 : 3 + n_in]
    state = refs[3 + n_in + len(STATE) : 3 + n_in + 2 * len(STATE)]
    if last:
        out_ref, ver_ref, ok_ref, ov_ref = refs[3 + n_in + 2 * len(STATE) :][:4]
    kk_ref, vv_ref, kc_ref, vc_ref, b_ref = refs[-5:]
    m_ref, acc_ref, mv_ref, lv_ref, av_ref, ck_ref, cv_ref = state
    me, z, x = me_index(), lax.axis_index("z"), lax.axis_index("x")
    first = first_of(own_ref, 0)
    swap = (first >= PAGES).astype(jnp.int32)
    mine = jnp.minimum(first, 2 * PAGES - 1 - first)
    blocks = [(r, i * PAY, d) for r, ds in zip(srcs, layout) for i, d in enumerate(ds)]
    n = len(blocks)
    lo_base = 2 * n + SLOTS
    ones = jnp.ones((EXTRA, HALF), BF)
    n_hi, n_lo = jnp.int32(0), jnp.int32(0)
    for i, (ref, base, _) in enumerate(blocks):
        f = first_of(ref, base)
        other = (f >= PAGES).astype(jnp.int32)
        later = (jnp.minimum(f, 2 * PAGES - 1 - f) > mine).astype(jnp.int32)
        lo = base + other * HALF
        hi = base + HALF - other * HALF
        sel = jnp.where(later == 1, hi, lo)
        to = jnp.where(later == 1, n + n_hi, lo_base + n_lo)
        kk_ref[i * HALF : (i + 1) * HALF, :] = ref[pl.ds(pl.multiple_of(lo, 16), HALF), :]
        vv_ref[i, :WIDTH, :] = ref[pl.ds(pl.multiple_of(lo + TOK, 16), HALF), :]
        vv_ref[i, WIDTH:, :] = ones
        at = pl.ds(pl.multiple_of(to * HALF, HALF), HALF)
        kk_ref[at, :] = ref[pl.ds(pl.multiple_of(sel, 16), HALF), :]
        vv_ref[to, :WIDTH, :] = ref[pl.ds(pl.multiple_of(sel + TOK, 16), HALF), :]
        vv_ref[to, WIDTH:, :] = ones
        n_hi, n_lo = n_hi + later, n_lo + 1 - later
    for start, count in ((0, n + n_hi), (lo_base, n_lo)):
        for j in range(SLOTS - 1):
            at = pl.ds(pl.multiple_of((start + count + j) * HALF, HALF), HALF)
            kk_ref[at, :] = kk_ref[start * HALF : (start + 1) * HALF, :]
            vv_ref[start + count + j] = jnp.zeros((DEEP, HALF), BF)
    q_lo = swap * QH
    q_hi = QH - swap * QH
    ways = ((q_hi, 1, 0, n + n_hi), (q_lo, 0, lo_base, n_lo))
    for q_at, half, base, count in ways:
        chunks = (count + SLOTS - 1) // SLOTS
        flash_chunks(q_ref, q_at, half, kk_ref, vv_ref, base, chunks, m_ref, acc_ref)

    for i, (ref, base, (dz, dx)) in enumerate(blocks):
        col = ((z + dz + 8) % 8) * 4 + (x + dx + 4) % 4
        clipped_source(ref, base, col, me, kc_ref, vc_ref, i, ck_ref, cv_ref, b_ref)
    rows64 = GROUPS * 8
    dq = dq_ref[pl.ds(pl.multiple_of(me * rows64, rows64), rows64), :]
    verify_update(dot_t(dq, kc_ref[...]) * COEF, joined(vc_ref, 0, 2 * n), mv_ref, lv_ref, av_ref)
    if last:
        for t in range(QH // PART):
            cols = slice(t * PART, (t + 1) * PART)
            for at, half in ((q_hi, 1), (q_lo, 0)):
                a = acc_ref[half, :, cols]
                out = jnp.transpose(a[:WIDTH] / a[WIDTH : WIDTH + 1])
                out_ref[pl.ds(pl.multiple_of(at + t * PART, PART), PART), :] = out.astype(BF)
        ver_ref[...] = (av_ref[...] / lv_ref[...]).astype(BF)
        ok_ref[...] = ck_ref[...].astype(BF)
        ov_ref[...] = cv_ref[...].astype(BF)


STATE = [
    pltpu.VMEM((2, 8, QH), F32),
    pltpu.VMEM((2, DEEP, QH), F32),
    pltpu.VMEM((64, WIDTH), F32),
    pltpu.VMEM((64, WIDTH), F32),
    pltpu.VMEM((64, WIDTH), F32),
    pltpu.VMEM((TOK, WIDTH), F32),
    pltpu.VMEM((TOK, WIDTH), F32),
]
GRANT = pltpu.CompilerParams(vmem_limit_bytes=40 * 1024 * 1024)


def cost(n):
    return pl.CostEstimate(
        flops=n * 4 * TOK * QH * WIDTH, bytes_accessed=n * PAY * WIDTH * 2, transcendentals=0
    )


def step(q, own, dq, sources, layout, state, last=False):
    n = sum(len(d) for d in layout)
    outs = STATE
    alias = {3 + len(layout) + i: i for i in range(len(STATE))}
    if last:
        outs = STATE + [
            jax.ShapeDtypeStruct((2 * QH, WIDTH), BF),
            jax.ShapeDtypeStruct((64, WIDTH), BF),
            jax.ShapeDtypeStruct((TOK, WIDTH), BF),
            jax.ShapeDtypeStruct((TOK, WIDTH), BF),
        ]
    slots = 3 * n + 2 * SLOTS
    return pl.pallas_call(
        functools.partial(step_kernel, layout, last),
        out_shape=outs,
        in_specs=vmem(3 + len(layout) + len(STATE)),
        out_specs=vmem(len(outs)),
        scratch_shapes=[
            pltpu.VMEM((slots * HALF, WIDTH), BF),
            pltpu.VMEM((slots, DEEP, HALF), BF),
            pltpu.VMEM((n * TOK, WIDTH), BF),
            pltpu.VMEM((2 * n, HALF, WIDTH), BF),
            pltpu.VMEM((n * PAGES, WIDTH), F32),
        ],
        input_output_aliases=alias,
        cost_estimate=cost(n),
        compiler_params=GRANT,
    )(*(held(a) for a in (q, own, dq, *sources, *state)))


def shift(b, axis, d):
    n = lax.axis_size(axis)
    return lax.ppermute(b, axis, [(i, (i + d) % n) for i in range(n)])


def work(
    prefill_query, prefill_keys, prefill_values, token_pos, scale_exp, page_owner,
    draft_query, draft_keys, draft_values, parents,
):
    q = prefill_query.reshape(2 * QH, WIDTH)
    dq = draft_query.reshape(2 * QH, WIDTH)
    own = pl.pallas_call(
        pack_kernel,
        out_shape=pltpu.VMEM((PAY, WIDTH), BF),
        compiler_params=pltpu.CompilerParams(vmem_limit_bytes=4 * 1024 * 1024),
        in_specs=[pl.BlockSpec(memory_space=pl.ANY)] * 5,
        out_specs=vmem(1)[0],
        scratch_shapes=[
            pltpu.SMEM((TOK,), jnp.int32),
            pltpu.VMEM((2, PAGES), jnp.int32),
            pltpu.VMEM((1, PAGES), jnp.int32),
            pltpu.VMEM((TOK, WIDTH), BF),
            pltpu.SemaphoreType.DMA((5,)),
        ],
        name="pack",
    )(
        outside(token_pos),
        outside(jnp.transpose(scale_exp, (1, 2, 0)).reshape(2, PAGES)),
        outside(page_owner.reshape(1, PAGES)),
        outside(prefill_keys.reshape(TOK, WIDTH)),
        outside(prefill_values.reshape(TOK, WIDTH)),
    )
    tree = jnp.concatenate(
        [draft_keys.reshape(HALF, 2 * WIDTH), draft_values.reshape(HALF, 2 * WIDTH)], axis=1
    )
    xs = [shift(own, "x", 1), shift(own, "x", -1), shift(own, "x", 2)]
    far = shift(tree, "side", 1)
    near_x = jnp.concatenate(xs, axis=0)
    own_call = pl.pallas_call(
        own_kernel,
        out_shape=STATE,
        in_specs=vmem(6),
        out_specs=vmem(len(STATE)),
        scratch_shapes=[
            pltpu.VMEM((TOK, WIDTH), BF),
            pltpu.VMEM((2, HALF, WIDTH), BF),
            pltpu.VMEM((PAGES, WIDTH), F32),
        ],
        cost_estimate=cost(2),
        compiler_params=GRANT,
        name="own",
    )
    state = own_call(*(held(a) for a in (q, own, dq, tree, far)), parents.reshape(1, TOK))
    dxs = (-1, 1, 2)
    state = step(q, own, dq, [near_x], [[(0, d) for d in dxs]], state)
    ra = la = own
    rb = lb = near_x
    for s in range(1, 4):
        ra, la = shift(ra, "z", 1), shift(la, "z", -1)
        rb, lb = shift(rb, "z", 1), shift(lb, "z", -1)
        state = step(
            q, own, dq, [ra, la, rb, lb],
            [[(-s, 0)], [(s, 0)], [(-s, d) for d in dxs], [(s, d) for d in dxs]],
            state,
        )
    oa = shift(la, "z", -1)
    ob = shift(rb[: 2 * PAY], "z", 1)
    oc = shift(lb[2 * PAY :], "z", -1)
    out, ver, ck, cv = step(
        q, own, dq, [oa, ob, oc],
        [[(4, 0)], [(4, d) for d in dxs[:2]], [(4, dxs[2])]],
        state, last=True,
    )[len(STATE) :]
    return (
        out.reshape(TOK, GROUPS, WIDTH),
        ck.reshape(TOK, 1, WIDTH),
        cv.reshape(TOK, 1, WIDTH),
        ver.reshape(8, GROUPS, WIDTH),
    )


def solution(mesh):
    finer = Mesh(
        mesh.devices.reshape(8, 4, mesh.shape["head"], mesh.shape["side"]),
        ("z", "x", "head", "side"),
    )
    full = P(CTX, ("head", "side"), None)
    in_specs = (
        full, full, full, P(CTX), full, P(CTX),
        P(None, ("head", "side"), None),
        P("side", "head", None), P("side", "head", None), P(),
    )
    return jax.shard_map(
        work, mesh=finer, in_specs=in_specs, out_specs=(full, full, full, full), check_vma=False
    )
```

time: 99.7 us -> 88.7 us (0.89)
  Pallas kernels: 38.6 us -> 31.4 us
  local copies, waits for them, and re-layouts: 3.14 us -> 0.95 us
  waiting for transfers between devices: 22.2 us -> 20.7 us
    pallas_call x5, Pallas kernels: 34.5 us -> 27 us  [step(): pl.pallas_call(functools.partial(step_kernel, layout, last), out_shape=ou...]
    unnamed x23 -> x11, local copies, waits for them, and re-layouts: 3.08 us -> 0.89 us
    ppermute x19, waiting for transfers between devices: 22.2 us -> 20.7 us  [shift(): return lax.ppermute(b, axis, [(i, (i + d) % n) for i in range(n)])]
  transfers between devices with their start and end apart: 19 -> 19, of which waited for: 6 -> 6; matrix products, arithmetic and copies ran while one was open for 0% -> 1% of each run, Pallas kernels for 32% -> 29%
where the time goes in v1:
time: 88.7 us; the launch traced here: 88.5 us
  starting transfers between devices  34.6 us (39%)
  Pallas kernels  31.4 us (35%)
  waiting for transfers between devices  20.7 us (23%)
  local copies, waits for them, and re-layouts  0.95 us (1%)
    ppermute x19, starting transfers between devices, shift(): return lax.ppermute(b, axis, [(i, (i + d) % n) for i in range(n)])  34.6 us
    pallas_call x5, Pallas kernels, step(): pl.pallas_call(functools.partial(step_kernel, layout, last), out_shape=ou...  27 us
    ppermute x19, waiting for transfers between devices, shift(): return lax.ppermute(b, axis, [(i, (i + d) % n) for i in range(n)])  20.7 us
    pallas_call x1, Pallas kernels, work(): own_call(*(held(a) for a in (q, own, dq, tree, far)), parents.reshape(1,...  3.29 us
  transfers between devices with their start and end apart: 19, of which 6 were waited for; matrix products, arithmetic and copies ran while one was open for 1% of the time, Pallas kernels for 29%

profile of v1, /device:TPU:8, one launch (start us, length us, event | category | flops | bytes accessed | tf_op | source)
XLA Modules:
  0.0 88.5 jit_solution(11728761976301548501)
XLA Ops:
  0.7 1.1 %pack.1.own_ref.refs_1_ = bf16[528,128]{1,0:T(8,128)(2,1)S(1)} custom-call(s32[256]{0:T(256)} %pos_hbm.1, s32[2,32]{1,0:T(2,128)} %bitcast.36, s32[1,32]{1,0:T(1,128)} %bitcast.37, bf16[256,128]{1,0:T(8,128)(2,1)} %bitcast.34, bf16[256,128]{1,0:T(8,128)(2,1)} %bitcast.35), custom_call_target="tpu_custom_call" | custom-call | tf_op jit(solution)/shard_map/pack/pallas_call | solution.py:371
  1.8 1.6 %collective-permute-start.4 = (bf16[528,128]{1,0:T(8,128)(2,1)S(1)}, bf16[528,128]{1,0:T(8,128)(2,1)S(1)}, u32[]{:S(2)}, u32[]{:S(2)}) collective-permute-start(bf16[528,128]{1,0:T(8,128)(2,1)S(1)} %pack.1.own_ref.refs_1_), channel_id=1, source_target_pairs={{0,8},{8,16},{16,24},{24,0},{1,9},{9,17},{17,25},{25,1},{2,10},{10... | collective-permute-start | bytes 405512 | tf_op jit(solution)/shard_map/ppermute | solution.py:362
  3.4 1.7 %collective-permute-start.5 = (bf16[528,128]{1,0:T(8,128)(2,1)S(1)}, bf16[528,128]{1,0:T(8,128)(2,1)S(1)}, u32[]{:S(2)}, u32[]{:S(2)}) collective-permute-start(bf16[528,128]{1,0:T(8,128)(2,1)S(1)} %pack.1.own_ref.refs_1_), channel_id=1, source_target_pairs={{0,24},{8,0},{16,8},{24,16},{1,25},{9,1},{17,9},{25,17},{2,26},{10... | collective-permute-start | bytes 405512 | tf_op jit(solution)/shard_map/ppermute | solution.py:362
  5.1 1.8 %collective-permute-start.6 = (bf16[528,128]{1,0:T(8,128)(2,1)S(1)}, bf16[528,128]{1,0:T(8,128)(2,1)S(1)}, u32[]{:S(2)}, u32[]{:S(2)}) collective-permute-start(bf16[528,128]{1,0:T(8,128)(2,1)S(1)} %pack.1.own_ref.refs_1_), channel_id=1, source_target_pairs={{0,16},{8,24},{16,0},{24,8},{1,17},{9,25},{17,1},{25,9},{2,18},{10... | collective-permute-start | bytes 405512 | tf_op jit(solution)/shard_map/ppermute | solution.py:362
  7.0 1.5 %collective-permute-done.4 = bf16[528,128]{1,0:T(8,128)(2,1)S(1)} collective-permute-done((bf16[528,128]{1,0:T(8,128)(2,1)S(1)}, bf16[528,128]{1,0:T(8,128)(2,1)S(1)}, u32[]{:S(2)}, u32[]{:S(2)}) %collective-permute-start.4) | collective-permute-done | bytes 135200 | tf_op jit(solution)/shard_map/ppermute | solution.py:362
  8.4 2.2 %collective-permute-done.5 = bf16[528,128]{1,0:T(8,128)(2,1)S(1)} collective-permute-done((bf16[528,128]{1,0:T(8,128)(2,1)S(1)}, bf16[528,128]{1,0:T(8,128)(2,1)S(1)}, u32[]{:S(2)}, u32[]{:S(2)}) %collective-permute-start.5) | collective-permute-done | bytes 135200 | tf_op jit(solution)/shard_map/ppermute | solution.py:362
  10.7 1.7 %collective-permute-done.6 = bf16[528,128]{1,0:T(8,128)(2,1)S(1)} collective-permute-done((bf16[528,128]{1,0:T(8,128)(2,1)S(1)}, bf16[528,128]{1,0:T(8,128)(2,1)S(1)}, u32[]{:S(2)}, u32[]{:S(2)}) %collective-permute-start.6) | collective-permute-done | bytes 135200 | tf_op jit(solution)/shard_map/ppermute | solution.py:362
  12.3 5.9 %collective-permute-start.11 = (bf16[1584,128]{1,0:T(8,128)(2,1)S(1)}, bf16[1584,128]{1,0:T(8,128)(2,1)S(1)}, u32[]{:S(2)}, u32[]{:S(2)}) collective-permute-start(bf16[1584,128]{1,0:T(8,128)(2,1)S(1)} %constant_dynamic-update-slice_fusion.refs_3_), channel_id=1, source_target_pairs={{0,224},{32,0},{64,32},{96,64},{128,96},{160,128},{192,160},{224,1... | collective-permute-start | bytes 1216520 | tf_op jit(solution)/shard_map/ppermute | solution.py:362
  18.3 0.0 collective-permute-start.7
  18.3 8.0 %collective-permute-done.11.refs_6_ = bf16[1584,128]{1,0:T(8,128)(2,1)S(1)} collective-permute-done((bf16[1584,128]{1,0:T(8,128)(2,1)S(1)}, bf16[1584,128]{1,0:T(8,128)(2,1)S(1)}, u32[]{:S(2)}, u32[]{:S(2)}) %collective-permute-start.11) | collective-permute-done | bytes 405536 | tf_op jit(solution)/shard_map/ppermute | solution.py:362
  26.3 3.7 %collective-permute-start.12 = (bf16[1584,128]{1,0:T(8,128)(2,1)S(1)}, bf16[1584,128]{1,0:T(8,128)(2,1)S(1)}, u32[]{:S(2)}, u32[]{:S(2)}) collective-permute-start(bf16[1584,128]{1,0:T(8,128)(2,1)S(1)} %collective-permute-done.11.refs_6_), channel_id=1, source_target_pairs={{0,224},{32,0},{64,32},{96,64},{128,96},{160,128},{192,160},{224,1... | collective-permute-start | bytes 1216520 | tf_op jit(solution)/shard_map/ppermute | solution.py:362
  30.0 0.0 collective-permute-done.7.refs_5_
  30.0 3.2 %collective-permute-start = (bf16[528,128]{1,0:T(8,128)(2,1)S(1)}, bf16[528,128]{1,0:T(8,128)(2,1)S(1)}, u32[]{:S(2)}, u32[]{:S(2)}) collective-permute-start(bf16[528,128]{1,0:T(8,128)(2,1)S(1)} %pack.1.own_ref.refs_1_), channel_id=1, source_target_pairs={{0,224},{32,0},{64,32},{96,64},{128,96},{160,128},{192,160},{224,1... | collective-permute-start | bytes 405512 | tf_op jit(solution)/shard_map/ppermute | solution.py:362
  33.2 0.8 bitcast_dynamic-update-slice_fusion.1
  34.1 6.0 %collective-permute-done.refs_4_ = bf16[528,128]{1,0:T(8,128)(2,1)S(1)} collective-permute-done((bf16[528,128]{1,0:T(8,128)(2,1)S(1)}, bf16[528,128]{1,0:T(8,128)(2,1)S(1)}, u32[]{:S(2)}, u32[]{:S(2)}) %collective-permute-start) | collective-permute-done | bytes 135200 | tf_op jit(solution)/shard_map/ppermute | solution.py:362
  40.0 3.7 %collective-permute-start.1 = (bf16[528,128]{1,0:T(8,128)(2,1)S(1)}, bf16[528,128]{1,0:T(8,128)(2,1)S(1)}, u32[]{:S(2)}, u32[]{:S(2)}) collective-permute-start(bf16[528,128]{1,0:T(8,128)(2,1)S(1)} %collective-permute-done.refs_4_), channel_id=1, source_target_pairs={{0,224},{32,0},{64,32},{96,64},{128,96},{160,128},{192,160},{224,1... | collective-permute-start | bytes 405512 | tf_op jit(solution)/shard_map/ppermute | solution.py:362
  43.7 0.0 collective-permute-start.13
  43.7 2.0 %collective-permute-start.9 = (bf16[1584,128]{1,0:T(8,128)(2,1)S(1)}, bf16[1584,128]{1,0:T(8,128)(2,1)S(1)}, u32[]{:S(2)}, u32[]{:S(2)}) collective-permute-start(bf16[1584,128]{1,0:T(8,128)(2,1)S(1)} %collective-permute-done.8.refs_5_), channel_id=1, source_target_pairs={{0,32},{32,64},{64,96},{96,128},{128,160},{160,192},{192,224},{224... | collective-permute-start | bytes 1216520 | tf_op jit(solution)/shard_map/ppermute | solution.py:362
  45.8 0.5 collective-permute-start.18
  46.3 0.0 collective-permute-start.16
  46.3 1.4 %collective-permute-done.1.refs_4_ = bf16[528,128]{1,0:T(8,128)(2,1)S(1)} collective-permute-done((bf16[528,128]{1,0:T(8,128)(2,1)S(1)}, bf16[528,128]{1,0:T(8,128)(2,1)S(1)}, u32[]{:S(2)}, u32[]{:S(2)}) %collective-permute-start.1) | collective-permute-done | bytes 135200 | tf_op jit(solution)/shard_map/ppermute | solution.py:362
  47.7 3.7 %collective-permute-start.2 = (bf16[528,128]{1,0:T(8,128)(2,1)S(1)}, bf16[528,128]{1,0:T(8,128)(2,1)S(1)}, u32[]{:S(2)}, u32[]{:S(2)}) collective-permute-start(bf16[528,128]{1,0:T(8,128)(2,1)S(1)} %collective-permute-done.1.refs_4_), channel_id=1, source_target_pairs={{0,224},{32,0},{64,32},{96,64},{128,96},{160,128},{192,160},{224,1... | collective-permute-start | bytes 405512 | tf_op jit(solution)/shard_map/ppermute | solution.py:362
  51.4 3.3 %own.1 = (f32[2,8,1024]{2,1,0:T(8,128)S(1)}, f32[2,144,1024]{2,1,0:T(8,128)S(1)}, f32[64,128]{1,0:T(8,128)S(1)}, f32[64,128]{1,0:T(8,128)S(1)}, f32[64,128]{1,0:...) custom-call(bf16[2048,128]{1,0:T(8,128)(2,1)S(1)} %bitcast.19, bf16[528,128]{1,0:T(8,128)(2,1)S(1)} %pack.1.own_ref.refs_1_, ...), custom_call_target="tpu_custom_call" | custom-call | flops 268435456 | bytes 270336 | tf_op jit(solution)/shard_map/own/pallas_call | solution.py:412
  54.7 2.9 %shard_map.129 = (f32[2,8,1024]{2,1,0:T(8,128)S(1)}, f32[2,144,1024]{2,1,0:T(8,128)S(1)}, f32[64,128]{1,0:T(8,128)S(1)}, f32[64,128]{1,0:T(8,128)S(1)}, f32[64,1...) custom-call(bf16[2048,128]{1,0:T(8,128)(2,1)S(1)} %bitcast.20, ...), custom_call_target="tpu_custom_call", output_to_operand_aliasing={{0}: (4, {}), {1}: (5, {}), {2}: (6, {}), {3}: (7, {}), {4}... | custom-call | flops 402653184 | bytes 405504 | tf_op jit(solution)/shard_map/pallas_call | solution.py:342
  57.6 0.3 collective-permute-start.17
  57.9 3.0 %collective-permute-start.3 = (bf16[528,128]{1,0:T(8,128)(2,1)S(1)}, bf16[528,128]{1,0:T(8,128)(2,1)S(1)}, u32[]{:S(2)}, u32[]{:S(2)}) collective-permute-start(bf16[528,128]{1,0:T(8,128)(2,1)S(1)} %collective-permute-done.2.refs_4_), channel_id=1, source_target_pairs={{0,224},{32,0},{64,32},{96,64},{128,96},{160,128},{192,160},{224,1... | collective-permute-start | bytes 405512 | tf_op jit(solution)/shard_map/ppermute | solution.py:362
  61.0 0.1 collective-permute-start.10
  61.1 6.4 %shard_map.130 = (f32[2,8,1024]{2,1,0:T(8,128)S(1)}, f32[2,144,1024]{2,1,0:T(8,128)S(1)}, f32[64,128]{1,0:T(8,128)S(1)}, f32[64,128]{1,0:T(8,128)S(1)}, f32[64,1...) custom-call(bf16[2048,128]{1,0:T(8,128)(2,1)S(1)} %bitcast.21, ...), custom_call_target="tpu_custom_call", output_to_operand_aliasing={{0}: (7, {}), {1}: (8, {}), {2}: (9, {}), {3}: (10, {}), {4... | custom-call | flops 1073741824 | bytes 1081344 | tf_op jit(solution)/shard_map/pallas_call | solution.py:342
  67.5 3.3 %collective-permute-start.14 = (bf16[528,128]{1,0:T(8,128)(2,1)S(1)}, bf16[528,128]{1,0:T(8,128)(2,1)S(1)}, u32[]{:S(2)}, u32[]{:S(2)}) collective-permute-start(bf16[528,128]{1,0:T(8,128)(2,1)S(1)} %slice.9), channel_id=1, source_target_pairs={{0,224},{32,0},{64,32},{96,64},{128,96},{160,128},{192,160},{224,1... | collective-permute-start | bytes 405512 | tf_op jit(solution)/shard_map/ppermute | solution.py:362
  70.7 6.6 %shard_map.131 = (f32[2,8,1024]{2,1,0:T(8,128)S(1)}, f32[2,144,1024]{2,1,0:T(8,128)S(1)}, f32[64,128]{1,0:T(8,128)S(1)}, f32[64,128]{1,0:T(8,128)S(1)}, f32[64,1...) custom-call(bf16[2048,128]{1,0:T(8,128)(2,1)S(1)} %bitcast.22, ...), custom_call_target="tpu_custom_call", output_to_operand_aliasing={{0}: (7, {}), {1}: (8, {}), {2}: (9, {}), {3}: (10, {}), {4... | custom-call | flops 1073741824 | bytes 1081344 | tf_op jit(solution)/shard_map/pallas_call | solution.py:342
  77.3 6.4 %shard_map.132 = (f32[2,8,1024]{2,1,0:T(8,128)S(1)}, f32[2,144,1024]{2,1,0:T(8,128)S(1)}, f32[64,128]{1,0:T(8,128)S(1)}, f32[64,128]{1,0:T(8,128)S(1)}, f32[64,1...) custom-call(bf16[2048,128]{1,0:T(8,128)(2,1)S(1)} %bitcast.23, ...), custom_call_target="tpu_custom_call", output_to_operand_aliasing={{0}: (7, {}), {1}: (8, {}), {2}: (9, {}), {3}: (10, {}), {4... | custom-call | flops 1073741824 | bytes 1081344 | tf_op jit(solution)/shard_map/pallas_call | solution.py:342
  83.7 4.8 %shard_map.133 = (f32[2,8,1024]{2,1,0:T(8,128)S(1)}, f32[2,144,1024]{2,1,0:T(8,128)S(1)}, f32[64,128]{1,0:T(8,128)S(1)}, f32[64,128]{1,0:T(8,128)S(1)}, f32[64,1...) custom-call(bf16[2048,128]{1,0:T(8,128)(2,1)S(1)} %bitcast.24, ...), custom_call_target="tpu_custom_call", output_to_operand_aliasing={{0}: (6, {}), {1}: (7, {}), {2}: (8, {}), {3}: (9, {}), {4}... | custom-call | flops 536870912 | bytes 540672 | tf_op jit(solution)/shard_map/pallas_call | solution.py:342
  (28 shorter events, 0.1 us)
Async XLA Ops:
  0.6 45.1 %copy-start.3 = (bf16[128,2,128]{2,1,0:T(2,128)(2,1)S(1)}, bf16[128,2,128]{2,1,0:T(2,128)(2,1)}, u32[]{:S(2)}) copy-start(bf16[128,2,128]{2,1,0:T(2,128)(2,1)} %param.18) | copy-start | bytes 196612
  0.6 50.7 %copy-start = (bf16[256,8,128]{2,1,0:T(8,128)(2,1)S(1)}, bf16[256,8,128]{2,1,0:T(8,128)(2,1)}, u32[]{:S(2)}) copy-start(bf16[256,8,128]{2,1,0:T(8,128)(2,1)} %param.10) | copy-start | bytes 1572868
  0.7 50.7 %copy-start.1 = (bf16[256,8,128]{2,1,0:T(8,128)(2,1)S(1)}, bf16[256,8,128]{2,1,0:T(8,128)(2,1)}, u32[]{:S(2)}) copy-start(bf16[256,8,128]{2,1,0:T(8,128)(2,1)} %param.16) | copy-start | bytes 1572868
  0.7 50.7 %copy-start.2 = (s32[256]{0:T(256)S(1)}, s32[256]{0:T(256)}, u32[]{:S(2)}) copy-start(s32[256]{0:T(256)} %param.19) | copy-start | bytes 3076
  1.8 6.6 %collective-permute-start.4 = (bf16[528,128]{1,0:T(8,128)(2,1)S(1)}, bf16[528,128]{1,0:T(8,128)(2,1)S(1)}, u32[]{:S(2)}, u32[]{:S(2)}) collective-permute-start(bf16[528,128]{1,0:T(8,128)(2,1)S(1)} %pack.1.own_ref.refs_1_), channel_id=1, source_target_pairs={{0,8},{8,16},{16,24},{24,0},{1,9},{9,17},{17,25},{25,1},{2,10},{10... | collective-permute-start | bytes 405512 | tf_op jit(solution)/shard_map/ppermute | solution.py:362
  3.4 7.2 %collective-permute-start.5 = (bf16[528,128]{1,0:T(8,128)(2,1)S(1)}, bf16[528,128]{1,0:T(8,128)(2,1)S(1)}, u32[]{:S(2)}, u32[]{:S(2)}) collective-permute-start(bf16[528,128]{1,0:T(8,128)(2,1)S(1)} %pack.1.own_ref.refs_1_), channel_id=1, source_target_pairs={{0,24},{8,0},{16,8},{24,16},{1,25},{9,1},{17,9},{25,17},{2,26},{10... | collective-permute-start | bytes 405512 | tf_op jit(solution)/shard_map/ppermute | solution.py:362
  5.1 7.2 %collective-permute-start.6 = (bf16[528,128]{1,0:T(8,128)(2,1)S(1)}, bf16[528,128]{1,0:T(8,128)(2,1)S(1)}, u32[]{:S(2)}, u32[]{:S(2)}) collective-permute-start(bf16[528,128]{1,0:T(8,128)(2,1)S(1)} %pack.1.own_ref.refs_1_), channel_id=1, source_target_pairs={{0,16},{8,24},{16,0},{24,8},{1,17},{9,25},{17,1},{25,9},{2,18},{10... | collective-permute-start | bytes 405512 | tf_op jit(solution)/shard_map/ppermute | solution.py:362
  12.3 13.9 %collective-permute-start.11 = (bf16[1584,128]{1,0:T(8,128)(2,1)S(1)}, bf16[1584,128]{1,0:T(8,128)(2,1)S(1)}, u32[]{:S(2)}, u32[]{:S(2)}) collective-permute-start(bf16[1584,128]{1,0:T(8,128)(2,1)S(1)} %constant_dynamic-update-slice_fusion.refs_3_), channel_id=1, source_target_pairs={{0,224},{32,0},{64,32},{96,64},{128,96},{160,128},{192,160},{224,1... | collective-permute-start | bytes 1216520 | tf_op jit(solution)/shard_map/ppermute | solution.py:362
  18.3 11.7 %collective-permute-start.7 = (bf16[1584,128]{1,0:T(8,128)(2,1)S(1)}, bf16[1584,128]{1,0:T(8,128)(2,1)S(1)}, u32[]{:S(2)}, u32[]{:S(2)}) collective-permute-start(bf16[1584,128]{1,0:T(8,128)(2,1)S(1)} %constant_dynamic-update-slice_fusion.refs_3_), channel_id=1, source_target_pairs={{0,32},{32,64},{64,96},{96,128},{128,160},{160,192},{192,224},{224... | collective-permute-start | bytes 1216520 | tf_op jit(solution)/shard_map/ppermute | solution.py:362
  26.3 17.4 %collective-permute-start.12 = (bf16[1584,128]{1,0:T(8,128)(2,1)S(1)}, bf16[1584,128]{1,0:T(8,128)(2,1)S(1)}, u32[]{:S(2)}, u32[]{:S(2)}) collective-permute-start(bf16[1584,128]{1,0:T(8,128)(2,1)S(1)} %collective-permute-done.11.refs_6_), channel_id=1, source_target_pairs={{0,224},{32,0},{64,32},{96,64},{128,96},{160,128},{192,160},{224,1... | collective-permute-start | bytes 1216520 | tf_op jit(solution)/shard_map/ppermute | solution.py:362
  30.0 13.8 %collective-permute-start.8 = (bf16[1584,128]{1,0:T(8,128)(2,1)S(1)}, bf16[1584,128]{1,0:T(8,128)(2,1)S(1)}, u32[]{:S(2)}, u32[]{:S(2)}) collective-permute-start(bf16[1584,128]{1,0:T(8,128)(2,1)S(1)} %collective-permute-done.7.refs_5_), channel_id=1, source_target_pairs={{0,32},{32,64},{64,96},{96,128},{128,160},{160,192},{192,224},{224... | collective-permute-start | bytes 1216520 | tf_op jit(solution)/shard_map/ppermute | solution.py:362
  30.0 10.0 %collective-permute-start = (bf16[528,128]{1,0:T(8,128)(2,1)S(1)}, bf16[528,128]{1,0:T(8,128)(2,1)S(1)}, u32[]{:S(2)}, u32[]{:S(2)}) collective-permute-start(bf16[528,128]{1,0:T(8,128)(2,1)S(1)} %pack.1.own_ref.refs_1_), channel_id=1, source_target_pairs={{0,224},{32,0},{64,32},{96,64},{128,96},{160,128},{192,160},{224,1... | collective-permute-start | bytes 405512 | tf_op jit(solution)/shard_map/ppermute | solution.py:362
  33.2 13.1 %collective-permute-start.15 = (bf16[528,128]{1,0:T(8,128)(2,1)S(1)}, bf16[528,128]{1,0:T(8,128)(2,1)S(1)}, u32[]{:S(2)}, u32[]{:S(2)}) collective-permute-start(bf16[528,128]{1,0:T(8,128)(2,1)S(1)} %pack.1.own_ref.refs_1_), channel_id=1, source_target_pairs={{0,32},{32,64},{64,96},{96,128},{128,160},{160,192},{192,224},{224... | collective-permute-start | bytes 405512 | tf_op jit(solution)/shard_map/ppermute | solution.py:362
  40.0 7.7 %collective-permute-start.1 = (bf16[528,128]{1,0:T(8,128)(2,1)S(1)}, bf16[528,128]{1,0:T(8,128)(2,1)S(1)}, u32[]{:S(2)}, u32[]{:S(2)}) collective-permute-start(bf16[528,128]{1,0:T(8,128)(2,1)S(1)} %collective-permute-done.refs_4_), channel_id=1, source_target_pairs={{0,224},{32,0},{64,32},{96,64},{128,96},{160,128},{192,160},{224,1... | collective-permute-start | bytes 405512 | tf_op jit(solution)/shard_map/ppermute | solution.py:362
  43.7 23.7 %collective-permute-start.13 = (bf16[1584,128]{1,0:T(8,128)(2,1)S(1)}, bf16[1584,128]{1,0:T(8,128)(2,1)S(1)}, u32[]{:S(2)}, u32[]{:S(2)}) collective-permute-start(bf16[1584,128]{1,0:T(8,128)(2,1)S(1)} %collective-permute-done.12.refs_6_), channel_id=1, source_target_pairs={{0,224},{32,0},{64,32},{96,64},{128,96},{160,128},{192,160},{224,1... | collective-permute-start | bytes 1216520 | tf_op jit(solution)/shard_map/ppermute | solution.py:362
  43.7 17.2 %collective-permute-start.9 = (bf16[1584,128]{1,0:T(8,128)(2,1)S(1)}, bf16[1584,128]{1,0:T(8,128)(2,1)S(1)}, u32[]{:S(2)}, u32[]{:S(2)}) collective-permute-start(bf16[1584,128]{1,0:T(8,128)(2,1)S(1)} %collective-permute-done.8.refs_5_), channel_id=1, source_target_pairs={{0,32},{32,64},{64,96},{96,128},{128,160},{160,192},{192,224},{224... | collective-permute-start | bytes 1216520 | tf_op jit(solution)/shard_map/ppermute | solution.py:362
  45.8 5.6 %collective-permute-start.18 = (bf16[128,512]{1,0:T(8,128)(2,1)S(1)}, bf16[128,512]{1,0:T(8,128)(2,1)S(1)}, u32[]{:S(2)}, u32[]{:S(2)}) collective-permute-start(bf16[128,512]{1,0:T(8,128)(2,1)S(1)} %bitcast_dynamic-update-slice_fusion.tree_ref), channel_id=1, source_target_pairs={{0,1},{1,0},{2,3},{3,2},{4,5},{5,4},{6,7},{7,6},{8,9},{9,8},{10,11... | collective-permute-start | bytes 393224 | tf_op jit(solution)/shard_map/ppermute | solution.py:362
  46.3 11.3 %collective-permute-start.16 = (bf16[528,128]{1,0:T(8,128)(2,1)S(1)}, bf16[528,128]{1,0:T(8,128)(2,1)S(1)}, u32[]{:S(2)}, u32[]{:S(2)}) collective-permute-start(bf16[528,128]{1,0:T(8,128)(2,1)S(1)} %collective-permute-done.15.refs_3_), channel_id=1, source_target_pairs={{0,32},{32,64},{64,96},{96,128},{128,160},{160,192},{192,224},{224... | collective-permute-start | bytes 405512 | tf_op jit(solution)/shard_map/ppermute | solution.py:362
  47.7 10.2 %collective-permute-start.2 = (bf16[528,128]{1,0:T(8,128)(2,1)S(1)}, bf16[528,128]{1,0:T(8,128)(2,1)S(1)}, u32[]{:S(2)}, u32[]{:S(2)}) collective-permute-start(bf16[528,128]{1,0:T(8,128)(2,1)S(1)} %collective-permute-done.1.refs_4_), channel_id=1, source_target_pairs={{0,224},{32,0},{64,32},{96,64},{128,96},{160,128},{192,160},{224,1... | collective-permute-start | bytes 405512 | tf_op jit(solution)/shard_map/ppermute | solution.py:362
  57.6 19.7 %collective-permute-start.17 = (bf16[528,128]{1,0:T(8,128)(2,1)S(1)}, bf16[528,128]{1,0:T(8,128)(2,1)S(1)}, u32[]{:S(2)}, u32[]{:S(2)}) collective-permute-start(bf16[528,128]{1,0:T(8,128)(2,1)S(1)} %collective-permute-done.16.refs_3_), channel_id=1, source_target_pairs={{0,32},{32,64},{64,96},{96,128},{128,160},{160,192},{192,224},{224... | collective-permute-start | bytes 405512 | tf_op jit(solution)/shard_map/ppermute | solution.py:362
  57.9 25.8 %collective-permute-start.3 = (bf16[528,128]{1,0:T(8,128)(2,1)S(1)}, bf16[528,128]{1,0:T(8,128)(2,1)S(1)}, u32[]{:S(2)}, u32[]{:S(2)}) collective-permute-start(bf16[528,128]{1,0:T(8,128)(2,1)S(1)} %collective-permute-done.2.refs_4_), channel_id=1, source_target_pairs={{0,224},{32,0},{64,32},{96,64},{128,96},{160,128},{192,160},{224,1... | collective-permute-start | bytes 405512 | tf_op jit(solution)/shard_map/ppermute | solution.py:362
  61.0 22.7 %collective-permute-start.10 = (bf16[1056,128]{1,0:T(8,128)(2,1)S(1)}, bf16[1056,128]{1,0:T(8,128)(2,1)S(1)}, u32[]{:S(2)}, u32[]{:S(2)}) collective-permute-start(bf16[1056,128]{1,0:T(8,128)(2,1)S(1)} %slice.8), channel_id=1, source_target_pairs={{0,32},{32,64},{64,96},{96,128},{128,160},{160,192},{192,224},{224... | collective-permute-start | bytes 811016 | tf_op jit(solution)/shard_map/ppermute | solution.py:362
  67.5 16.3 %collective-permute-start.14 = (bf16[528,128]{1,0:T(8,128)(2,1)S(1)}, bf16[528,128]{1,0:T(8,128)(2,1)S(1)}, u32[]{:S(2)}, u32[]{:S(2)}) collective-permute-start(bf16[528,128]{1,0:T(8,128)(2,1)S(1)} %slice.9), channel_id=1, source_target_pairs={{0,224},{32,0},{64,32},{96,64},{128,96},{160,128},{192,160},{224,1... | collective-permute-start | bytes 405512 | tf_op jit(solution)/shard_map/ppermute | solution.py:362

commit v2 on v1

--- a/solution.py
+++ b/solution.py
@@ -22,7 +22,7 @@
 DEEP = WIDTH + EXTRA
 QH = HALF * GROUPS
 SLOTS = 4
-PART = 256
+PART = 512
 COEF = WIDTH**-0.5 * LOG_TWO_E
 BF = jnp.bfloat16
 F32 = jnp.float32
@@ -93,9 +93,9 @@
 
 
 def weights_of(s, old):
-    top = jnp.ceil(jnp.max(s, axis=0, keepdims=True))
+    top = jnp.ceil(jnp.max(s, axis=0, keepdims=True) * COEF)
     new = top if old is None else jnp.maximum(old, top)
-    return new, jnp.exp2(s - new).astype(BF)
+    return new, jnp.exp2(s * COEF - new).astype(BF)
 
 
 def verify_update(s, v_t, m_ref, l_ref, acc_ref, start=False):
@@ -183,13 +183,13 @@
         token = iota((HALF, PART), 1) // GROUPS + t * PART // GROUPS
         open_ = iota((HALF, PART), 0) <= token
         q = q_ref[pl.ds(pl.multiple_of(hi * GROUPS + t * PART, PART), PART), :]
-        s = dot_t(k_both, q) * COEF
+        s = dot_t(k_both, q)
         s = jnp.concatenate([s[:HALF], jnp.where(open_, s[HALF:], NEG)], axis=0)
         new, p = weights_of(s, None)
         acc_ref[1, :, cols] = dot(v_both, p)
         m_ref[1, :, cols] = jnp.broadcast_to(new, (8, PART))
         q = q_ref[pl.ds(pl.multiple_of(lo * GROUPS + t * PART, PART), PART), :]
-        new, p = weights_of(jnp.where(open_, dot_t(k_lo, q) * COEF, NEG), None)
+        new, p = weights_of(jnp.where(open_, dot_t(k_lo, q), NEG), None)
         acc_ref[0, :, cols] = dot(v_lo, p)
         m_ref[0, :, cols] = jnp.broadcast_to(new, (8, PART))
 
@@ -219,30 +219,36 @@
     verify_update(dot_t(dq, kc_ref[...]) * COEF, joined(vc_ref, 0, 2), mv_ref, lv_ref, av_ref)
 
 
-def flash_chunks(q_ref, q_at, half, k_ref, v_ref, base, chunks, m_ref, acc_ref):
-    span = SLOTS * HALF
-
-    def chunk(i, _):
-        slot = base + i * SLOTS
+def flash_chunks(q_ref, q_at, half, k_ref, v_ref, base, count, m_ref, acc_ref, s_ref):
+    def chunk(slot, slots):
+        span = slots * HALF
         k = k_ref[pl.ds(pl.multiple_of(slot * HALF, HALF), span), :]
-        v = joined(v_ref, slot, SLOTS)
-
-        def scores(t):
+        v = joined(v_ref, slot, slots)
+        tiles = range(QH // PART)
+        tops = []
+        for t in tiles:
             q = q_ref[pl.ds(pl.multiple_of(q_at + t * PART, PART), PART), :]
-            return dot_t(k, q) * COEF
-
-        s = scores(0)
-        for t in range(QH // PART):
-            ahead = scores(t + 1) if t + 1 < QH // PART else None
+            s = dot_t(k, q)
+            s_ref[t, :span] = s
+            tops.append(jnp.ceil(jnp.max(s, axis=0, keepdims=True) * COEF))
+        for t in tiles:
             cols = slice(t * PART, (t + 1) * PART)
             old = m_ref[half, 0:1, cols]
-            new, p = weights_of(s, old)
+            new = jnp.maximum(old, tops[t])
+            p = jnp.exp2(s_ref[t, :span] * COEF - new).astype(BF)
             acc_ref[half, :, cols] = acc_ref[half, :, cols] * jnp.exp2(old - new) + dot(v, p)
             m_ref[half, :, cols] = jnp.broadcast_to(new, (8, PART))
-            s = ahead
+
+    def full(i, _):
+        chunk(base + i * SLOTS, SLOTS)
         return 0
 
-    lax.fori_loop(0, chunks, chunk, 0)
+    many = (count + 1) // SLOTS
+    lax.fori_loop(0, many, full, 0)
+
+    @pl.when(count > many * SLOTS)
+    def _():
+        chunk(base + many * SLOTS, SLOTS // 2)
 
 
 def step_kernel(layout, last, *refs):
@@ -252,7 +258,7 @@
     state = refs[3 + n_in + len(STATE) : 3 + n_in + 2 * len(STATE)]
     if last:
         out_ref, ver_ref, ok_ref, ov_ref = refs[3 + n_in + 2 * len(STATE) :][:4]
-    kk_ref, vv_ref, kc_ref, vc_ref, b_ref = refs[-5:]
+    kk_ref, vv_ref, kc_ref, vc_ref, b_ref, s_ref = refs[-6:]
     m_ref, acc_ref, mv_ref, lv_ref, av_ref, ck_ref, cv_ref = state
     me, z, x = me_index(), lax.axis_index("z"), lax.axis_index("x")
     first = first_of(own_ref, 0)
@@ -280,7 +286,7 @@
         vv_ref[to, WIDTH:, :] = ones
         n_hi, n_lo = n_hi + later, n_lo + 1 - later
     for start, count in ((0, n + n_hi), (lo_base, n_lo)):
-        for j in range(SLOTS - 1):
+        for j in range(1):
             at = pl.ds(pl.multiple_of((start + count + j) * HALF, HALF), HALF)
             kk_ref[at, :] = kk_ref[start * HALF : (start + 1) * HALF, :]
             vv_ref[start + count + j] = jnp.zeros((DEEP, HALF), BF)
@@ -288,8 +294,7 @@
     q_hi = QH - swap * QH
     ways = ((q_hi, 1, 0, n + n_hi), (q_lo, 0, lo_base, n_lo))
     for q_at, half, base, count in ways:
-        chunks = (count + SLOTS - 1) // SLOTS
-        flash_chunks(q_ref, q_at, half, kk_ref, vv_ref, base, chunks, m_ref, acc_ref)
+        flash_chunks(q_ref, q_at, half, kk_ref, vv_ref, base, count, m_ref, acc_ref, s_ref)
 
     for i, (ref, base, (dz, dx)) in enumerate(blocks):
         col = ((z + dz + 8) % 8) * 4 + (x + dx + 4) % 4
@@ -350,6 +355,7 @@
             pltpu.VMEM((n * TOK, WIDTH), BF),
             pltpu.VMEM((2 * n, HALF, WIDTH), BF),
             pltpu.VMEM((n * PAGES, WIDTH), F32),
+            pltpu.VMEM((QH // PART, SLOTS * HALF, PART), F32),
         ],
         input_output_aliases=alias,
         cost_estimate=cost(n),
@@ -409,7 +415,7 @@
         compiler_params=GRANT,
         name="own",
     )
-    state = own_call(*(held(a) for a in (q, own, dq, tree, far)), parents.reshape(1, TOK))
+    state = own_call(*(held(a) for a in (q, own, dq, tree, far, parents.reshape(1, TOK))))
     dxs = (-1, 1, 2)
     state = step(q, own, dq, [near_x], [[(0, d) for d in dxs]], state)
     ra = la = own
@@ -422,12 +428,11 @@
             [[(-s, 0)], [(s, 0)], [(-s, d) for d in dxs], [(s, d) for d in dxs]],
             state,
         )
-    oa = shift(la, "z", -1)
     ob = shift(rb[: 2 * PAY], "z", 1)
-    oc = shift(lb[2 * PAY :], "z", -1)
+    oc = shift(jnp.concatenate([la, lb[2 * PAY :]], axis=0), "z", -1)
     out, ver, ck, cv = step(
-        q, own, dq, [oa, ob, oc],
-        [[(4, 0)], [(4, d) for d in dxs[:2]], [(4, dxs[2])]],
+        q, own, dq, [ob, oc],
+        [[(4, d) for d in dxs[:2]], [(4, 0), (4, dxs[2])]],
         state, last=True,
     )[len(STATE) :]
     return (

time: 88.7 us -> 82.6 us (0.931)
  Pallas kernels: 31.4 us -> 27.7 us
  starting transfers between devices: 34.6 us -> 31 us
  waiting for transfers between devices: 20.7 us -> 21.9 us
    pallas_call x5, Pallas kernels: 27 us -> 23.2 us  [step(): pl.pallas_call(functools.partial(step_kernel, layout, last), out_shape=ou...]
    ppermute x19 -> x18, starting transfers between devices: 34.6 us -> 31 us  [shift(): return lax.ppermute(b, axis, [(i, (i + d) % n) for i in range(n)])]
    ppermute x19 -> x18, waiting for transfers between devices: 20.7 us -> 21.9 us  [shift(): return lax.ppermute(b, axis, [(i, (i + d) % n) for i in range(n)])]
  transfers between devices with their start and end apart: 19 -> 18, of which waited for: 6 -> 8; matrix products, arithmetic and copies ran while one was open for 1% -> 1% of each run, Pallas kernels for 29% -> 27%
where the time goes in v2:
time: 82.6 us; the launch traced here: 82.5 us
  starting transfers between devices  31 us (38%)
  Pallas kernels  27.7 us (34%)
  waiting for transfers between devices  21.9 us (27%)
  local copies, waits for them, and re-layouts  0.95 us (1%)
    ppermute x18, starting transfers between devices, shift(): return lax.ppermute(b, axis, [(i, (i + d) % n) for i in range(n)])  31 us
    pallas_call x5, Pallas kernels, step(): pl.pallas_call(functools.partial(step_kernel, layout, last), out_shape=ou...  23.2 us
    ppermute x18, waiting for transfers between devices, shift(): return lax.ppermute(b, axis, [(i, (i + d) % n) for i in range(n)])  21.9 us
    pallas_call x1, Pallas kernels, work(): own_call(*(held(a) for a in (q, own, dq, tree, far, parents.reshape(1, TO...  3.35 us
  transfers between devices with their start and end apart: 18, of which 8 were waited for; matrix products, arithmetic and copies ran while one was open for 1% of the time, Pallas kernels for 27%

profile of v2, /device:TPU:8, one launch (start us, length us, event | category | flops | bytes accessed | tf_op | source)
XLA Modules:
  0.0 82.5 jit_solution(2898084461564870273)
XLA Ops:
  0.7 1.1 %pack.1.own_ref.refs_1_ = bf16[528,128]{1,0:T(8,128)(2,1)S(1)} custom-call(s32[256]{0:T(256)} %pos_hbm.1, s32[2,32]{1,0:T(2,128)} %bitcast.36, s32[1,32]{1,0:T(1,128)} %bitcast.37, bf16[256,128]{1,0:T(8,128)(2,1)} %bitcast.34, bf16[256,128]{1,0:T(8,128)(2,1)} %bitcast.35), custom_call_target="tpu_custom_call" | custom-call | tf_op jit(solution)/shard_map/pack/pallas_call | solution.py:377
  1.8 1.6 %collective-permute-start = (bf16[528,128]{1,0:T(8,128)(2,1)S(1)}, bf16[528,128]{1,0:T(8,128)(2,1)S(1)}, u32[]{:S(2)}, u32[]{:S(2)}) collective-permute-start(bf16[528,128]{1,0:T(8,128)(2,1)S(1)} %pack.1.own_ref.refs_1_), channel_id=1, source_target_pairs={{0,8},{8,16},{16,24},{24,0},{1,9},{9,17},{17,25},{25,1},{2,10},{10... | collective-permute-start | bytes 405512 | tf_op jit(solution)/shard_map/ppermute | solution.py:368
  3.4 1.7 %collective-permute-start.1 = (bf16[528,128]{1,0:T(8,128)(2,1)S(1)}, bf16[528,128]{1,0:T(8,128)(2,1)S(1)}, u32[]{:S(2)}, u32[]{:S(2)}) collective-permute-start(bf16[528,128]{1,0:T(8,128)(2,1)S(1)} %pack.1.own_ref.refs_1_), channel_id=1, source_target_pairs={{0,24},{8,0},{16,8},{24,16},{1,25},{9,1},{17,9},{25,17},{2,26},{10... | collective-permute-start | bytes 405512 | tf_op jit(solution)/shard_map/ppermute | solution.py:368
  5.1 1.8 %collective-permute-start.2 = (bf16[528,128]{1,0:T(8,128)(2,1)S(1)}, bf16[528,128]{1,0:T(8,128)(2,1)S(1)}, u32[]{:S(2)}, u32[]{:S(2)}) collective-permute-start(bf16[528,128]{1,0:T(8,128)(2,1)S(1)} %pack.1.own_ref.refs_1_), channel_id=1, source_target_pairs={{0,16},{8,24},{16,0},{24,8},{1,17},{9,25},{17,1},{25,9},{2,18},{10... | collective-permute-start | bytes 405512 | tf_op jit(solution)/shard_map/ppermute | solution.py:368
  7.0 1.5 %collective-permute-done = bf16[528,128]{1,0:T(8,128)(2,1)S(1)} collective-permute-done((bf16[528,128]{1,0:T(8,128)(2,1)S(1)}, bf16[528,128]{1,0:T(8,128)(2,1)S(1)}, u32[]{:S(2)}, u32[]{:S(2)}) %collective-permute-start) | collective-permute-done | bytes 135200 | tf_op jit(solution)/shard_map/ppermute | solution.py:368
  8.4 2.2 %collective-permute-done.1 = bf16[528,128]{1,0:T(8,128)(2,1)S(1)} collective-permute-done((bf16[528,128]{1,0:T(8,128)(2,1)S(1)}, bf16[528,128]{1,0:T(8,128)(2,1)S(1)}, u32[]{:S(2)}, u32[]{:S(2)}) %collective-permute-start.1) | collective-permute-done | bytes 135200 | tf_op jit(solution)/shard_map/ppermute | solution.py:368
  10.7 1.7 %collective-permute-done.2 = bf16[528,128]{1,0:T(8,128)(2,1)S(1)} collective-permute-done((bf16[528,128]{1,0:T(8,128)(2,1)S(1)}, bf16[528,128]{1,0:T(8,128)(2,1)S(1)}, u32[]{:S(2)}, u32[]{:S(2)}) %collective-permute-start.2) | collective-permute-done | bytes 135200 | tf_op jit(solution)/shard_map/ppermute | solution.py:368
  12.3 5.9 %collective-permute-start.10 = (bf16[1584,128]{1,0:T(8,128)(2,1)S(1)}, bf16[1584,128]{1,0:T(8,128)(2,1)S(1)}, u32[]{:S(2)}, u32[]{:S(2)}) collective-permute-start(bf16[1584,128]{1,0:T(8,128)(2,1)S(1)} %constant_dynamic-update-slice_fusion.refs_3_), channel_id=1, source_target_pairs={{0,224},{32,0},{64,32},{96,64},{128,96},{160,128},{192,160},{224,1... | collective-permute-start | bytes 1216520 | tf_op jit(solution)/shard_map/ppermute | solution.py:368
  18.3 0.0 collective-permute-start.3
  18.3 8.0 %collective-permute-done.10.refs_6_ = bf16[1584,128]{1,0:T(8,128)(2,1)S(1)} collective-permute-done((bf16[1584,128]{1,0:T(8,128)(2,1)S(1)}, bf16[1584,128]{1,0:T(8,128)(2,1)S(1)}, u32[]{:S(2)}, u32[]{:S(2)}) %collective-permute-start.10) | collective-permute-done | bytes 405536 | tf_op jit(solution)/shard_map/ppermute | solution.py:368
  26.3 3.7 %collective-permute-start.11 = (bf16[1584,128]{1,0:T(8,128)(2,1)S(1)}, bf16[1584,128]{1,0:T(8,128)(2,1)S(1)}, u32[]{:S(2)}, u32[]{:S(2)}) collective-permute-start(bf16[1584,128]{1,0:T(8,128)(2,1)S(1)} %collective-permute-done.10.refs_6_), channel_id=1, source_target_pairs={{0,224},{32,0},{64,32},{96,64},{128,96},{160,128},{192,160},{224,1... | collective-permute-start | bytes 1216520 | tf_op jit(solution)/shard_map/ppermute | solution.py:368
  30.0 0.0 collective-permute-start.14
  30.0 3.2 %collective-permute-start.7 = (bf16[528,128]{1,0:T(8,128)(2,1)S(1)}, bf16[528,128]{1,0:T(8,128)(2,1)S(1)}, u32[]{:S(2)}, u32[]{:S(2)}) collective-permute-start(bf16[528,128]{1,0:T(8,128)(2,1)S(1)} %pack.1.own_ref.refs_1_), channel_id=1, source_target_pairs={{0,224},{32,0},{64,32},{96,64},{128,96},{160,128},{192,160},{224,1... | collective-permute-start | bytes 405512 | tf_op jit(solution)/shard_map/ppermute | solution.py:368
  33.2 0.8 %bitcast_dynamic-update-slice_fusion.1 = bf16[128,512]{1,0:T(8,128)(2,1)S(1)} fusion(bf16[16,8,2,128]{3,2,1,0:T(2,128)(2,1)} %bitcast.32), kind=kLoop, calls=%fused_computation.2 | loop fusion | bytes 131072
  34.1 6.0 %collective-permute-done.7.refs_4_ = bf16[528,128]{1,0:T(8,128)(2,1)S(1)} collective-permute-done((bf16[528,128]{1,0:T(8,128)(2,1)S(1)}, bf16[528,128]{1,0:T(8,128)(2,1)S(1)}, u32[]{:S(2)}, u32[]{:S(2)}) %collective-permute-start.7) | collective-permute-done | bytes 135200 | tf_op jit(solution)/shard_map/ppermute | solution.py:368
  40.0 3.7 %collective-permute-start.8 = (bf16[528,128]{1,0:T(8,128)(2,1)S(1)}, bf16[528,128]{1,0:T(8,128)(2,1)S(1)}, u32[]{:S(2)}, u32[]{:S(2)}) collective-permute-start(bf16[528,128]{1,0:T(8,128)(2,1)S(1)} %collective-permute-done.7.refs_4_), channel_id=1, source_target_pairs={{0,224},{32,0},{64,32},{96,64},{128,96},{160,128},{192,160},{224,1... | collective-permute-start | bytes 405512 | tf_op jit(solution)/shard_map/ppermute | solution.py:368
  43.7 0.0 collective-permute-start.12
  43.8 0.5 collective-permute-start.17
  44.3 0.4 collective-permute-done.4.refs_5_
  44.7 1.6 %collective-permute-start.5 = (bf16[1584,128]{1,0:T(8,128)(2,1)S(1)}, bf16[1584,128]{1,0:T(8,128)(2,1)S(1)}, u32[]{:S(2)}, u32[]{:S(2)}) collective-permute-start(bf16[1584,128]{1,0:T(8,128)(2,1)S(1)} %collective-permute-done.4.refs_5_), channel_id=1, source_target_pairs={{0,32},{32,64},{64,96},{96,128},{128,160},{160,192},{192,224},{224... | collective-permute-start | bytes 1216520 | tf_op jit(solution)/shard_map/ppermute | solution.py:368
  46.3 0.1 collective-permute-start.15
  46.4 1.3 %collective-permute-done.8.refs_4_ = bf16[528,128]{1,0:T(8,128)(2,1)S(1)} collective-permute-done((bf16[528,128]{1,0:T(8,128)(2,1)S(1)}, bf16[528,128]{1,0:T(8,128)(2,1)S(1)}, u32[]{:S(2)}, u32[]{:S(2)}) %collective-permute-start.8) | collective-permute-done | bytes 135200 | tf_op jit(solution)/shard_map/ppermute | solution.py:368
  47.7 3.7 %collective-permute-start.9 = (bf16[528,128]{1,0:T(8,128)(2,1)S(1)}, bf16[528,128]{1,0:T(8,128)(2,1)S(1)}, u32[]{:S(2)}, u32[]{:S(2)}) collective-permute-start(bf16[528,128]{1,0:T(8,128)(2,1)S(1)} %collective-permute-done.8.refs_4_), channel_id=1, source_target_pairs={{0,224},{32,0},{64,32},{96,64},{128,96},{160,128},{192,160},{224,1... | collective-permute-start | bytes 405512 | tf_op jit(solution)/shard_map/ppermute | solution.py:368
  51.4 3.3 %own.1 = (f32[2,8,1024]{2,1,0:T(8,128)S(1)}, f32[2,144,1024]{2,1,0:T(8,128)S(1)}, f32[64,128]{1,0:T(8,128)S(1)}, f32[64,128]{1,0:T(8,128)S(1)}, f32[64,128]{1,0:...) custom-call(bf16[2048,128]{1,0:T(8,128)(2,1)S(1)} %bitcast.19, bf16[528,128]{1,0:T(8,128)(2,1)S(1)} %pack.1.own_ref.refs_1_, ...), custom_call_target="tpu_custom_call" | custom-call | flops 268435456 | bytes 270336 | tf_op jit(solution)/shard_map/own/pallas_call | solution.py:418
  54.7 2.4 %shard_map.129 = (f32[2,8,1024]{2,1,0:T(8,128)S(1)}, f32[2,144,1024]{2,1,0:T(8,128)S(1)}, f32[64,128]{1,0:T(8,128)S(1)}, f32[64,128]{1,0:T(8,128)S(1)}, f32[64,1...) custom-call(bf16[2048,128]{1,0:T(8,128)(2,1)S(1)} %bitcast.20, ...), custom_call_target="tpu_custom_call", output_to_operand_aliasing={{0}: (4, {}), {1}: (5, {}), {2}: (6, {}), {3}: (7, {}), {4}... | custom-call | flops 402653184 | bytes 405504 | tf_op jit(solution)/shard_map/pallas_call | solution.py:347
  57.2 1.0 %collective-permute-done.15.refs_3_ = bf16[528,128]{1,0:T(8,128)(2,1)S(1)} collective-permute-done((bf16[528,128]{1,0:T(8,128)(2,1)S(1)}, bf16[528,128]{1,0:T(8,128)(2,1)S(1)}, u32[]{:S(2)}, u32[]{:S(2)}) %collective-permute-start.15) | collective-permute-done | bytes 135200 | tf_op jit(solution)/shard_map/ppermute | solution.py:368
  58.2 3.3 %collective-permute-start.13 = (bf16[1056,128]{1,0:T(8,128)(2,1)S(1)}, bf16[1056,128]{1,0:T(8,128)(2,1)S(1)}, u32[]{:S(2)}, u32[]{:S(2)}) collective-permute-start(bf16[1056,128]{1,0:T(8,128)(2,1)S(1)} %pad_maximum_fusion), channel_id=1, source_target_pairs={{0,224},{32,0},{64,32},{96,64},{128,96},{160,128},{192,160},{224,1... | collective-permute-start | bytes 811016 | tf_op jit(solution)/shard_map/ppermute | solution.py:368
  61.6 0.1 collective-permute-start.6
  61.6 5.6 %shard_map.130 = (f32[2,8,1024]{2,1,0:T(8,128)S(1)}, f32[2,144,1024]{2,1,0:T(8,128)S(1)}, f32[64,128]{1,0:T(8,128)S(1)}, f32[64,128]{1,0:T(8,128)S(1)}, f32[64,1...) custom-call(bf16[2048,128]{1,0:T(8,128)(2,1)S(1)} %bitcast.21, ...), custom_call_target="tpu_custom_call", output_to_operand_aliasing={{0}: (7, {}), {1}: (8, {}), {2}: (9, {}), {3}: (10, {}), {4... | custom-call | flops 1073741824 | bytes 1081344 | tf_op jit(solution)/shard_map/pallas_call | solution.py:347
  67.3 5.6 %shard_map.131 = (f32[2,8,1024]{2,1,0:T(8,128)S(1)}, f32[2,144,1024]{2,1,0:T(8,128)S(1)}, f32[64,128]{1,0:T(8,128)S(1)}, f32[64,128]{1,0:T(8,128)S(1)}, f32[64,1...) custom-call(bf16[2048,128]{1,0:T(8,128)(2,1)S(1)} %bitcast.22, ...), custom_call_target="tpu_custom_call", output_to_operand_aliasing={{0}: (7, {}), {1}: (8, {}), {2}: (9, {}), {3}: (10, {}), {4... | custom-call | flops 1073741824 | bytes 1081344 | tf_op jit(solution)/shard_map/pallas_call | solution.py:347
  72.9 5.4 %shard_map.132 = (f32[2,8,1024]{2,1,0:T(8,128)S(1)}, f32[2,144,1024]{2,1,0:T(8,128)S(1)}, f32[64,128]{1,0:T(8,128)S(1)}, f32[64,128]{1,0:T(8,128)S(1)}, f32[64,1...) custom-call(bf16[2048,128]{1,0:T(8,128)(2,1)S(1)} %bitcast.23, ...), custom_call_target="tpu_custom_call", output_to_operand_aliasing={{0}: (7, {}), {1}: (8, {}), {2}: (9, {}), {3}: (10, {}), {4... | custom-call | flops 1073741824 | bytes 1081344 | tf_op jit(solution)/shard_map/pallas_call | solution.py:347
  78.3 4.2 %shard_map.133 = (f32[2,8,1024]{2,1,0:T(8,128)S(1)}, f32[2,144,1024]{2,1,0:T(8,128)S(1)}, f32[64,128]{1,0:T(8,128)S(1)}, f32[64,128]{1,0:T(8,128)S(1)}, f32[64,1...) custom-call(bf16[2048,128]{1,0:T(8,128)(2,1)S(1)} %bitcast.24, ...), custom_call_target="tpu_custom_call", output_to_operand_aliasing={{0}: (5, {}), {1}: (6, {}), {2}: (7, {}), {3}: (8, {}), {4}... | custom-call | flops 536870912 | bytes 540672 | tf_op jit(solution)/shard_map/pallas_call | solution.py:347
  (27 shorter events, 0.2 us)
Async XLA Ops:
  0.6 43.1 %copy-start.3 = (bf16[128,2,128]{2,1,0:T(2,128)(2,1)S(1)}, bf16[128,2,128]{2,1,0:T(2,128)(2,1)}, u32[]{:S(2)}) copy-start(bf16[128,2,128]{2,1,0:T(2,128)(2,1)} %param.18) | copy-start | bytes 196612
  0.6 50.7 %copy-start = (bf16[256,8,128]{2,1,0:T(8,128)(2,1)S(1)}, bf16[256,8,128]{2,1,0:T(8,128)(2,1)}, u32[]{:S(2)}) copy-start(bf16[256,8,128]{2,1,0:T(8,128)(2,1)} %param.10) | copy-start | bytes 1572868
  0.7 50.7 %copy-start.1 = (bf16[256,8,128]{2,1,0:T(8,128)(2,1)S(1)}, bf16[256,8,128]{2,1,0:T(8,128)(2,1)}, u32[]{:S(2)}) copy-start(bf16[256,8,128]{2,1,0:T(8,128)(2,1)} %param.16) | copy-start | bytes 1572868
  0.7 50.7 %copy-start.2 = (s32[256]{0:T(256)S(1)}, s32[256]{0:T(256)}, u32[]{:S(2)}) copy-start(s32[256]{0:T(256)} %param.19) | copy-start | bytes 3076
  1.8 6.6 %collective-permute-start = (bf16[528,128]{1,0:T(8,128)(2,1)S(1)}, bf16[528,128]{1,0:T(8,128)(2,1)S(1)}, u32[]{:S(2)}, u32[]{:S(2)}) collective-permute-start(bf16[528,128]{1,0:T(8,128)(2,1)S(1)} %pack.1.own_ref.refs_1_), channel_id=1, source_target_pairs={{0,8},{8,16},{16,24},{24,0},{1,9},{9,17},{17,25},{25,1},{2,10},{10... | collective-permute-start | bytes 405512 | tf_op jit(solution)/shard_map/ppermute | solution.py:368
  3.4 7.2 %collective-permute-start.1 = (bf16[528,128]{1,0:T(8,128)(2,1)S(1)}, bf16[528,128]{1,0:T(8,128)(2,1)S(1)}, u32[]{:S(2)}, u32[]{:S(2)}) collective-permute-start(bf16[528,128]{1,0:T(8,128)(2,1)S(1)} %pack.1.own_ref.refs_1_), channel_id=1, source_target_pairs={{0,24},{8,0},{16,8},{24,16},{1,25},{9,1},{17,9},{25,17},{2,26},{10... | collective-permute-start | bytes 405512 | tf_op jit(solution)/shard_map/ppermute | solution.py:368
  5.1 7.2 %collective-permute-start.2 = (bf16[528,128]{1,0:T(8,128)(2,1)S(1)}, bf16[528,128]{1,0:T(8,128)(2,1)S(1)}, u32[]{:S(2)}, u32[]{:S(2)}) collective-permute-start(bf16[528,128]{1,0:T(8,128)(2,1)S(1)} %pack.1.own_ref.refs_1_), channel_id=1, source_target_pairs={{0,16},{8,24},{16,0},{24,8},{1,17},{9,25},{17,1},{25,9},{2,18},{10... | collective-permute-start | bytes 405512 | tf_op jit(solution)/shard_map/ppermute | solution.py:368
  12.3 13.9 %collective-permute-start.10 = (bf16[1584,128]{1,0:T(8,128)(2,1)S(1)}, bf16[1584,128]{1,0:T(8,128)(2,1)S(1)}, u32[]{:S(2)}, u32[]{:S(2)}) collective-permute-start(bf16[1584,128]{1,0:T(8,128)(2,1)S(1)} %constant_dynamic-update-slice_fusion.refs_3_), channel_id=1, source_target_pairs={{0,224},{32,0},{64,32},{96,64},{128,96},{160,128},{192,160},{224,1... | collective-permute-start | bytes 1216520 | tf_op jit(solution)/shard_map/ppermute | solution.py:368
  18.3 14.9 %collective-permute-start.3 = (bf16[1584,128]{1,0:T(8,128)(2,1)S(1)}, bf16[1584,128]{1,0:T(8,128)(2,1)S(1)}, u32[]{:S(2)}, u32[]{:S(2)}) collective-permute-start(bf16[1584,128]{1,0:T(8,128)(2,1)S(1)} %constant_dynamic-update-slice_fusion.refs_3_), channel_id=1, source_target_pairs={{0,32},{32,64},{64,96},{96,128},{128,160},{160,192},{192,224},{224... | collective-permute-start | bytes 1216520 | tf_op jit(solution)/shard_map/ppermute | solution.py:368
  26.3 17.4 %collective-permute-start.11 = (bf16[1584,128]{1,0:T(8,128)(2,1)S(1)}, bf16[1584,128]{1,0:T(8,128)(2,1)S(1)}, u32[]{:S(2)}, u32[]{:S(2)}) collective-permute-start(bf16[1584,128]{1,0:T(8,128)(2,1)S(1)} %collective-permute-done.10.refs_6_), channel_id=1, source_target_pairs={{0,224},{32,0},{64,32},{96,64},{128,96},{160,128},{192,160},{224,1... | collective-permute-start | bytes 1216520 | tf_op jit(solution)/shard_map/ppermute | solution.py:368
  30.0 16.3 %collective-permute-start.14 = (bf16[528,128]{1,0:T(8,128)(2,1)S(1)}, bf16[528,128]{1,0:T(8,128)(2,1)S(1)}, u32[]{:S(2)}, u32[]{:S(2)}) collective-permute-start(bf16[528,128]{1,0:T(8,128)(2,1)S(1)} %pack.1.own_ref.refs_1_), channel_id=1, source_target_pairs={{0,32},{32,64},{64,96},{96,128},{128,160},{160,192},{192,224},{224... | collective-permute-start | bytes 405512 | tf_op jit(solution)/shard_map/ppermute | solution.py:368
  30.0 10.0 %collective-permute-start.7 = (bf16[528,128]{1,0:T(8,128)(2,1)S(1)}, bf16[528,128]{1,0:T(8,128)(2,1)S(1)}, u32[]{:S(2)}, u32[]{:S(2)}) collective-permute-start(bf16[528,128]{1,0:T(8,128)(2,1)S(1)} %pack.1.own_ref.refs_1_), channel_id=1, source_target_pairs={{0,224},{32,0},{64,32},{96,64},{128,96},{160,128},{192,160},{224,1... | collective-permute-start | bytes 405512 | tf_op jit(solution)/shard_map/ppermute | solution.py:368
  33.2 11.5 %collective-permute-start.4 = (bf16[1584,128]{1,0:T(8,128)(2,1)S(1)}, bf16[1584,128]{1,0:T(8,128)(2,1)S(1)}, u32[]{:S(2)}, u32[]{:S(2)}) collective-permute-start(bf16[1584,128]{1,0:T(8,128)(2,1)S(1)} %collective-permute-done.3.refs_5_), channel_id=1, source_target_pairs={{0,32},{32,64},{64,96},{96,128},{128,160},{160,192},{192,224},{224... | collective-permute-start | bytes 1216520 | tf_op jit(solution)/shard_map/ppermute | solution.py:368
  40.0 7.7 %collective-permute-start.8 = (bf16[528,128]{1,0:T(8,128)(2,1)S(1)}, bf16[528,128]{1,0:T(8,128)(2,1)S(1)}, u32[]{:S(2)}, u32[]{:S(2)}) collective-permute-start(bf16[528,128]{1,0:T(8,128)(2,1)S(1)} %collective-permute-done.7.refs_4_), channel_id=1, source_target_pairs={{0,224},{32,0},{64,32},{96,64},{128,96},{160,128},{192,160},{224,1... | collective-permute-start | bytes 405512 | tf_op jit(solution)/shard_map/ppermute | solution.py:368
  43.7 14.4 %collective-permute-start.12 = (bf16[1584,128]{1,0:T(8,128)(2,1)S(1)}, bf16[1584,128]{1,0:T(8,128)(2,1)S(1)}, u32[]{:S(2)}, u32[]{:S(2)}) collective-permute-start(bf16[1584,128]{1,0:T(8,128)(2,1)S(1)} %collective-permute-done.11.refs_6_), channel_id=1, source_target_pairs={{0,224},{32,0},{64,32},{96,64},{128,96},{160,128},{192,160},{224,1... | collective-permute-start | bytes 1216520 | tf_op jit(solution)/shard_map/ppermute | solution.py:368
  43.8 7.6 %collective-permute-start.17 = (bf16[128,512]{1,0:T(8,128)(2,1)S(1)}, bf16[128,512]{1,0:T(8,128)(2,1)S(1)}, u32[]{:S(2)}, u32[]{:S(2)}) collective-permute-start(bf16[128,512]{1,0:T(8,128)(2,1)S(1)} %bitcast_dynamic-update-slice_fusion.tree_ref), channel_id=1, source_target_pairs={{0,1},{1,0},{2,3},{3,2},{4,5},{5,4},{6,7},{7,6},{8,9},{9,8},{10,11... | collective-permute-start | bytes 393224 | tf_op jit(solution)/shard_map/ppermute | solution.py:368
  44.7 16.9 %collective-permute-start.5 = (bf16[1584,128]{1,0:T(8,128)(2,1)S(1)}, bf16[1584,128]{1,0:T(8,128)(2,1)S(1)}, u32[]{:S(2)}, u32[]{:S(2)}) collective-permute-start(bf16[1584,128]{1,0:T(8,128)(2,1)S(1)} %collective-permute-done.4.refs_5_), channel_id=1, source_target_pairs={{0,32},{32,64},{64,96},{96,128},{128,160},{160,192},{192,224},{224... | collective-permute-start | bytes 1216520 | tf_op jit(solution)/shard_map/ppermute | solution.py:368
  46.3 11.9 %collective-permute-start.15 = (bf16[528,128]{1,0:T(8,128)(2,1)S(1)}, bf16[528,128]{1,0:T(8,128)(2,1)S(1)}, u32[]{:S(2)}, u32[]{:S(2)}) collective-permute-start(bf16[528,128]{1,0:T(8,128)(2,1)S(1)} %collective-permute-done.14.refs_3_), channel_id=1, source_target_pairs={{0,32},{32,64},{64,96},{96,128},{128,160},{160,192},{192,224},{224... | collective-permute-start | bytes 405512 | tf_op jit(solution)/shard_map/ppermute | solution.py:368
  47.7 10.5 %collective-permute-start.9 = (bf16[528,128]{1,0:T(8,128)(2,1)S(1)}, bf16[528,128]{1,0:T(8,128)(2,1)S(1)}, u32[]{:S(2)}, u32[]{:S(2)}) collective-permute-start(bf16[528,128]{1,0:T(8,128)(2,1)S(1)} %collective-permute-done.8.refs_4_), channel_id=1, source_target_pairs={{0,224},{32,0},{64,32},{96,64},{128,96},{160,128},{192,160},{224,1... | collective-permute-start | bytes 405512 | tf_op jit(solution)/shard_map/ppermute | solution.py:368
  58.2 14.7 %collective-permute-start.16 = (bf16[528,128]{1,0:T(8,128)(2,1)S(1)}, bf16[528,128]{1,0:T(8,128)(2,1)S(1)}, u32[]{:S(2)}, u32[]{:S(2)}) collective-permute-start(bf16[528,128]{1,0:T(8,128)(2,1)S(1)} %collective-permute-done.15.refs_3_), channel_id=1, source_target_pairs={{0,32},{32,64},{64,96},{96,128},{128,160},{160,192},{192,224},{224... | collective-permute-start | bytes 405512 | tf_op jit(solution)/shard_map/ppermute | solution.py:368
  58.2 20.0 %collective-permute-start.13 = (bf16[1056,128]{1,0:T(8,128)(2,1)S(1)}, bf16[1056,128]{1,0:T(8,128)(2,1)S(1)}, u32[]{:S(2)}, u32[]{:S(2)}) collective-permute-start(bf16[1056,128]{1,0:T(8,128)(2,1)S(1)} %pad_maximum_fusion), channel_id=1, source_target_pairs={{0,224},{32,0},{64,32},{96,64},{128,96},{160,128},{192,160},{224,1... | collective-permute-start | bytes 811016 | tf_op jit(solution)/shard_map/ppermute | solution.py:368
  61.6 16.7 %collective-permute-start.6 = (bf16[1056,128]{1,0:T(8,128)(2,1)S(1)}, bf16[1056,128]{1,0:T(8,128)(2,1)S(1)}, u32[]{:S(2)}, u32[]{:S(2)}) collective-permute-start(bf16[1056,128]{1,0:T(8,128)(2,1)S(1)} %slice.8), channel_id=1, source_target_pairs={{0,32},{32,64},{64,96},{96,128},{128,160},{160,192},{192,224},{224... | collective-permute-start | bytes 811016 | tf_op jit(solution)/shard_map/ppermute | solution.py:368

commit v3 on v2

--- a/solution.py
+++ b/solution.py
@@ -292,9 +292,16 @@
             vv_ref[start + count + j] = jnp.zeros((DEEP, HALF), BF)
     q_lo = swap * QH
     q_hi = QH - swap * QH
-    ways = ((q_hi, 1, 0, n + n_hi), (q_lo, 0, lo_base, n_lo))
-    for q_at, half, base, count in ways:
-        flash_chunks(q_ref, q_at, half, kk_ref, vv_ref, base, count, m_ref, acc_ref, s_ref)
+
+    def way(w, _):
+        late = w == 0
+        q_at = jnp.where(late, q_hi, q_lo)
+        base = jnp.where(late, 0, lo_base)
+        count = jnp.where(late, n + n_hi, n_lo)
+        flash_chunks(q_ref, q_at, 1 - w, kk_ref, vv_ref, base, count, m_ref, acc_ref, s_ref)
+        return 0
+
+    lax.fori_loop(0, 2, way, 0)
 
     for i, (ref, base, (dz, dx)) in enumerate(blocks):
         col = ((z + dz + 8) % 8) * 4 + (x + dx + 4) % 4
@@ -401,6 +408,7 @@
     xs = [shift(own, "x", 1), shift(own, "x", -1), shift(own, "x", 2)]
     far = shift(tree, "side", 1)
     near_x = jnp.concatenate(xs, axis=0)
+    dxs = (-1, 1, 2)
     own_call = pl.pallas_call(
         own_kernel,
         out_shape=STATE,
@@ -416,23 +424,28 @@
         name="own",
     )
     state = own_call(*(held(a) for a in (q, own, dq, tree, far, parents.reshape(1, TOK))))
-    dxs = (-1, 1, 2)
-    state = step(q, own, dq, [near_x], [[(0, d) for d in dxs]], state)
-    ra = la = own
+    ra, la = shift(own, "z", 1), shift(own, "z", -1)
+    state = step(
+        q, own, dq, [near_x, ra, la],
+        [[(0, d) for d in dxs], [(-1, 0)], [(1, 0)]],
+        state,
+    )
     rb = lb = near_x
     for s in range(1, 4):
-        ra, la = shift(ra, "z", 1), shift(la, "z", -1)
         rb, lb = shift(rb, "z", 1), shift(lb, "z", -1)
-        state = step(
-            q, own, dq, [ra, la, rb, lb],
-            [[(-s, 0)], [(s, 0)], [(-s, d) for d in dxs], [(s, d) for d in dxs]],
-            state,
-        )
+        sources = [rb, lb]
+        layout = [[(-s, d) for d in dxs], [(s, d) for d in dxs]]
+        if s < 3:
+            ra, la = shift(ra, "z", 1), shift(la, "z", -1)
+            sources += [ra, la]
+            layout += [[(-s - 1, 0)], [(s + 1, 0)]]
+        state = step(q, own, dq, sources, layout, state)
     ob = shift(rb[: 2 * PAY], "z", 1)
-    oc = shift(jnp.concatenate([la, lb[2 * PAY :]], axis=0), "z", -1)
+    oa = shift(la, "z", -1)
+    oc = shift(lb[2 * PAY :], "z", -1)
     out, ver, ck, cv = step(
-        q, own, dq, [ob, oc],
-        [[(4, d) for d in dxs[:2]], [(4, 0), (4, dxs[2])]],
+        q, own, dq, [oa, ob, oc],
+        [[(4, 0)], [(4, d) for d in dxs[:2]], [(4, dxs[2])]],
         state, last=True,
     )[len(STATE) :]
     return (

time: 82.6 us -> 87.1 us (1.054)
  starting transfers between devices: 31 us -> 34.3 us
    ppermute x18 -> x19, starting transfers between devices: 31 us -> 34.3 us  [shift(): return lax.ppermute(b, axis, [(i, (i + d) % n) for i in range(n)])]
    ppermute x18 -> x19, waiting for transfers between devices: 21.9 us -> 22.3 us  [shift(): return lax.ppermute(b, axis, [(i, (i + d) % n) for i in range(n)])]
  transfers between devices with their start and end apart: 18 -> 19, of which waited for: 8 -> 7; matrix products, arithmetic and copies ran while one was open for 1% -> 1% of each run, Pallas kernels for 27% -> 27%
where the time goes in v3:
time: 87.1 us; the launch traced here: 86.9 us
  starting transfers between devices  34.3 us (39%)
  Pallas kernels  28.5 us (33%)
  waiting for transfers between devices  22.3 us (26%)
  local copies, waits for them, and re-layouts  0.95 us (1%)
    ppermute x19, starting transfers between devices, shift(): return lax.ppermute(b, axis, [(i, (i + d) % n) for i in range(n)])  34.3 us
    pallas_call x5, Pallas kernels, step(): pl.pallas_call(functools.partial(step_kernel, layout, last), out_shape=ou...  24.1 us
    ppermute x19, waiting for transfers between devices, shift(): return lax.ppermute(b, axis, [(i, (i + d) % n) for i in range(n)])  22.3 us
    pallas_call x1, Pallas kernels, work(): own_call(*(held(a) for a in (q, own, dq, tree, far, parents.reshape(1, TO...  3.35 us
  transfers between devices with their start and end apart: 19, of which 7 were waited for; matrix products, arithmetic and copies ran while one was open for 1% of the time, Pallas kernels for 27%

profile of v3, /device:TPU:8, one launch (start us, length us, event | category | flops | bytes accessed | tf_op | source)
XLA Modules:
  0.0 86.9 jit_solution(1087768727793848222)
XLA Ops:
  0.7 1.1 %pack.1.own_ref.refs_1_ = bf16[528,128]{1,0:T(8,128)(2,1)S(1)} custom-call(s32[256]{0:T(256)} %pos_hbm.1, s32[2,32]{1,0:T(2,128)} %bitcast.36, s32[1,32]{1,0:T(1,128)} %bitcast.37, bf16[256,128]{1,0:T(8,128)(2,1)} %bitcast.34, bf16[256,128]{1,0:T(8,128)(2,1)} %bitcast.35), custom_call_target="tpu_custom_call" | custom-call | tf_op jit(solution)/shard_map/pack/pallas_call | solution.py:384
  1.8 1.6 %collective-permute-start.4 = (bf16[528,128]{1,0:T(8,128)(2,1)S(1)}, bf16[528,128]{1,0:T(8,128)(2,1)S(1)}, u32[]{:S(2)}, u32[]{:S(2)}) collective-permute-start(bf16[528,128]{1,0:T(8,128)(2,1)S(1)} %pack.1.own_ref.refs_1_), channel_id=1, source_target_pairs={{0,8},{8,16},{16,24},{24,0},{1,9},{9,17},{17,25},{25,1},{2,10},{10... | collective-permute-start | bytes 405512 | tf_op jit(solution)/shard_map/ppermute | solution.py:375
  3.4 1.7 %collective-permute-start.5 = (bf16[528,128]{1,0:T(8,128)(2,1)S(1)}, bf16[528,128]{1,0:T(8,128)(2,1)S(1)}, u32[]{:S(2)}, u32[]{:S(2)}) collective-permute-start(bf16[528,128]{1,0:T(8,128)(2,1)S(1)} %pack.1.own_ref.refs_1_), channel_id=1, source_target_pairs={{0,24},{8,0},{16,8},{24,16},{1,25},{9,1},{17,9},{25,17},{2,26},{10... | collective-permute-start | bytes 405512 | tf_op jit(solution)/shard_map/ppermute | solution.py:375
  5.1 1.8 %collective-permute-start.6 = (bf16[528,128]{1,0:T(8,128)(2,1)S(1)}, bf16[528,128]{1,0:T(8,128)(2,1)S(1)}, u32[]{:S(2)}, u32[]{:S(2)}) collective-permute-start(bf16[528,128]{1,0:T(8,128)(2,1)S(1)} %pack.1.own_ref.refs_1_), channel_id=1, source_target_pairs={{0,16},{8,24},{16,0},{24,8},{1,17},{9,25},{17,1},{25,9},{2,18},{10... | collective-permute-start | bytes 405512 | tf_op jit(solution)/shard_map/ppermute | solution.py:375
  7.0 1.5 %collective-permute-done.4 = bf16[528,128]{1,0:T(8,128)(2,1)S(1)} collective-permute-done((bf16[528,128]{1,0:T(8,128)(2,1)S(1)}, bf16[528,128]{1,0:T(8,128)(2,1)S(1)}, u32[]{:S(2)}, u32[]{:S(2)}) %collective-permute-start.4) | collective-permute-done | bytes 135200 | tf_op jit(solution)/shard_map/ppermute | solution.py:375
  8.4 2.2 %collective-permute-done.5 = bf16[528,128]{1,0:T(8,128)(2,1)S(1)} collective-permute-done((bf16[528,128]{1,0:T(8,128)(2,1)S(1)}, bf16[528,128]{1,0:T(8,128)(2,1)S(1)}, u32[]{:S(2)}, u32[]{:S(2)}) %collective-permute-start.5) | collective-permute-done | bytes 135200 | tf_op jit(solution)/shard_map/ppermute | solution.py:375
  10.7 1.7 %collective-permute-done.6 = bf16[528,128]{1,0:T(8,128)(2,1)S(1)} collective-permute-done((bf16[528,128]{1,0:T(8,128)(2,1)S(1)}, bf16[528,128]{1,0:T(8,128)(2,1)S(1)}, u32[]{:S(2)}, u32[]{:S(2)}) %collective-permute-start.6) | collective-permute-done | bytes 135200 | tf_op jit(solution)/shard_map/ppermute | solution.py:375
  12.3 5.9 %collective-permute-start.11 = (bf16[1584,128]{1,0:T(8,128)(2,1)S(1)}, bf16[1584,128]{1,0:T(8,128)(2,1)S(1)}, u32[]{:S(2)}, u32[]{:S(2)}) collective-permute-start(bf16[1584,128]{1,0:T(8,128)(2,1)S(1)} %constant_dynamic-update-slice_fusion.refs_3_), channel_id=1, source_target_pairs={{0,224},{32,0},{64,32},{96,64},{128,96},{160,128},{192,160},{224,1... | collective-permute-start | bytes 1216520 | tf_op jit(solution)/shard_map/ppermute | solution.py:375
  18.3 0.0 collective-permute-start.7
  18.3 8.0 %collective-permute-done.11.refs_4_ = bf16[1584,128]{1,0:T(8,128)(2,1)S(1)} collective-permute-done((bf16[1584,128]{1,0:T(8,128)(2,1)S(1)}, bf16[1584,128]{1,0:T(8,128)(2,1)S(1)}, u32[]{:S(2)}, u32[]{:S(2)}) %collective-permute-start.11) | collective-permute-done | bytes 405536 | tf_op jit(solution)/shard_map/ppermute | solution.py:375
  26.3 3.7 %collective-permute-start.12 = (bf16[1584,128]{1,0:T(8,128)(2,1)S(1)}, bf16[1584,128]{1,0:T(8,128)(2,1)S(1)}, u32[]{:S(2)}, u32[]{:S(2)}) collective-permute-start(bf16[1584,128]{1,0:T(8,128)(2,1)S(1)} %collective-permute-done.11.refs_4_), channel_id=1, source_target_pairs={{0,224},{32,0},{64,32},{96,64},{128,96},{160,128},{192,160},{224,1... | collective-permute-start | bytes 1216520 | tf_op jit(solution)/shard_map/ppermute | solution.py:375
  30.0 3.2 %collective-permute-start = (bf16[528,128]{1,0:T(8,128)(2,1)S(1)}, bf16[528,128]{1,0:T(8,128)(2,1)S(1)}, u32[]{:S(2)}, u32[]{:S(2)}) collective-permute-start(bf16[528,128]{1,0:T(8,128)(2,1)S(1)} %pack.1.own_ref.refs_1_), channel_id=1, source_target_pairs={{0,224},{32,0},{64,32},{96,64},{128,96},{160,128},{192,160},{224,1... | collective-permute-start | bytes 405512 | tf_op jit(solution)/shard_map/ppermute | solution.py:375
  33.2 0.8 bitcast_dynamic-update-slice_fusion.1
  34.1 6.0 %collective-permute-done.refs_5_ = bf16[528,128]{1,0:T(8,128)(2,1)S(1)} collective-permute-done((bf16[528,128]{1,0:T(8,128)(2,1)S(1)}, bf16[528,128]{1,0:T(8,128)(2,1)S(1)}, u32[]{:S(2)}, u32[]{:S(2)}) %collective-permute-start) | collective-permute-done | bytes 135200 | tf_op jit(solution)/shard_map/ppermute | solution.py:375
  40.0 3.7 %collective-permute-start.1 = (bf16[528,128]{1,0:T(8,128)(2,1)S(1)}, bf16[528,128]{1,0:T(8,128)(2,1)S(1)}, u32[]{:S(2)}, u32[]{:S(2)}) collective-permute-start(bf16[528,128]{1,0:T(8,128)(2,1)S(1)} %collective-permute-done.refs_5_), channel_id=1, source_target_pairs={{0,224},{32,0},{64,32},{96,64},{128,96},{160,128},{192,160},{224,1... | collective-permute-start | bytes 405512 | tf_op jit(solution)/shard_map/ppermute | solution.py:375
  43.7 0.0 collective-permute-start.13
  43.7 2.0 %collective-permute-start.9 = (bf16[1584,128]{1,0:T(8,128)(2,1)S(1)}, bf16[1584,128]{1,0:T(8,128)(2,1)S(1)}, u32[]{:S(2)}, u32[]{:S(2)}) collective-permute-start(bf16[1584,128]{1,0:T(8,128)(2,1)S(1)} %collective-permute-done.8.refs_3_), channel_id=1, source_target_pairs={{0,32},{32,64},{64,96},{96,128},{128,160},{160,192},{192,224},{224... | collective-permute-start | bytes 1216520 | tf_op jit(solution)/shard_map/ppermute | solution.py:375
  45.8 0.5 collective-permute-start.18
  46.3 0.0 collective-permute-start.16
  46.3 1.4 %collective-permute-done.1.refs_6_ = bf16[528,128]{1,0:T(8,128)(2,1)S(1)} collective-permute-done((bf16[528,128]{1,0:T(8,128)(2,1)S(1)}, bf16[528,128]{1,0:T(8,128)(2,1)S(1)}, u32[]{:S(2)}, u32[]{:S(2)}) %collective-permute-start.1) | collective-permute-done | bytes 135200 | tf_op jit(solution)/shard_map/ppermute | solution.py:375
  47.7 3.7 %collective-permute-start.2 = (bf16[528,128]{1,0:T(8,128)(2,1)S(1)}, bf16[528,128]{1,0:T(8,128)(2,1)S(1)}, u32[]{:S(2)}, u32[]{:S(2)}) collective-permute-start(bf16[528,128]{1,0:T(8,128)(2,1)S(1)} %collective-permute-done.1.refs_6_), channel_id=1, source_target_pairs={{0,224},{32,0},{64,32},{96,64},{128,96},{160,128},{192,160},{224,1... | collective-permute-start | bytes 405512 | tf_op jit(solution)/shard_map/ppermute | solution.py:375
  51.4 3.3 %own.1 = (f32[2,8,1024]{2,1,0:T(8,128)S(1)}, f32[2,144,1024]{2,1,0:T(8,128)S(1)}, f32[64,128]{1,0:T(8,128)S(1)}, f32[64,128]{1,0:T(8,128)S(1)}, f32[64,128]{1,0:...) custom-call(bf16[2048,128]{1,0:T(8,128)(2,1)S(1)} %bitcast.19, bf16[528,128]{1,0:T(8,128)(2,1)S(1)} %pack.1.own_ref.refs_1_, ...), custom_call_target="tpu_custom_call" | custom-call | flops 268435456 | bytes 270336 | tf_op jit(solution)/shard_map/own/pallas_call | solution.py:426
  54.7 1.7 %collective-permute-done.16.refs_5_ = bf16[528,128]{1,0:T(8,128)(2,1)S(1)} collective-permute-done((bf16[528,128]{1,0:T(8,128)(2,1)S(1)}, bf16[528,128]{1,0:T(8,128)(2,1)S(1)}, u32[]{:S(2)}, u32[]{:S(2)}) %collective-permute-start.16) | collective-permute-done | bytes 135200 | tf_op jit(solution)/shard_map/ppermute | solution.py:375
  56.4 1.7 %collective-permute-start.17 = (bf16[528,128]{1,0:T(8,128)(2,1)S(1)}, bf16[528,128]{1,0:T(8,128)(2,1)S(1)}, u32[]{:S(2)}, u32[]{:S(2)}) collective-permute-start(bf16[528,128]{1,0:T(8,128)(2,1)S(1)} %collective-permute-done.16.refs_5_), channel_id=1, source_target_pairs={{0,32},{32,64},{64,96},{96,128},{128,160},{160,192},{192,224},{224... | collective-permute-start | bytes 405512 | tf_op jit(solution)/shard_map/ppermute | solution.py:375
  58.1 4.2 %shard_map.129 = (f32[2,8,1024]{2,1,0:T(8,128)S(1)}, f32[2,144,1024]{2,1,0:T(8,128)S(1)}, f32[64,128]{1,0:T(8,128)S(1)}, f32[64,128]{1,0:T(8,128)S(1)}, f32[64,1...) custom-call(bf16[2048,128]{1,0:T(8,128)(2,1)S(1)} %bitcast.20, ...), custom_call_target="tpu_custom_call", output_to_operand_aliasing={{0}: (6, {}), {1}: (7, {}), {2}: (8, {}), {3}: (9, {}), {4}... | custom-call | flops 671088640 | bytes 675840 | tf_op jit(solution)/shard_map/pallas_call | solution.py:354
  62.3 1.6 %collective-permute-start.3 = (bf16[528,128]{1,0:T(8,128)(2,1)S(1)}, bf16[528,128]{1,0:T(8,128)(2,1)S(1)}, u32[]{:S(2)}, u32[]{:S(2)}) collective-permute-start(bf16[528,128]{1,0:T(8,128)(2,1)S(1)} %collective-permute-done.2.refs_6_), channel_id=1, source_target_pairs={{0,224},{32,0},{64,32},{96,64},{128,96},{160,128},{192,160},{224,1... | collective-permute-start | bytes 405512 | tf_op jit(solution)/shard_map/ppermute | solution.py:375
  63.9 0.6 collective-permute-start.10
  64.5 5.7 %shard_map.130 = (f32[2,8,1024]{2,1,0:T(8,128)S(1)}, f32[2,144,1024]{2,1,0:T(8,128)S(1)}, f32[64,128]{1,0:T(8,128)S(1)}, f32[64,128]{1,0:T(8,128)S(1)}, f32[64,1...) custom-call(bf16[2048,128]{1,0:T(8,128)(2,1)S(1)} %bitcast.21, ...), custom_call_target="tpu_custom_call", output_to_operand_aliasing={{0}: (7, {}), {1}: (8, {}), {2}: (9, {}), {3}: (10, {}), {4... | custom-call | flops 1073741824 | bytes 1081344 | tf_op jit(solution)/shard_map/pallas_call | solution.py:354
  70.2 2.5 %collective-permute-start.14 = (bf16[528,128]{1,0:T(8,128)(2,1)S(1)}, bf16[528,128]{1,0:T(8,128)(2,1)S(1)}, u32[]{:S(2)}, u32[]{:S(2)}) collective-permute-start(bf16[528,128]{1,0:T(8,128)(2,1)S(1)} %slice.9), channel_id=1, source_target_pairs={{0,224},{32,0},{64,32},{96,64},{128,96},{160,128},{192,160},{224,1... | collective-permute-start | bytes 405512 | tf_op jit(solution)/shard_map/ppermute | solution.py:375
  72.7 5.7 %shard_map.131 = (f32[2,8,1024]{2,1,0:T(8,128)S(1)}, f32[2,144,1024]{2,1,0:T(8,128)S(1)}, f32[64,128]{1,0:T(8,128)S(1)}, f32[64,128]{1,0:T(8,128)S(1)}, f32[64,1...) custom-call(bf16[2048,128]{1,0:T(8,128)(2,1)S(1)} %bitcast.22, ...), custom_call_target="tpu_custom_call", output_to_operand_aliasing={{0}: (7, {}), {1}: (8, {}), {2}: (9, {}), {3}: (10, {}), {4... | custom-call | flops 1073741824 | bytes 1081344 | tf_op jit(solution)/shard_map/pallas_call | solution.py:354
  78.3 4.3 %shard_map.132 = (f32[2,8,1024]{2,1,0:T(8,128)S(1)}, f32[2,144,1024]{2,1,0:T(8,128)S(1)}, f32[64,128]{1,0:T(8,128)S(1)}, f32[64,128]{1,0:T(8,128)S(1)}, f32[64,1...) custom-call(bf16[2048,128]{1,0:T(8,128)(2,1)S(1)} %bitcast.23, ...), custom_call_target="tpu_custom_call", output_to_operand_aliasing={{0}: (5, {}), {1}: (6, {}), {2}: (7, {}), {3}: (8, {}), {4}... | custom-call | flops 805306368 | bytes 811008 | tf_op jit(solution)/shard_map/pallas_call | solution.py:354
  82.7 4.3 %shard_map.133 = (f32[2,8,1024]{2,1,0:T(8,128)S(1)}, f32[2,144,1024]{2,1,0:T(8,128)S(1)}, f32[64,128]{1,0:T(8,128)S(1)}, f32[64,128]{1,0:T(8,128)S(1)}, f32[64,1...) custom-call(bf16[2048,128]{1,0:T(8,128)(2,1)S(1)} %bitcast.24, ...), custom_call_target="tpu_custom_call", output_to_operand_aliasing={{0}: (6, {}), {1}: (7, {}), {2}: (8, {}), {3}: (9, {}), {4}... | custom-call | flops 536870912 | bytes 540672 | tf_op jit(solution)/shard_map/pallas_call | solution.py:354
  (28 shorter events, 0.1 us)
Async XLA Ops:
  0.6 45.1 %copy-start.3 = (bf16[128,2,128]{2,1,0:T(2,128)(2,1)S(1)}, bf16[128,2,128]{2,1,0:T(2,128)(2,1)}, u32[]{:S(2)}) copy-start(bf16[128,2,128]{2,1,0:T(2,128)(2,1)} %param.18) | copy-start | bytes 196612
  0.6 50.7 %copy-start = (bf16[256,8,128]{2,1,0:T(8,128)(2,1)S(1)}, bf16[256,8,128]{2,1,0:T(8,128)(2,1)}, u32[]{:S(2)}) copy-start(bf16[256,8,128]{2,1,0:T(8,128)(2,1)} %param.10) | copy-start | bytes 1572868
  0.7 50.7 %copy-start.1 = (bf16[256,8,128]{2,1,0:T(8,128)(2,1)S(1)}, bf16[256,8,128]{2,1,0:T(8,128)(2,1)}, u32[]{:S(2)}) copy-start(bf16[256,8,128]{2,1,0:T(8,128)(2,1)} %param.16) | copy-start | bytes 1572868
  0.7 50.7 %copy-start.2 = (s32[256]{0:T(256)S(1)}, s32[256]{0:T(256)}, u32[]{:S(2)}) copy-start(s32[256]{0:T(256)} %param.19) | copy-start | bytes 3076
  1.8 6.6 %collective-permute-start.4 = (bf16[528,128]{1,0:T(8,128)(2,1)S(1)}, bf16[528,128]{1,0:T(8,128)(2,1)S(1)}, u32[]{:S(2)}, u32[]{:S(2)}) collective-permute-start(bf16[528,128]{1,0:T(8,128)(2,1)S(1)} %pack.1.own_ref.refs_1_), channel_id=1, source_target_pairs={{0,8},{8,16},{16,24},{24,0},{1,9},{9,17},{17,25},{25,1},{2,10},{10... | collective-permute-start | bytes 405512 | tf_op jit(solution)/shard_map/ppermute | solution.py:375
  3.4 7.2 %collective-permute-start.5 = (bf16[528,128]{1,0:T(8,128)(2,1)S(1)}, bf16[528,128]{1,0:T(8,128)(2,1)S(1)}, u32[]{:S(2)}, u32[]{:S(2)}) collective-permute-start(bf16[528,128]{1,0:T(8,128)(2,1)S(1)} %pack.1.own_ref.refs_1_), channel_id=1, source_target_pairs={{0,24},{8,0},{16,8},{24,16},{1,25},{9,1},{17,9},{25,17},{2,26},{10... | collective-permute-start | bytes 405512 | tf_op jit(solution)/shard_map/ppermute | solution.py:375
  5.1 7.2 %collective-permute-start.6 = (bf16[528,128]{1,0:T(8,128)(2,1)S(1)}, bf16[528,128]{1,0:T(8,128)(2,1)S(1)}, u32[]{:S(2)}, u32[]{:S(2)}) collective-permute-start(bf16[528,128]{1,0:T(8,128)(2,1)S(1)} %pack.1.own_ref.refs_1_), channel_id=1, source_target_pairs={{0,16},{8,24},{16,0},{24,8},{1,17},{9,25},{17,1},{25,9},{2,18},{10... | collective-permute-start | bytes 405512 | tf_op jit(solution)/shard_map/ppermute | solution.py:375
  12.3 13.9 %collective-permute-start.11 = (bf16[1584,128]{1,0:T(8,128)(2,1)S(1)}, bf16[1584,128]{1,0:T(8,128)(2,1)S(1)}, u32[]{:S(2)}, u32[]{:S(2)}) collective-permute-start(bf16[1584,128]{1,0:T(8,128)(2,1)S(1)} %constant_dynamic-update-slice_fusion.refs_3_), channel_id=1, source_target_pairs={{0,224},{32,0},{64,32},{96,64},{128,96},{160,128},{192,160},{224,1... | collective-permute-start | bytes 1216520 | tf_op jit(solution)/shard_map/ppermute | solution.py:375
  18.3 11.7 %collective-permute-start.7 = (bf16[1584,128]{1,0:T(8,128)(2,1)S(1)}, bf16[1584,128]{1,0:T(8,128)(2,1)S(1)}, u32[]{:S(2)}, u32[]{:S(2)}) collective-permute-start(bf16[1584,128]{1,0:T(8,128)(2,1)S(1)} %constant_dynamic-update-slice_fusion.refs_3_), channel_id=1, source_target_pairs={{0,32},{32,64},{64,96},{96,128},{128,160},{160,192},{192,224},{224... | collective-permute-start | bytes 1216520 | tf_op jit(solution)/shard_map/ppermute | solution.py:375
  26.3 17.4 %collective-permute-start.12 = (bf16[1584,128]{1,0:T(8,128)(2,1)S(1)}, bf16[1584,128]{1,0:T(8,128)(2,1)S(1)}, u32[]{:S(2)}, u32[]{:S(2)}) collective-permute-start(bf16[1584,128]{1,0:T(8,128)(2,1)S(1)} %collective-permute-done.11.refs_4_), channel_id=1, source_target_pairs={{0,224},{32,0},{64,32},{96,64},{128,96},{160,128},{192,160},{224,1... | collective-permute-start | bytes 1216520 | tf_op jit(solution)/shard_map/ppermute | solution.py:375
  30.0 13.8 %collective-permute-start.8 = (bf16[1584,128]{1,0:T(8,128)(2,1)S(1)}, bf16[1584,128]{1,0:T(8,128)(2,1)S(1)}, u32[]{:S(2)}, u32[]{:S(2)}) collective-permute-start(bf16[1584,128]{1,0:T(8,128)(2,1)S(1)} %collective-permute-done.7.refs_3_), channel_id=1, source_target_pairs={{0,32},{32,64},{64,96},{96,128},{128,160},{160,192},{192,224},{224... | collective-permute-start | bytes 1216520 | tf_op jit(solution)/shard_map/ppermute | solution.py:375
  30.0 10.0 %collective-permute-start = (bf16[528,128]{1,0:T(8,128)(2,1)S(1)}, bf16[528,128]{1,0:T(8,128)(2,1)S(1)}, u32[]{:S(2)}, u32[]{:S(2)}) collective-permute-start(bf16[528,128]{1,0:T(8,128)(2,1)S(1)} %pack.1.own_ref.refs_1_), channel_id=1, source_target_pairs={{0,224},{32,0},{64,32},{96,64},{128,96},{160,128},{192,160},{224,1... | collective-permute-start | bytes 405512 | tf_op jit(solution)/shard_map/ppermute | solution.py:375
  33.2 13.1 %collective-permute-start.15 = (bf16[528,128]{1,0:T(8,128)(2,1)S(1)}, bf16[528,128]{1,0:T(8,128)(2,1)S(1)}, u32[]{:S(2)}, u32[]{:S(2)}) collective-permute-start(bf16[528,128]{1,0:T(8,128)(2,1)S(1)} %pack.1.own_ref.refs_1_), channel_id=1, source_target_pairs={{0,32},{32,64},{64,96},{96,128},{128,160},{160,192},{192,224},{224... | collective-permute-start | bytes 405512 | tf_op jit(solution)/shard_map/ppermute | solution.py:375
  40.0 7.7 %collective-permute-start.1 = (bf16[528,128]{1,0:T(8,128)(2,1)S(1)}, bf16[528,128]{1,0:T(8,128)(2,1)S(1)}, u32[]{:S(2)}, u32[]{:S(2)}) collective-permute-start(bf16[528,128]{1,0:T(8,128)(2,1)S(1)} %collective-permute-done.refs_5_), channel_id=1, source_target_pairs={{0,224},{32,0},{64,32},{96,64},{128,96},{160,128},{192,160},{224,1... | collective-permute-start | bytes 405512 | tf_op jit(solution)/shard_map/ppermute | solution.py:375
  43.7 26.5 %collective-permute-start.13 = (bf16[1584,128]{1,0:T(8,128)(2,1)S(1)}, bf16[1584,128]{1,0:T(8,128)(2,1)S(1)}, u32[]{:S(2)}, u32[]{:S(2)}) collective-permute-start(bf16[1584,128]{1,0:T(8,128)(2,1)S(1)} %collective-permute-done.12.refs_4_), channel_id=1, source_target_pairs={{0,224},{32,0},{64,32},{96,64},{128,96},{160,128},{192,160},{224,1... | collective-permute-start | bytes 1216520 | tf_op jit(solution)/shard_map/ppermute | solution.py:375
  43.7 20.2 %collective-permute-start.9 = (bf16[1584,128]{1,0:T(8,128)(2,1)S(1)}, bf16[1584,128]{1,0:T(8,128)(2,1)S(1)}, u32[]{:S(2)}, u32[]{:S(2)}) collective-permute-start(bf16[1584,128]{1,0:T(8,128)(2,1)S(1)} %collective-permute-done.8.refs_3_), channel_id=1, source_target_pairs={{0,32},{32,64},{64,96},{96,128},{128,160},{160,192},{192,224},{224... | collective-permute-start | bytes 1216520 | tf_op jit(solution)/shard_map/ppermute | solution.py:375
  45.8 5.6 %collective-permute-start.18 = (bf16[128,512]{1,0:T(8,128)(2,1)S(1)}, bf16[128,512]{1,0:T(8,128)(2,1)S(1)}, u32[]{:S(2)}, u32[]{:S(2)}) collective-permute-start(bf16[128,512]{1,0:T(8,128)(2,1)S(1)} %bitcast_dynamic-update-slice_fusion.tree_ref), channel_id=1, source_target_pairs={{0,1},{1,0},{2,3},{3,2},{4,5},{5,4},{6,7},{7,6},{8,9},{9,8},{10,11... | collective-permute-start | bytes 393224 | tf_op jit(solution)/shard_map/ppermute | solution.py:375
  46.3 10.1 %collective-permute-start.16 = (bf16[528,128]{1,0:T(8,128)(2,1)S(1)}, bf16[528,128]{1,0:T(8,128)(2,1)S(1)}, u32[]{:S(2)}, u32[]{:S(2)}) collective-permute-start(bf16[528,128]{1,0:T(8,128)(2,1)S(1)} %collective-permute-done.15.refs_4_), channel_id=1, source_target_pairs={{0,32},{32,64},{64,96},{96,128},{128,160},{160,192},{192,224},{224... | collective-permute-start | bytes 405512 | tf_op jit(solution)/shard_map/ppermute | solution.py:375
  47.7 14.6 %collective-permute-start.2 = (bf16[528,128]{1,0:T(8,128)(2,1)S(1)}, bf16[528,128]{1,0:T(8,128)(2,1)S(1)}, u32[]{:S(2)}, u32[]{:S(2)}) collective-permute-start(bf16[528,128]{1,0:T(8,128)(2,1)S(1)} %collective-permute-done.1.refs_6_), channel_id=1, source_target_pairs={{0,224},{32,0},{64,32},{96,64},{128,96},{160,128},{192,160},{224,1... | collective-permute-start | bytes 405512 | tf_op jit(solution)/shard_map/ppermute | solution.py:375
  56.4 16.3 %collective-permute-start.17 = (bf16[528,128]{1,0:T(8,128)(2,1)S(1)}, bf16[528,128]{1,0:T(8,128)(2,1)S(1)}, u32[]{:S(2)}, u32[]{:S(2)}) collective-permute-start(bf16[528,128]{1,0:T(8,128)(2,1)S(1)} %collective-permute-done.16.refs_5_), channel_id=1, source_target_pairs={{0,32},{32,64},{64,96},{96,128},{128,160},{160,192},{192,224},{224... | collective-permute-start | bytes 405512 | tf_op jit(solution)/shard_map/ppermute | solution.py:375
  62.3 20.3 %collective-permute-start.3 = (bf16[528,128]{1,0:T(8,128)(2,1)S(1)}, bf16[528,128]{1,0:T(8,128)(2,1)S(1)}, u32[]{:S(2)}, u32[]{:S(2)}) collective-permute-start(bf16[528,128]{1,0:T(8,128)(2,1)S(1)} %collective-permute-done.2.refs_6_), channel_id=1, source_target_pairs={{0,224},{32,0},{64,32},{96,64},{128,96},{160,128},{192,160},{224,1... | collective-permute-start | bytes 405512 | tf_op jit(solution)/shard_map/ppermute | solution.py:375
  63.9 18.7 %collective-permute-start.10 = (bf16[1056,128]{1,0:T(8,128)(2,1)S(1)}, bf16[1056,128]{1,0:T(8,128)(2,1)S(1)}, u32[]{:S(2)}, u32[]{:S(2)}) collective-permute-start(bf16[1056,128]{1,0:T(8,128)(2,1)S(1)} %slice.8), channel_id=1, source_target_pairs={{0,32},{32,64},{64,96},{96,128},{128,160},{160,192},{192,224},{224... | collective-permute-start | bytes 811016 | tf_op jit(solution)/shard_map/ppermute | solution.py:375
  70.2 12.4 %collective-permute-start.14 = (bf16[528,128]{1,0:T(8,128)(2,1)S(1)}, bf16[528,128]{1,0:T(8,128)(2,1)S(1)}, u32[]{:S(2)}, u32[]{:S(2)}) collective-permute-start(bf16[528,128]{1,0:T(8,128)(2,1)S(1)} %slice.9), channel_id=1, source_target_pairs={{0,224},{32,0},{64,32},{96,64},{128,96},{160,128},{192,160},{224,1... | collective-permute-start | bytes 405512 | tf_op jit(solution)/shard_map/ppermute | solution.py:375

commit v4 on v3

--- a/solution.py
+++ b/solution.py
@@ -159,13 +159,7 @@
     return jnp.concatenate([ref[first + i] for i in range(count)], axis=1)
 
 
-def own_kernel(
-    q_ref, own_ref, dq_ref, tree_ref, far_ref, par_ref,
-    m_ref, acc_ref, mv_ref, lv_ref, av_ref, ck_ref, cv_ref,
-    kc_ref, vc_ref, b_ref,
-):
-    me = me_index()
-    side = lax.axis_index("side")
+def own_kernel(q_ref, own_ref, m_ref, acc_ref):
     first = first_of(own_ref, 0)
     swap = (first >= PAGES).astype(jnp.int32)
     lo = pl.multiple_of(swap * HALF, HALF)
@@ -193,6 +187,11 @@
         acc_ref[0, :, cols] = dot(v_lo, p)
         m_ref[0, :, cols] = jnp.broadcast_to(new, (8, PART))
 
+
+def tree_kernel(own_ref, dq_ref, tree_ref, far_ref, par_ref, *refs):
+    mv_ref, lv_ref, av_ref, ck_ref, cv_ref, kc_ref, vc_ref, b_ref = refs[5:]
+    me = me_index()
+    side = lax.axis_index("side")
     link = (par_ref[...] == iota((TOK, TOK), 0)) | (iota((TOK, TOK), 0) == iota((TOK, TOK), 1))
     link = link.astype(F32).astype(BF)
     for _ in range(8):
@@ -214,7 +213,7 @@
     dq = dq_ref[pl.ds(pl.multiple_of(me * rows64, rows64), rows64), :]
     s = jnp.where(allowed, dot_t(dq, rows_of(0)) * COEF, NEG)
     v_t = jnp.transpose(rows_of(2 * WIDTH).astype(F32)).astype(BF)
-    verify_update(s, v_t, mv_ref, lv_ref, av_ref, start=True)
+    verify_update(s, v_t, mv_ref, lv_ref, av_ref)
     clipped_source(own_ref, 0, me, me, kc_ref, vc_ref, 0, ck_ref, cv_ref, b_ref)
     verify_update(dot_t(dq, kc_ref[...]) * COEF, joined(vc_ref, 0, 2), mv_ref, lv_ref, av_ref)
 
@@ -251,11 +250,13 @@
         chunk(base + many * SLOTS, SLOTS // 2)
 
 
-def step_kernel(layout, last, *refs):
+def step_kernel(layout, place, *refs):
     n_in = len(layout)
+    first_call, last = place == 0, place == 2
+    held_in = 2 if first_call else len(STATE)
     q_ref, own_ref, dq_ref = refs[:3]
     srcs = refs[3 : 3 + n_in]
-    state = refs[3 + n_in + len(STATE) : 3 + n_in + 2 * len(STATE)]
+    state = refs[3 + n_in + held_in : 3 + n_in + held_in + len(STATE)]
     if last:
         out_ref, ver_ref, ok_ref, ov_ref = refs[3 + n_in + 2 * len(STATE) :][:4]
     kk_ref, vv_ref, kc_ref, vc_ref, b_ref, s_ref = refs[-6:]
@@ -308,7 +309,8 @@
         clipped_source(ref, base, col, me, kc_ref, vc_ref, i, ck_ref, cv_ref, b_ref)
     rows64 = GROUPS * 8
     dq = dq_ref[pl.ds(pl.multiple_of(me * rows64, rows64), rows64), :]
-    verify_update(dot_t(dq, kc_ref[...]) * COEF, joined(vc_ref, 0, 2 * n), mv_ref, lv_ref, av_ref)
+    s = dot_t(dq, kc_ref[...]) * COEF
+    verify_update(s, joined(vc_ref, 0, 2 * n), mv_ref, lv_ref, av_ref, start=first_call)
     if last:
         for t in range(QH // PART):
             cols = slice(t * PART, (t + 1) * PART)
@@ -339,11 +341,11 @@
     )
 
 
-def step(q, own, dq, sources, layout, state, last=False):
+def step(q, own, dq, sources, layout, state, place=1):
     n = sum(len(d) for d in layout)
     outs = STATE
-    alias = {3 + len(layout) + i: i for i in range(len(STATE))}
-    if last:
+    alias = {3 + len(layout) + i: i for i in range(len(state))}
+    if place == 2:
         outs = STATE + [
             jax.ShapeDtypeStruct((2 * QH, WIDTH), BF),
             jax.ShapeDtypeStruct((64, WIDTH), BF),
@@ -352,9 +354,9 @@
         ]
     slots = 3 * n + 2 * SLOTS
     return pl.pallas_call(
-        functools.partial(step_kernel, layout, last),
+        functools.partial(step_kernel, layout, place),
         out_shape=outs,
-        in_specs=vmem(3 + len(layout) + len(STATE)),
+        in_specs=vmem(3 + len(layout) + len(state)),
         out_specs=vmem(len(outs)),
         scratch_shapes=[
             pltpu.VMEM((slots * HALF, WIDTH), BF),
@@ -411,24 +413,34 @@
     dxs = (-1, 1, 2)
     own_call = pl.pallas_call(
         own_kernel,
-        out_shape=STATE,
-        in_specs=vmem(6),
-        out_specs=vmem(len(STATE)),
+        out_shape=STATE[:2],
+        in_specs=vmem(2),
+        out_specs=vmem(2),
+        cost_estimate=cost(2),
+        compiler_params=GRANT,
+        name="own",
+    )
+    state = own_call(held(q), held(own))
+    tree_call = pl.pallas_call(
+        tree_kernel,
+        out_shape=STATE[2:],
+        in_specs=vmem(10),
+        out_specs=vmem(5),
         scratch_shapes=[
             pltpu.VMEM((TOK, WIDTH), BF),
             pltpu.VMEM((2, HALF, WIDTH), BF),
             pltpu.VMEM((PAGES, WIDTH), F32),
         ],
+        input_output_aliases={5 + i: i for i in range(5)},
         cost_estimate=cost(2),
         compiler_params=GRANT,
-        name="own",
-    )
-    state = own_call(*(held(a) for a in (q, own, dq, tree, far, parents.reshape(1, TOK))))
+        name="tree",
+    )
     ra, la = shift(own, "z", 1), shift(own, "z", -1)
     state = step(
         q, own, dq, [near_x, ra, la],
         [[(0, d) for d in dxs], [(-1, 0)], [(1, 0)]],
-        state,
+        state, place=0,
     )
     rb = lb = near_x
     for s in range(1, 4):
@@ -440,13 +452,18 @@
             sources += [ra, la]
             layout += [[(-s - 1, 0)], [(s + 1, 0)]]
         state = step(q, own, dq, sources, layout, state)
+        if s == 2:
+            ver = tree_call(
+                *(held(a) for a in (own, dq, tree, far, parents.reshape(1, TOK), *state[2:]))
+            )
+            state = [*state[:2], *ver]
     ob = shift(rb[: 2 * PAY], "z", 1)
     oa = shift(la, "z", -1)
     oc = shift(lb[2 * PAY :], "z", -1)
     out, ver, ck, cv = step(
         q, own, dq, [oa, ob, oc],
         [[(4, 0)], [(4, d) for d in dxs[:2]], [(4, dxs[2])]],
-        state, last=True,
+        state, place=2,
     )[len(STATE) :]
     return (
         out.reshape(TOK, GROUPS, WIDTH),

time: 87.1 us -> 89.4 us (1.026)
  waiting for transfers between devices: 22.3 us -> 28.1 us
  starting transfers between devices: 34.3 us -> 30.7 us
    ppermute x19, waiting for transfers between devices: 22.3 us -> 28.1 us  [shift(): return lax.ppermute(b, axis, [(i, (i + d) % n) for i in range(n)])]
    ppermute x19, starting transfers between devices: 34.3 us -> 30.7 us  [shift(): return lax.ppermute(b, axis, [(i, (i + d) % n) for i in range(n)])]
    pallas_call x6 -> x7, Pallas kernels: 27.4 us -> 27.5 us  [the longest x5 24 us: step(): pl.pallas_call(functools.partial(step_kernel, layout, place), out_shape=o...]
  transfers between devices with their start and end apart: 19 -> 19, of which waited for: 7 -> 7; matrix products, arithmetic and copies ran while one was open for 1% -> 1% of each run, Pallas kernels for 27% -> 26%
where the time goes in v4:
time: 89.4 us; the launch traced here: 89.2 us
  starting transfers between devices  30.7 us (34%)
  Pallas kernels  28.6 us (32%)
  waiting for transfers between devices  28.1 us (31%)
  local copies, waits for them, and re-layouts  0.95 us (1%)
    ppermute x19, starting transfers between devices, shift(): return lax.ppermute(b, axis, [(i, (i + d) % n) for i in range(n)])  30.7 us
    ppermute x19, waiting for transfers between devices, shift(): return lax.ppermute(b, axis, [(i, (i + d) % n) for i in range(n)])  28.1 us
    pallas_call x5, Pallas kernels, step(): pl.pallas_call(functools.partial(step_kernel, layout, place), out_shape=o...  24 us
    pallas_call x1, Pallas kernels, work(): tree_call(*(held(a) for a in (own, dq, tree, far, parents.reshape(1, TOK)...  2.1 us
  transfers between devices with their start and end apart: 19, of which 7 were waited for; matrix products, arithmetic and copies ran while one was open for 1% of the time, Pallas kernels for 26%

profile of v4, /device:TPU:8, one launch (start us, length us, event | category | flops | bytes accessed | tf_op | source)
XLA Modules:
  0.0 89.2 jit_solution(478566216222636492)
XLA Ops:
  0.7 1.1 %pack.1.own_ref.refs_1_ = bf16[528,128]{1,0:T(8,128)(2,1)S(1)} custom-call(s32[256]{0:T(256)} %pos_hbm.1, s32[2,32]{1,0:T(2,128)} %bitcast.36, s32[1,32]{1,0:T(1,128)} %bitcast.37, bf16[256,128]{1,0:T(8,128)(2,1)} %bitcast.34, bf16[256,128]{1,0:T(8,128)(2,1)} %bitcast.35), custom_call_target="tpu_custom_call" | custom-call | tf_op jit(solution)/shard_map/pack/pallas_call | solution.py:386
  1.8 1.6 %collective-permute-start.4 = (bf16[528,128]{1,0:T(8,128)(2,1)S(1)}, bf16[528,128]{1,0:T(8,128)(2,1)S(1)}, u32[]{:S(2)}, u32[]{:S(2)}) collective-permute-start(bf16[528,128]{1,0:T(8,128)(2,1)S(1)} %pack.1.own_ref.refs_1_), channel_id=1, source_target_pairs={{0,8},{8,16},{16,24},{24,0},{1,9},{9,17},{17,25},{25,1},{2,10},{10... | collective-permute-start | bytes 405512 | tf_op jit(solution)/shard_map/ppermute | solution.py:377
  3.4 1.7 %collective-permute-start.5 = (bf16[528,128]{1,0:T(8,128)(2,1)S(1)}, bf16[528,128]{1,0:T(8,128)(2,1)S(1)}, u32[]{:S(2)}, u32[]{:S(2)}) collective-permute-start(bf16[528,128]{1,0:T(8,128)(2,1)S(1)} %pack.1.own_ref.refs_1_), channel_id=1, source_target_pairs={{0,24},{8,0},{16,8},{24,16},{1,25},{9,1},{17,9},{25,17},{2,26},{10... | collective-permute-start | bytes 405512 | tf_op jit(solution)/shard_map/ppermute | solution.py:377
  5.1 1.8 %collective-permute-start.6 = (bf16[528,128]{1,0:T(8,128)(2,1)S(1)}, bf16[528,128]{1,0:T(8,128)(2,1)S(1)}, u32[]{:S(2)}, u32[]{:S(2)}) collective-permute-start(bf16[528,128]{1,0:T(8,128)(2,1)S(1)} %pack.1.own_ref.refs_1_), channel_id=1, source_target_pairs={{0,16},{8,24},{16,0},{24,8},{1,17},{9,25},{17,1},{25,9},{2,18},{10... | collective-permute-start | bytes 405512 | tf_op jit(solution)/shard_map/ppermute | solution.py:377
  6.9 1.5 %collective-permute-done.4 = bf16[528,128]{1,0:T(8,128)(2,1)S(1)} collective-permute-done((bf16[528,128]{1,0:T(8,128)(2,1)S(1)}, bf16[528,128]{1,0:T(8,128)(2,1)S(1)}, u32[]{:S(2)}, u32[]{:S(2)}) %collective-permute-start.4) | collective-permute-done | bytes 135200 | tf_op jit(solution)/shard_map/ppermute | solution.py:377
  8.4 2.2 %collective-permute-done.5 = bf16[528,128]{1,0:T(8,128)(2,1)S(1)} collective-permute-done((bf16[528,128]{1,0:T(8,128)(2,1)S(1)}, bf16[528,128]{1,0:T(8,128)(2,1)S(1)}, u32[]{:S(2)}, u32[]{:S(2)}) %collective-permute-start.5) | collective-permute-done | bytes 135200 | tf_op jit(solution)/shard_map/ppermute | solution.py:377
  10.6 1.7 %collective-permute-done.6 = bf16[528,128]{1,0:T(8,128)(2,1)S(1)} collective-permute-done((bf16[528,128]{1,0:T(8,128)(2,1)S(1)}, bf16[528,128]{1,0:T(8,128)(2,1)S(1)}, u32[]{:S(2)}, u32[]{:S(2)}) %collective-permute-start.6) | collective-permute-done | bytes 135200 | tf_op jit(solution)/shard_map/ppermute | solution.py:377
  12.3 2.0 %collective-permute-start.7 = (bf16[1584,128]{1,0:T(8,128)(2,1)S(1)}, bf16[1584,128]{1,0:T(8,128)(2,1)S(1)}, u32[]{:S(2)}, u32[]{:S(2)}) collective-permute-start(bf16[1584,128]{1,0:T(8,128)(2,1)S(1)} %constant_dynamic-update-slice_fusion.refs_3_), channel_id=1, source_target_pairs={{0,32},{32,64},{64,96},{96,128},{128,160},{160,192},{192,224},{224... | collective-permute-start | bytes 1216520 | tf_op jit(solution)/shard_map/ppermute | solution.py:377
  14.3 4.0 %collective-permute-start.11 = (bf16[1584,128]{1,0:T(8,128)(2,1)S(1)}, bf16[1584,128]{1,0:T(8,128)(2,1)S(1)}, u32[]{:S(2)}, u32[]{:S(2)}) collective-permute-start(bf16[1584,128]{1,0:T(8,128)(2,1)S(1)} %constant_dynamic-update-slice_fusion.refs_3_), channel_id=1, source_target_pairs={{0,224},{32,0},{64,32},{96,64},{128,96},{160,128},{192,160},{224,1... | collective-permute-start | bytes 1216520 | tf_op jit(solution)/shard_map/ppermute | solution.py:377
  18.4 8.7 %collective-permute-done.7.refs_3_ = bf16[1584,128]{1,0:T(8,128)(2,1)S(1)} collective-permute-done((bf16[1584,128]{1,0:T(8,128)(2,1)S(1)}, bf16[1584,128]{1,0:T(8,128)(2,1)S(1)}, u32[]{:S(2)}, u32[]{:S(2)}) %collective-permute-start.7) | collective-permute-done | bytes 405536 | tf_op jit(solution)/shard_map/ppermute | solution.py:377
  27.0 3.2 %collective-permute-start.12 = (bf16[1584,128]{1,0:T(8,128)(2,1)S(1)}, bf16[1584,128]{1,0:T(8,128)(2,1)S(1)}, u32[]{:S(2)}, u32[]{:S(2)}) collective-permute-start(bf16[1584,128]{1,0:T(8,128)(2,1)S(1)} %collective-permute-done.11.refs_4_), channel_id=1, source_target_pairs={{0,224},{32,0},{64,32},{96,64},{128,96},{160,128},{192,160},{224,1... | collective-permute-start | bytes 1216520 | tf_op jit(solution)/shard_map/ppermute | solution.py:377
  30.3 0.5 collective-permute-start
  30.8 1.5 %collective-permute-start.15 = (bf16[528,128]{1,0:T(8,128)(2,1)S(1)}, bf16[528,128]{1,0:T(8,128)(2,1)S(1)}, u32[]{:S(2)}, u32[]{:S(2)}) collective-permute-start(bf16[528,128]{1,0:T(8,128)(2,1)S(1)} %pack.1.own_ref.refs_1_), channel_id=1, source_target_pairs={{0,32},{32,64},{64,96},{96,128},{128,160},{160,192},{192,224},{224... | collective-permute-start | bytes 405512 | tf_op jit(solution)/shard_map/ppermute | solution.py:377
  32.3 8.0 %collective-permute-done.refs_5_ = bf16[528,128]{1,0:T(8,128)(2,1)S(1)} collective-permute-done((bf16[528,128]{1,0:T(8,128)(2,1)S(1)}, bf16[528,128]{1,0:T(8,128)(2,1)S(1)}, u32[]{:S(2)}, u32[]{:S(2)}) %collective-permute-start) | collective-permute-done | bytes 135200 | tf_op jit(solution)/shard_map/ppermute | solution.py:377
  40.3 3.7 %collective-permute-start.1 = (bf16[528,128]{1,0:T(8,128)(2,1)S(1)}, bf16[528,128]{1,0:T(8,128)(2,1)S(1)}, u32[]{:S(2)}, u32[]{:S(2)}) collective-permute-start(bf16[528,128]{1,0:T(8,128)(2,1)S(1)} %collective-permute-done.refs_5_), channel_id=1, source_target_pairs={{0,224},{32,0},{64,32},{96,64},{128,96},{160,128},{192,160},{224,1... | collective-permute-start | bytes 405512 | tf_op jit(solution)/shard_map/ppermute | solution.py:377
  44.0 0.8 bitcast_dynamic-update-slice_fusion.1
  44.9 0.1 collective-permute-start.16
  45.0 1.6 %collective-permute-done.1.refs_6_ = bf16[528,128]{1,0:T(8,128)(2,1)S(1)} collective-permute-done((bf16[528,128]{1,0:T(8,128)(2,1)S(1)}, bf16[528,128]{1,0:T(8,128)(2,1)S(1)}, u32[]{:S(2)}, u32[]{:S(2)}) %collective-permute-start.1) | collective-permute-done | bytes 135200 | tf_op jit(solution)/shard_map/ppermute | solution.py:377
  46.6 3.7 %collective-permute-start.2 = (bf16[528,128]{1,0:T(8,128)(2,1)S(1)}, bf16[528,128]{1,0:T(8,128)(2,1)S(1)}, u32[]{:S(2)}, u32[]{:S(2)}) collective-permute-start(bf16[528,128]{1,0:T(8,128)(2,1)S(1)} %collective-permute-done.1.refs_6_), channel_id=1, source_target_pairs={{0,224},{32,0},{64,32},{96,64},{128,96},{160,128},{192,160},{224,1... | collective-permute-start | bytes 405512 | tf_op jit(solution)/shard_map/ppermute | solution.py:377
  50.3 0.5 collective-permute-start.18
  50.8 1.4 %own.1 = (f32[2,8,1024]{2,1,0:T(8,128)S(1)}, f32[2,144,1024]{2,1,0:T(8,128)S(1)}) custom-call(bf16[2048,128]{1,0:T(8,128)(2,1)S(1)} %bitcast.25, bf16[528,128]{1,0:T(8,128)(2,1)S(1)} %pack.1.own_ref.refs_1_), custom_call_target="tpu_custom_call" | custom-call | flops 268435456 | bytes 270336 | tf_op jit(solution)/shard_map/own/pallas_call | solution.py:423
  52.2 4.4 %collective-permute-done.16.refs_5_ = bf16[528,128]{1,0:T(8,128)(2,1)S(1)} collective-permute-done((bf16[528,128]{1,0:T(8,128)(2,1)S(1)}, bf16[528,128]{1,0:T(8,128)(2,1)S(1)}, u32[]{:S(2)}, u32[]{:S(2)}) %collective-permute-start.16) | collective-permute-done | bytes 135200 | tf_op jit(solution)/shard_map/ppermute | solution.py:377
  56.6 4.2 %shard_map.129 = (f32[2,8,1024]{2,1,0:T(8,128)S(1)}, f32[2,144,1024]{2,1,0:T(8,128)S(1)}, f32[64,128]{1,0:T(8,128)S(1)}, f32[64,128]{1,0:T(8,128)S(1)}, f32[64,1...) custom-call(bf16[2048,128]{1,0:T(8,128)(2,1)S(1)} %bitcast.26, ...), custom_call_target="tpu_custom_call", output_to_operand_aliasing={{0}: (6, {}), {1}: (7, {})} | custom-call | flops 671088640 | bytes 675840 | tf_op jit(solution)/shard_map/pallas_call | solution.py:356
  60.8 0.0 collective-permute-done.2.refs_6_
  60.8 3.3 %collective-permute-start.3 = (bf16[528,128]{1,0:T(8,128)(2,1)S(1)}, bf16[528,128]{1,0:T(8,128)(2,1)S(1)}, u32[]{:S(2)}, u32[]{:S(2)}) collective-permute-start(bf16[528,128]{1,0:T(8,128)(2,1)S(1)} %collective-permute-done.2.refs_6_), channel_id=1, source_target_pairs={{0,224},{32,0},{64,32},{96,64},{128,96},{160,128},{192,160},{224,1... | collective-permute-start | bytes 405512 | tf_op jit(solution)/shard_map/ppermute | solution.py:377
  64.1 0.1 collective-permute-start.10
  64.2 5.7 %shard_map.130 = (f32[2,8,1024]{2,1,0:T(8,128)S(1)}, f32[2,144,1024]{2,1,0:T(8,128)S(1)}, f32[64,128]{1,0:T(8,128)S(1)}, f32[64,128]{1,0:T(8,128)S(1)}, f32[64,1...) custom-call(bf16[2048,128]{1,0:T(8,128)(2,1)S(1)} %bitcast.27, ...), custom_call_target="tpu_custom_call", output_to_operand_aliasing={{0}: (7, {}), {1}: (8, {}), {2}: (9, {}), {3}: (10, {}), {4... | custom-call | flops 1073741824 | bytes 1081344 | tf_op jit(solution)/shard_map/pallas_call | solution.py:356
  69.9 2.9 %collective-permute-start.14 = (bf16[528,128]{1,0:T(8,128)(2,1)S(1)}, bf16[528,128]{1,0:T(8,128)(2,1)S(1)}, u32[]{:S(2)}, u32[]{:S(2)}) collective-permute-start(bf16[528,128]{1,0:T(8,128)(2,1)S(1)} %slice.9), channel_id=1, source_target_pairs={{0,224},{32,0},{64,32},{96,64},{128,96},{160,128},{192,160},{224,1... | collective-permute-start | bytes 405512 | tf_op jit(solution)/shard_map/ppermute | solution.py:377
  72.9 5.7 %shard_map.131 = (f32[2,8,1024]{2,1,0:T(8,128)S(1)}, f32[2,144,1024]{2,1,0:T(8,128)S(1)}, f32[64,128]{1,0:T(8,128)S(1)}, f32[64,128]{1,0:T(8,128)S(1)}, f32[64,1...) custom-call(bf16[2048,128]{1,0:T(8,128)(2,1)S(1)} %bitcast.28, ...), custom_call_target="tpu_custom_call", output_to_operand_aliasing={{0}: (7, {}), {1}: (8, {}), {2}: (9, {}), {3}: (10, {}), {4... | custom-call | flops 1073741824 | bytes 1081344 | tf_op jit(solution)/shard_map/pallas_call | solution.py:356
  78.6 2.1 %tree.1 = (f32[64,128]{1,0:T(8,128)S(1)}, f32[64,128]{1,0:T(8,128)S(1)}, f32[64,128]{1,0:T(8,128)S(1)}, f32[256,128]{1,0:T(8,128)S(1)}, f32[256,128]{1,0:T(8,128)S(1)}) custom-call(bf16[528,128]{1,0:T(8,128)(2,1)S(1)} %pack.1.own_ref.refs_1_, ...), custom_call_target="tpu_custom_call", output_to_operand_aliasing={{0}: (5, {}), {1}: (6, {}), {2}: (7, {}), {3}: (8, {}), {4}... | custom-call | flops 268435456 | bytes 270336 | tf_op jit(solution)/shard_map/tree/pallas_call | solution.py:456
  80.7 4.3 %shard_map.132 = (f32[2,8,1024]{2,1,0:T(8,128)S(1)}, f32[2,144,1024]{2,1,0:T(8,128)S(1)}, f32[64,128]{1,0:T(8,128)S(1)}, f32[64,128]{1,0:T(8,128)S(1)}, f32[64,1...) custom-call(bf16[2048,128]{1,0:T(8,128)(2,1)S(1)} %bitcast.29, ...), custom_call_target="tpu_custom_call", output_to_operand_aliasing={{0}: (5, {}), {1}: (6, {}), {2}: (7, {}), {3}: (8, {}), {4}... | custom-call | flops 805306368 | bytes 811008 | tf_op jit(solution)/shard_map/pallas_call | solution.py:356
  85.0 4.3 %shard_map.133 = (f32[2,8,1024]{2,1,0:T(8,128)S(1)}, f32[2,144,1024]{2,1,0:T(8,128)S(1)}, f32[64,128]{1,0:T(8,128)S(1)}, f32[64,128]{1,0:T(8,128)S(1)}, f32[64,1...) custom-call(bf16[2048,128]{1,0:T(8,128)(2,1)S(1)} %bitcast.30, ...), custom_call_target="tpu_custom_call", output_to_operand_aliasing={{0}: (6, {}), {1}: (7, {}), {2}: (8, {}), {3}: (9, {}), {4}... | custom-call | flops 536870912 | bytes 540672 | tf_op jit(solution)/shard_map/pallas_call | solution.py:356
  (29 shorter events, 0.2 us)
Async XLA Ops:
  0.6 49.6 %copy-start.3 = (bf16[128,2,128]{2,1,0:T(2,128)(2,1)S(1)}, bf16[128,2,128]{2,1,0:T(2,128)(2,1)}, u32[]{:S(2)}) copy-start(bf16[128,2,128]{2,1,0:T(2,128)(2,1)} %param.18) | copy-start | bytes 196612
  0.6 50.2 %copy-start.1 = (bf16[256,8,128]{2,1,0:T(8,128)(2,1)S(1)}, bf16[256,8,128]{2,1,0:T(8,128)(2,1)}, u32[]{:S(2)}) copy-start(bf16[256,8,128]{2,1,0:T(8,128)(2,1)} %param.10) | copy-start | bytes 1572868
  0.7 56.0 %copy-start = (bf16[256,8,128]{2,1,0:T(8,128)(2,1)S(1)}, bf16[256,8,128]{2,1,0:T(8,128)(2,1)}, u32[]{:S(2)}) copy-start(bf16[256,8,128]{2,1,0:T(8,128)(2,1)} %param.16) | copy-start | bytes 1572868
  1.8 6.6 %collective-permute-start.4 = (bf16[528,128]{1,0:T(8,128)(2,1)S(1)}, bf16[528,128]{1,0:T(8,128)(2,1)S(1)}, u32[]{:S(2)}, u32[]{:S(2)}) collective-permute-start(bf16[528,128]{1,0:T(8,128)(2,1)S(1)} %pack.1.own_ref.refs_1_), channel_id=1, source_target_pairs={{0,8},{8,16},{16,24},{24,0},{1,9},{9,17},{17,25},{25,1},{2,10},{10... | collective-permute-start | bytes 405512 | tf_op jit(solution)/shard_map/ppermute | solution.py:377
  3.4 7.2 %collective-permute-start.5 = (bf16[528,128]{1,0:T(8,128)(2,1)S(1)}, bf16[528,128]{1,0:T(8,128)(2,1)S(1)}, u32[]{:S(2)}, u32[]{:S(2)}) collective-permute-start(bf16[528,128]{1,0:T(8,128)(2,1)S(1)} %pack.1.own_ref.refs_1_), channel_id=1, source_target_pairs={{0,24},{8,0},{16,8},{24,16},{1,25},{9,1},{17,9},{25,17},{2,26},{10... | collective-permute-start | bytes 405512 | tf_op jit(solution)/shard_map/ppermute | solution.py:377
  5.1 7.2 %collective-permute-start.6 = (bf16[528,128]{1,0:T(8,128)(2,1)S(1)}, bf16[528,128]{1,0:T(8,128)(2,1)S(1)}, u32[]{:S(2)}, u32[]{:S(2)}) collective-permute-start(bf16[528,128]{1,0:T(8,128)(2,1)S(1)} %pack.1.own_ref.refs_1_), channel_id=1, source_target_pairs={{0,16},{8,24},{16,0},{24,8},{1,17},{9,25},{17,1},{25,9},{2,18},{10... | collective-permute-start | bytes 405512 | tf_op jit(solution)/shard_map/ppermute | solution.py:377
  12.3 14.7 %collective-permute-start.7 = (bf16[1584,128]{1,0:T(8,128)(2,1)S(1)}, bf16[1584,128]{1,0:T(8,128)(2,1)S(1)}, u32[]{:S(2)}, u32[]{:S(2)}) collective-permute-start(bf16[1584,128]{1,0:T(8,128)(2,1)S(1)} %constant_dynamic-update-slice_fusion.refs_3_), channel_id=1, source_target_pairs={{0,32},{32,64},{64,96},{96,128},{128,160},{160,192},{192,224},{224... | collective-permute-start | bytes 1216520 | tf_op jit(solution)/shard_map/ppermute | solution.py:377
  14.3 12.7 %collective-permute-start.11 = (bf16[1584,128]{1,0:T(8,128)(2,1)S(1)}, bf16[1584,128]{1,0:T(8,128)(2,1)S(1)}, u32[]{:S(2)}, u32[]{:S(2)}) collective-permute-start(bf16[1584,128]{1,0:T(8,128)(2,1)S(1)} %constant_dynamic-update-slice_fusion.refs_3_), channel_id=1, source_target_pairs={{0,224},{32,0},{64,32},{96,64},{128,96},{160,128},{192,160},{224,1... | collective-permute-start | bytes 1216520 | tf_op jit(solution)/shard_map/ppermute | solution.py:377
  27.0 17.0 %collective-permute-start.8 = (bf16[1584,128]{1,0:T(8,128)(2,1)S(1)}, bf16[1584,128]{1,0:T(8,128)(2,1)S(1)}, u32[]{:S(2)}, u32[]{:S(2)}) collective-permute-start(bf16[1584,128]{1,0:T(8,128)(2,1)S(1)} %collective-permute-done.7.refs_3_), channel_id=1, source_target_pairs={{0,32},{32,64},{64,96},{96,128},{128,160},{160,192},{192,224},{224... | collective-permute-start | bytes 1216520 | tf_op jit(solution)/shard_map/ppermute | solution.py:377
  27.0 23.2 %collective-permute-start.12 = (bf16[1584,128]{1,0:T(8,128)(2,1)S(1)}, bf16[1584,128]{1,0:T(8,128)(2,1)S(1)}, u32[]{:S(2)}, u32[]{:S(2)}) collective-permute-start(bf16[1584,128]{1,0:T(8,128)(2,1)S(1)} %collective-permute-done.11.refs_4_), channel_id=1, source_target_pairs={{0,224},{32,0},{64,32},{96,64},{128,96},{160,128},{192,160},{224,1... | collective-permute-start | bytes 1216520 | tf_op jit(solution)/shard_map/ppermute | solution.py:377
  30.3 10.0 %collective-permute-start = (bf16[528,128]{1,0:T(8,128)(2,1)S(1)}, bf16[528,128]{1,0:T(8,128)(2,1)S(1)}, u32[]{:S(2)}, u32[]{:S(2)}) collective-permute-start(bf16[528,128]{1,0:T(8,128)(2,1)S(1)} %pack.1.own_ref.refs_1_), channel_id=1, source_target_pairs={{0,224},{32,0},{64,32},{96,64},{128,96},{160,128},{192,160},{224,1... | collective-permute-start | bytes 405512 | tf_op jit(solution)/shard_map/ppermute | solution.py:377
  30.8 14.1 %collective-permute-start.15 = (bf16[528,128]{1,0:T(8,128)(2,1)S(1)}, bf16[528,128]{1,0:T(8,128)(2,1)S(1)}, u32[]{:S(2)}, u32[]{:S(2)}) collective-permute-start(bf16[528,128]{1,0:T(8,128)(2,1)S(1)} %pack.1.own_ref.refs_1_), channel_id=1, source_target_pairs={{0,32},{32,64},{64,96},{96,128},{128,160},{160,192},{192,224},{224... | collective-permute-start | bytes 405512 | tf_op jit(solution)/shard_map/ppermute | solution.py:377
  40.3 6.3 %collective-permute-start.1 = (bf16[528,128]{1,0:T(8,128)(2,1)S(1)}, bf16[528,128]{1,0:T(8,128)(2,1)S(1)}, u32[]{:S(2)}, u32[]{:S(2)}) collective-permute-start(bf16[528,128]{1,0:T(8,128)(2,1)S(1)} %collective-permute-done.refs_5_), channel_id=1, source_target_pairs={{0,224},{32,0},{64,32},{96,64},{128,96},{160,128},{192,160},{224,1... | collective-permute-start | bytes 405512 | tf_op jit(solution)/shard_map/ppermute | solution.py:377
  44.0 20.1 %collective-permute-start.9 = (bf16[1584,128]{1,0:T(8,128)(2,1)S(1)}, bf16[1584,128]{1,0:T(8,128)(2,1)S(1)}, u32[]{:S(2)}, u32[]{:S(2)}) collective-permute-start(bf16[1584,128]{1,0:T(8,128)(2,1)S(1)} %collective-permute-done.8.refs_3_), channel_id=1, source_target_pairs={{0,32},{32,64},{64,96},{96,128},{128,160},{160,192},{192,224},{224... | collective-permute-start | bytes 1216520 | tf_op jit(solution)/shard_map/ppermute | solution.py:377
  44.9 11.7 %collective-permute-start.16 = (bf16[528,128]{1,0:T(8,128)(2,1)S(1)}, bf16[528,128]{1,0:T(8,128)(2,1)S(1)}, u32[]{:S(2)}, u32[]{:S(2)}) collective-permute-start(bf16[528,128]{1,0:T(8,128)(2,1)S(1)} %collective-permute-done.15.refs_4_), channel_id=1, source_target_pairs={{0,32},{32,64},{64,96},{96,128},{128,160},{160,192},{192,224},{224... | collective-permute-start | bytes 405512 | tf_op jit(solution)/shard_map/ppermute | solution.py:377
  46.6 14.2 %collective-permute-start.2 = (bf16[528,128]{1,0:T(8,128)(2,1)S(1)}, bf16[528,128]{1,0:T(8,128)(2,1)S(1)}, u32[]{:S(2)}, u32[]{:S(2)}) collective-permute-start(bf16[528,128]{1,0:T(8,128)(2,1)S(1)} %collective-permute-done.1.refs_6_), channel_id=1, source_target_pairs={{0,224},{32,0},{64,32},{96,64},{128,96},{160,128},{192,160},{224,1... | collective-permute-start | bytes 405512 | tf_op jit(solution)/shard_map/ppermute | solution.py:377
  50.2 19.7 %collective-permute-start.13 = (bf16[1584,128]{1,0:T(8,128)(2,1)S(1)}, bf16[1584,128]{1,0:T(8,128)(2,1)S(1)}, u32[]{:S(2)}, u32[]{:S(2)}) collective-permute-start(bf16[1584,128]{1,0:T(8,128)(2,1)S(1)} %collective-permute-done.12.refs_4_), channel_id=1, source_target_pairs={{0,224},{32,0},{64,32},{96,64},{128,96},{160,128},{192,160},{224,1... | collective-permute-start | bytes 1216520 | tf_op jit(solution)/shard_map/ppermute | solution.py:377
  50.3 28.3 %collective-permute-start.18 = (bf16[128,512]{1,0:T(8,128)(2,1)S(1)}, bf16[128,512]{1,0:T(8,128)(2,1)S(1)}, u32[]{:S(2)}, u32[]{:S(2)}) collective-permute-start(bf16[128,512]{1,0:T(8,128)(2,1)S(1)} %bitcast_dynamic-update-slice_fusion.tree_ref), channel_id=1, source_target_pairs={{0,1},{1,0},{2,3},{3,2},{4,5},{5,4},{6,7},{7,6},{8,9},{9,8},{10,11... | collective-permute-start | bytes 393224 | tf_op jit(solution)/shard_map/ppermute | solution.py:377
  56.6 16.3 %collective-permute-start.17 = (bf16[528,128]{1,0:T(8,128)(2,1)S(1)}, bf16[528,128]{1,0:T(8,128)(2,1)S(1)}, u32[]{:S(2)}, u32[]{:S(2)}) collective-permute-start(bf16[528,128]{1,0:T(8,128)(2,1)S(1)} %collective-permute-done.16.refs_5_), channel_id=1, source_target_pairs={{0,32},{32,64},{64,96},{96,128},{128,160},{160,192},{192,224},{224... | collective-permute-start | bytes 405512 | tf_op jit(solution)/shard_map/ppermute | solution.py:377
  60.8 24.1 %collective-permute-start.3 = (bf16[528,128]{1,0:T(8,128)(2,1)S(1)}, bf16[528,128]{1,0:T(8,128)(2,1)S(1)}, u32[]{:S(2)}, u32[]{:S(2)}) collective-permute-start(bf16[528,128]{1,0:T(8,128)(2,1)S(1)} %collective-permute-done.2.refs_6_), channel_id=1, source_target_pairs={{0,224},{32,0},{64,32},{96,64},{128,96},{160,128},{192,160},{224,1... | collective-permute-start | bytes 405512 | tf_op jit(solution)/shard_map/ppermute | solution.py:377
  64.1 20.8 %collective-permute-start.10 = (bf16[1056,128]{1,0:T(8,128)(2,1)S(1)}, bf16[1056,128]{1,0:T(8,128)(2,1)S(1)}, u32[]{:S(2)}, u32[]{:S(2)}) collective-permute-start(bf16[1056,128]{1,0:T(8,128)(2,1)S(1)} %slice.8), channel_id=1, source_target_pairs={{0,32},{32,64},{64,96},{96,128},{128,160},{160,192},{192,224},{224... | collective-permute-start | bytes 811016 | tf_op jit(solution)/shard_map/ppermute | solution.py:377
  69.9 15.0 %collective-permute-start.14 = (bf16[528,128]{1,0:T(8,128)(2,1)S(1)}, bf16[528,128]{1,0:T(8,128)(2,1)S(1)}, u32[]{:S(2)}, u32[]{:S(2)}) collective-permute-start(bf16[528,128]{1,0:T(8,128)(2,1)S(1)} %slice.9), channel_id=1, source_target_pairs={{0,224},{32,0},{64,32},{96,64},{128,96},{160,128},{192,160},{224,1... | collective-permute-start | bytes 405512 | tf_op jit(solution)/shard_map/ppermute | solution.py:377
  72.9 5.7 %copy-start.2 = (s32[256]{0:T(256)S(1)}, s32[256]{0:T(256)}, u32[]{:S(2)}) copy-start(s32[256]{0:T(256)} %param.19) | copy-start | bytes 3076
